TPU v7x, 32 devices: a whole 2x2x4 slice. The times are simulated.
32 devices in a mesh: tm: 8 (over z, y), lat: 4 (over x, core).
Axes of the slice: x: 2, y: 2, z: 4, core: 2. Of those that a mesh axis runs over, the one named last changes fastest.
Arguments:
- traj: float32 [8, 83, 24, 192], P('tm', None, 'lat'), may hold values from -6 to 6
- noise: float32 [8, 83, 24, 192], P('tm', None, 'lat'), may hold values from -6 to 6
- step_index: int32 [8], P('tm'), may hold values from 0 to 999
- embed_weight: bfloat16 [83, 512], replicated, may hold values from -0.625 to 0.625
- time_weight: float32 [512, 512], replicated, may hold values from -0.25 to 0.25
- dw_weight: float32 [512, 25], replicated, may hold values from -1.25 to 1.25
- ln_gain: float32 [512], replicated, may hold values from 0.5 to 1.5
- up_weight: bfloat16 [512, 1024], replicated, may hold values from -0.25 to 0.25
- down_weight: bfloat16 [1024, 512], replicated, may hold values from -0.1875 to 0.1875
- out_weight: bfloat16 [512, 83], replicated, may hold values from -0.25 to 0.25
Outputs:
- trajectory: float32 [8, 83, 24, 192], P('tm', None, 'lat')
All inputs are finite; a program needn't handle non-finite values.
Results may differ from a plain program's by a relative error of at most 0.0025.
Values may be sent and summed in bfloat16 or wider, within the bound.
No kernel may reach another device: no remote copies, remote signals or barrier semaphores. Data moves between devices by JAX's collectives and lax.ppermute only.
A program may use at most 128 MiB of HBM per device.

v0:
```python
import math

import jax
import jax.numpy as jnp
from jax import lax
from jax.sharding import PartitionSpec as P

ITERS = 2
LEVELS = 1000


def with_halo(x, sides, width):
    for axis, dim in sides:
        devices, length = (lax.axis_size(axis), x.shape[dim])
        up = [(i, (i + 1) % devices) for i in range(devices - 1)]
        down = [(j, i) for i, j in up]
        last = lax.slice_in_dim(x, length - width, length, axis=dim)
        first = lax.slice_in_dim(x, 0, width, axis=dim)
        before = lax.ppermute(last, axis, up)
        after = lax.ppermute(first, axis, down)
        x = jnp.concatenate([before, x, after], axis=dim)
    return x


def entering(part, axis, combine, identity):
    place = lax.axis_index(axis)
    gathered = lax.all_gather(part, axis)
    state = jnp.zeros_like(part) + jnp.asarray(identity, part.dtype)

    def one(turn, state):
        return combine(state, lax.dynamic_index_in_dim(gathered, turn, 0, False))

    return lax.fori_loop(0, place, one, state)


def spread(value, axis, source):
    kept = jnp.where(lax.axis_index(axis) == source, value, 0).astype(value.dtype)
    return lax.psum(kept, axis)


def noise_levels(step_index):
    log_ratio = math.log(0.1) / (LEVELS - 1)
    return 2.0 * jnp.exp(step_index.astype(jnp.float32) * log_ratio)


def conditions(noise_level, time_weight):
    half_width = time_weight.shape[0] // 2
    frequency = jnp.exp(jnp.arange(half_width, dtype=jnp.float32) * (-math.log(100.0) / half_width))
    angles = jnp.log(noise_level)[:, None] * frequency[None, :]
    features = jnp.concatenate([jnp.cos(angles), jnp.sin(angles)], axis=1)
    return jax.nn.silu(jnp.dot(features, time_weight, precision=lax.Precision.HIGHEST))


def depthwise_taps(lat_padded, dw_weight):
    lat_rows = lat_padded.shape[1] - 4
    widened = lat_padded.astype(jnp.float32)
    lon_cols = widened.shape[2]
    widened = jnp.concatenate([widened[:, :, -2:], widened, widened[:, :, :2]], axis=2)
    summed = jnp.zeros((widened.shape[0], lat_rows, lon_cols), jnp.float32)
    for row_tap in range(5):
        for col_tap in range(5):
            summed = (
                summed
                + dw_weight[:, row_tap * 5 + col_tap][:, None, None]
                * widened[:, row_tap : row_tap + lat_rows, col_tap : col_tap + lon_cols]
            )
    return summed


def denoise(
    current, condition, embed_weight, dw_weight, ln_gain, up_weight, down_weight, out_weight
):
    channels, lat_rows, lon_cols = current.shape
    width = embed_weight.shape[1]
    as_rows = current.astype(jnp.bfloat16).reshape(channels, lat_rows * lon_cols)
    embedded = jnp.dot(embed_weight.T, as_rows, preferred_element_type=jnp.float32)
    activation = (embedded + condition[:, None]).astype(jnp.bfloat16)
    padded = with_halo(activation.reshape(width, lat_rows, lon_cols), (("lat", 1),), 2)
    convolved = depthwise_taps(padded, dw_weight).reshape(width, lat_rows * lon_cols)
    average = jnp.mean(convolved, axis=0)
    centred = convolved - average[None, :]
    variance = jnp.mean(centred * centred, axis=0)
    normed = (centred * lax.rsqrt(variance + 1e-06)[None, :] * ln_gain[:, None]).astype(
        jnp.bfloat16
    )
    hidden = jax.nn.gelu(
        jnp.dot(up_weight.T, normed, preferred_element_type=jnp.float32), approximate=True
    ).astype(jnp.bfloat16)
    block_out = (
        activation.astype(jnp.float32)
        + jnp.dot(down_weight.T, hidden, preferred_element_type=jnp.float32)
    ).astype(jnp.bfloat16)
    return jnp.dot(out_weight.T, block_out, preferred_element_type=jnp.float32).reshape(
        channels, lat_rows, lon_cols
    )


def add_terms(earlier, later):
    return earlier + later


def earlier_sum(increment):
    return entering(increment, "tm", add_terms, jnp.zeros_like(increment))


def shards(
    traj,
    noise,
    step_index,
    embed_weight,
    time_weight,
    dw_weight,
    ln_gain,
    up_weight,
    down_weight,
    out_weight,
):
    noise_level = noise_levels(step_index)
    condition = conditions(noise_level, time_weight)[0]
    level_now = noise_level[0]
    root = traj[0]
    anchor = spread(root, "tm", 0)
    current = root
    for picard_step in range(ITERS):
        drift_term = denoise(
            current, condition, embed_weight, dw_weight, ln_gain, up_weight, down_weight, out_weight
        )
        increment = 0.125 * level_now * drift_term + 0.125 * jnp.sqrt(level_now) * noise[0]
        current = anchor + earlier_sum(increment)
    return current[None]


def solution(mesh):
    in_specs = (
        P("tm", None, "lat", None),
        P("tm", None, "lat", None),
        P("tm"),
        P(),
        P(),
        P(),
        P(),
        P(),
        P(),
        P(),
    )
    out_specs = P("tm", None, "lat", None)
    return jax.shard_map(shards, mesh=mesh, in_specs=in_specs, out_specs=out_specs, check_vma=False)
```

profile of v0, /device:TPU:0, one launch (start us, length us, event | category | flops | bytes accessed | tf_op | source)
XLA Modules:
  0.0 313.9 jit_solution(5527043713613700483)
XLA Ops:
  7.4 1.8 fusion.162
  9.3 2.4 convert_reduce_fusion
  12.0 0.5 fusion.22
  12.6 0.6 copy.24
  13.3 2.4 collective-permute-start
  15.7 1.3 collective-permute-start.1
  17.0 0.9 fusion.177
  17.9 1.2 fusion.176
  19.3 2.0 collective-permute-done.1
  21.9 8.8 %fusion.170 = (f32[6,192]{1,0:T(8,128)S(1)}, f32[512,6,192]{0,2,1:T(8,128)S(1)}) fusion(f32[512,10,2]{0,2,1:T(2,128)S(1)} %get-tuple-element.84, f32[512,10,192]{0,2,1:T(8,128)S(1)} %maximum_convert_fusion, f32[512]{0:T(512)S(1)} %bitcast.124, f32[512]{0:T(512)S(1)} %bitcast.126, f32[512]{0:T(512)S(1)} %bitcast.130, ...), kind=kLoop, calls=%fused_computation.285 | loop fusion | flops 41286528 | bytes 18225664 | tf_op jit(solution)/shard_map/reduce_sum | solution.py:80
  30.8 0.5 multiply_reduce_fusion.1
  31.4 1.1 fusion.155
  32.6 3.5 %fusion.9 = bf16[1024,1152]{0,1:T(8,128)(2,1)} fusion(bf16[512,1152]{0,1:T(8,128)(2,1)S(1)} %fusion.155, bf16[512,1024]{1,0:T(8,128)(2,1)S(1)} %copy-done), kind=kOutput, calls=%fused_computation.51 | convolution fusion | flops 1218576384 | bytes 4587520 | tf_op jit(solution)/shard_map/dot_general | solution.py:87
  36.1 4.5 %fusion.24 = f32[83,1152]{1,0:T(8,128)} fusion(bf16[512,83]{0,1:T(8,128)(2,1)S(1)} %copy-done.47, bf16[1024,1152]{0,1:T(8,128)(2,1)} %fusion.9, bf16[1024,512]{1,0:T(8,128)(2,1)} %param.22, bf16[512,1152]{1,0:T(8,128)(2,1)S(1)} %copy-done.4, f32[]{:T(128)} %bitcast.3), kind=kOutput, calls=%fused_computation.108 | convolution fusion | flops 1307735424 | bytes 5054980 | tf_op jit(solution)/shard_map/dot_general | solution.py:93
  40.6 1.3 mul.669
  42.1 1.0 copy.27
  43.1 0.9 fusion.161
  44.1 79.5 %all-gather.3.cloned.1.call-done = f32[8,83,6,192]{3,1,2,0:T(8,128)} async-done(((f32[1,83,6,192]{3,1,2,0:T(8,128)}), f32[8,83,6,192]{3,1,2,0:T(8,128)}) %all-gather.3.cloned.1.call-update) | async-done | bytes 3059728 | tf_op jit(solution)/shard_map/all_gather | solution.py:27
  123.8 74.6 %all-reduce.2.cloned.1.call-done = f32[83,6,192]{2,0,1:T(8,128)} async-done(((f32[83,6,192]{2,0,1:T(8,128)}), f32[83,6,192]{2,0,1:T(8,128)}) %all-reduce.2.cloned.1.call-update) | async-done | bytes 382480 | tf_op jit(solution)/shard_map/psum | solution.py:38
  198.4 1.2 fusion.160
  200.0 0.5 fusion.23
  200.6 1.3 collective-permute-start.2
  202.1 1.3 collective-permute-start.3
  203.4 4.0 %collective-permute-done.3 = bf16[512,2,192]{0,2,1:T(8,128)(2,1)S(1)} collective-permute-done((bf16[512,2,192]{0,2,1:T(8,128)(2,1)S(1)}, bf16[512,2,192]{0,2,1:T(8,128)(2,1)S(1)}, u32[]{:S(2)}, u32[]{:S(2)}) %collective-permute-start.3) | collective-permute-done | bytes 393248 | tf_op jit(solution)/shard_map/ppermute | solution.py:20
  207.9 8.8 %fusion.168 = (f32[6,192]{1,0:T(8,128)S(1)}, f32[512,6,192]{0,2,1:T(8,128)S(1)}) fusion(f32[512,10,2]{0,2,1:T(2,128)S(1)} %get-tuple-element.82, f32[512,10,192]{0,2,1:T(8,128)S(1)} %maximum_convert_fusion.1, f32[512]{0:T(512)S(1)} %bitcast.125, f32[512]{0:T(512)S(1)} %bitcast.127, f32[512]{0:T(512)S(1)} %bitcast.131, ...), kind=kLoop, calls=%fused_computation.284 | loop fusion | flops 41286528 | bytes 18225664 | tf_op jit(solution)/shard_map/reduce_sum | solution.py:80
  216.8 0.5 multiply_reduce_fusion
  217.9 3.5 %fusion.17 = bf16[1024,1152]{0,1:T(8,128)(2,1)} fusion(bf16[512,1152]{0,1:T(8,128)(2,1)S(1)} %fusion.152, bf16[512,1024]{1,0:T(8,128)(2,1)S(1)} %copy-done), kind=kOutput, calls=%fused_computation.59 | convolution fusion | flops 1218576384 | bytes 4587520 | tf_op jit(solution)/shard_map/dot_general | solution.py:87
  221.4 3.7 %fusion.25 = f32[83,1152]{1,0:T(8,128)S(1)} fusion(bf16[512,83]{0,1:T(8,128)(2,1)S(1)} %copy-done.48, bf16[1024,1152]{0,1:T(8,128)(2,1)} %fusion.17, bf16[1024,512]{1,0:T(8,128)(2,1)} %param.22, bf16[1152,512]{1,0:T(8,128)(2,1)S(1)} %copy-done.2, f32[]{:T(128)} %bitcast.3), kind=kOutput, calls=%fused_computation.109 | convolution fusion | flops 1307735424 | bytes 5054980 | tf_op jit(solution)/shard_map/dot_general | solution.py:93
  225.6 1.0 copy.31
  226.6 78.3 %all-gather.5.cloned.1.call-done = f32[8,83,6,192]{3,1,2,0:T(8,128)} async-done(((f32[1,83,6,192]{3,1,2,0:T(8,128)}), f32[8,83,6,192]{3,1,2,0:T(8,128)}) %all-gather.5.cloned.1.call-update) | async-done | bytes 3059728 | tf_op jit(solution)/shard_map/all_gather | solution.py:27
  304.9 1.0 copy-done.5
  306.1 1.3 copy.34
  (133 shorter events, 3.5 us)
Async XLA Ops:
  6.5 26.0 %copy-start = (bf16[512,1024]{1,0:T(8,128)(2,1)S(1)}, bf16[512,1024]{1,0:T(8,128)(2,1)}, u32[]{:S(2)}) copy-start(bf16[512,1024]{1,0:T(8,128)(2,1)} %param.21) | copy-start | bytes 3145732
  6.5 5.5 %copy-start.9 = (bf16[83,512]{1,0:T(8,128)(2,1)S(1)}, bf16[83,512]{1,0:T(8,128)(2,1)}, u32[]{:S(2)}) copy-start(bf16[83,512]{1,0:T(8,128)(2,1)} %param.17) | copy-start | bytes 254980
  6.5 117.0 %all-gather.3.cloned.1.call-start = ((), (), s32[]{:S(2)}) async-start(), calls=%async_computation.1 | async-start | bytes 4866048 | tf_op jit(solution)/shard_map/all_gather | solution.py:27
  12.6 9.1 %copy-start.3 = (bf16[512,1152]{1,0:T(8,128)(2,1)}, bf16[512,1152]{1,0:T(8,128)(2,1)S(1)}, u32[]{:S(2)}) copy-start(bf16[512,1152]{1,0:T(8,128)(2,1)S(1)} %fusion.22) | copy-start | bytes 3538948
  13.3 6.1 %collective-permute-start = (bf16[512,2,192]{0,2,1:T(8,128)(2,1)S(1)}, bf16[512,2,192]{0,2,1:T(8,128)(2,1)S(1)}, u32[]{:S(2)}, u32[]{:S(2)}) collective-permute-start(bf16[512,2,192]{0,2,1:T(8,128)(2,1)S(1)} %get-tuple-element.87), channel_id=1, source_target_pairs={{0,1},{1,2},{2,3},{4,5},{5,6},{6,7},{8,9},{9,10},{10,11},{12,13},{... | collective-permute-start | bytes 1179656 | tf_op jit(solution)/shard_map/ppermute | solution.py:19
  15.7 5.7 %collective-permute-start.1 = (bf16[512,2,192]{0,2,1:T(8,128)(2,1)S(1)}, bf16[512,2,192]{0,2,1:T(8,128)(2,1)S(1)}, u32[]{:S(2)}, u32[]{:S(2)}) collective-permute-start(bf16[512,2,192]{0,2,1:T(8,128)(2,1)S(1)} %get-tuple-element.88), channel_id=1, source_target_pairs={{1,0},{2,1},{3,2},{5,4},{6,5},{7,6},{9,8},{10,9},{11,10},{13,12},{... | collective-permute-start | bytes 1179656 | tf_op jit(solution)/shard_map/ppermute | solution.py:20
  36.1 5.8 %copy-start.6 = (f32[1,83,6,192]{3,0,2,1:T(1,128)S(1)}, f32[1,83,6,192]{3,0,2,1:T(1,128)}, u32[]{:S(2)}) copy-start(f32[1,83,6,192]{3,0,2,1:T(1,128)} %param.15) | copy-start | bytes 1147396
  43.1 155.4 %all-reduce.2.cloned.1.call-start = ((), (), s32[]{:S(2)}) async-start(), calls=%async_computation | async-start | bytes 1081344 | tf_op jit(solution)/shard_map/psum | solution.py:38
  44.0 260.8 %all-gather.5.cloned.1.call-start = ((), (), s32[]{:S(2)}) async-start(), calls=%async_computation.2 | async-start | bytes 4866048 | tf_op jit(solution)/shard_map/all_gather | solution.py:27
  123.8 76.2 %copy-start.45 = (f32[512]{0:T(512)S(1)}, f32[512]{0:T(512)}, u32[]{:S(2)}) copy-start(f32[512]{0:T(512)} %copy-done.44) | copy-start | bytes 6148
  200.5 7.2 %copy-start.1 = (bf16[1152,512]{1,0:T(8,128)(2,1)}, bf16[1152,512]{1,0:T(8,128)(2,1)S(1)}, u32[]{:S(2)}) copy-start(bf16[1152,512]{1,0:T(8,128)(2,1)S(1)} %fusion.23) | copy-start | bytes 3538948
  200.6 2.8 collective-permute-start.2
  201.9 5.8 %copy-start.11 = (f32[512,1]{0,1:T(1,128)S(1)}, f32[512,1]{0,1:T(1,128)}, u32[]{:S(2)}) copy-start(f32[512,1]{0,1:T(1,128)} %copy-done.10) | copy-start | bytes 6148
  201.9 5.8 %copy-start.13 = (f32[512,1]{0,1:T(1,128)S(1)}, f32[512,1]{0,1:T(1,128)}, u32[]{:S(2)}) copy-start(f32[512,1]{0,1:T(1,128)} %copy-done.12) | copy-start | bytes 6148
  201.9 5.8 %copy-start.15 = (f32[512,1]{0,1:T(1,128)S(1)}, f32[512,1]{0,1:T(1,128)}, u32[]{:S(2)}) copy-start(f32[512,1]{0,1:T(1,128)} %copy-done.14) | copy-start | bytes 6148
  202.0 5.8 %copy-start.17 = (f32[512,1]{0,1:T(1,128)S(1)}, f32[512,1]{0,1:T(1,128)}, u32[]{:S(2)}) copy-start(f32[512,1]{0,1:T(1,128)} %copy-done.16) | copy-start | bytes 6148
  202.0 5.8 %copy-start.19 = (f32[512,1]{0,1:T(1,128)S(1)}, f32[512,1]{0,1:T(1,128)}, u32[]{:S(2)}) copy-start(f32[512,1]{0,1:T(1,128)} %copy-done.18) | copy-start | bytes 6148
  202.0 5.8 %copy-start.21 = (f32[512,1]{0,1:T(1,128)S(1)}, f32[512,1]{0,1:T(1,128)}, u32[]{:S(2)}) copy-start(f32[512,1]{0,1:T(1,128)} %copy-done.20) | copy-start | bytes 6148
  202.0 5.8 %copy-start.23 = (f32[512,1]{0,1:T(1,128)S(1)}, f32[512,1]{0,1:T(1,128)}, u32[]{:S(2)}) copy-start(f32[512,1]{0,1:T(1,128)} %copy-done.22) | copy-start | bytes 6148
  202.0 5.8 %copy-start.25 = (f32[512,1]{0,1:T(1,128)S(1)}, f32[512,1]{0,1:T(1,128)}, u32[]{:S(2)}) copy-start(f32[512,1]{0,1:T(1,128)} %copy-done.24) | copy-start | bytes 6148
  202.0 5.8 %copy-start.27 = (f32[512,1]{0,1:T(1,128)S(1)}, f32[512,1]{0,1:T(1,128)}, u32[]{:S(2)}) copy-start(f32[512,1]{0,1:T(1,128)} %copy-done.26) | copy-start | bytes 6148
  202.0 5.8 %copy-start.29 = (f32[512,1]{0,1:T(1,128)S(1)}, f32[512,1]{0,1:T(1,128)}, u32[]{:S(2)}) copy-start(f32[512,1]{0,1:T(1,128)} %copy-done.28) | copy-start | bytes 6148
  202.0 5.8 %copy-start.31 = (f32[512,1]{0,1:T(1,128)S(1)}, f32[512,1]{0,1:T(1,128)}, u32[]{:S(2)}) copy-start(f32[512,1]{0,1:T(1,128)} %copy-done.30) | copy-start | bytes 6148
  202.0 5.8 %copy-start.33 = (f32[512,1]{0,1:T(1,128)S(1)}, f32[512,1]{0,1:T(1,128)}, u32[]{:S(2)}) copy-start(f32[512,1]{0,1:T(1,128)} %copy-done.32) | copy-start | bytes 6148
  202.0 5.8 %copy-start.35 = (f32[512,1]{0,1:T(1,128)S(1)}, f32[512,1]{0,1:T(1,128)}, u32[]{:S(2)}) copy-start(f32[512,1]{0,1:T(1,128)} %copy-done.34) | copy-start | bytes 6148
  202.1 5.8 %copy-start.37 = (f32[512,1]{0,1:T(1,128)S(1)}, f32[512,1]{0,1:T(1,128)}, u32[]{:S(2)}) copy-start(f32[512,1]{0,1:T(1,128)} %copy-done.36) | copy-start | bytes 6148
  202.1 5.8 %copy-start.39 = (f32[512,1]{0,1:T(1,128)S(1)}, f32[512,1]{0,1:T(1,128)}, u32[]{:S(2)}) copy-start(f32[512,1]{0,1:T(1,128)} %copy-done.38) | copy-start | bytes 6148
  202.1 5.8 %copy-start.41 = (f32[512,1]{0,1:T(1,128)S(1)}, f32[512,1]{0,1:T(1,128)}, u32[]{:S(2)}) copy-start(f32[512,1]{0,1:T(1,128)} %copy-done.40) | copy-start | bytes 6148
  202.1 5.8 %copy-start.43 = (f32[512,1]{0,1:T(1,128)S(1)}, f32[512,1]{0,1:T(1,128)}, u32[]{:S(2)}) copy-start(f32[512,1]{0,1:T(1,128)} %copy-done.42) | copy-start | bytes 6148
  202.1 5.3 %collective-permute-start.3 = (bf16[512,2,192]{0,2,1:T(8,128)(2,1)S(1)}, bf16[512,2,192]{0,2,1:T(8,128)(2,1)S(1)}, u32[]{:S(2)}, u32[]{:S(2)}) collective-permute-start(bf16[512,2,192]{0,2,1:T(8,128)(2,1)S(1)} %get-tuple-element.86), channel_id=1, source_target_pairs={{1,0},{2,1},{3,2},{5,4},{6,5},{7,6},{9,8},{10,9},{11,10},{13,12},{... | collective-permute-start | bytes 1179656 | tf_op jit(solution)/shard_map/ppermute | solution.py:20
  217.9 3.6 %copy-start.2 = (bf16[1152,512]{1,0:T(8,128)(2,1)S(1)}, bf16[1152,512]{1,0:T(8,128)(2,1)}, u32[]{:S(2)}) copy-start(bf16[1152,512]{1,0:T(8,128)(2,1)} %copy-done.1) | copy-start | bytes 3538948
  221.4 4.0 %copy-start.7 = (f32[1,83,6,192]{3,0,2,1:T(1,128)S(1)}, f32[1,83,6,192]{3,0,2,1:T(1,128)}, u32[]{:S(2)}) copy-start(f32[1,83,6,192]{3,0,2,1:T(1,128)} %param.15) | copy-start | bytes 1147396
  (24 other events, 61.5 us)
Sparse Core Ops, SparseCore 0:
  43.2 80.3 all-gather.2
  127.0 71.4 all-reduce.1
  226.7 78.0 all-gather.4
where the time goes:
time: 320 us; the launch traced here: 314 us
  waiting for transfers between devices  238 us (74%)
  other arithmetic  25.8 us (8%)
  matrix products  18.1 us (6%)
  between operations  14.9 us (5%)
  local copies, waits for them, and re-layouts  9.97 us (3%)
  starting transfers between devices  6.4 us (2%)
    all_gather x2, waiting for transfers between devices, entering(): gathered = lax.all_gather(part, axis)  158 us
    psum x1, waiting for transfers between devices, spread(): return lax.psum(kept, axis)  74.6 us
    reduce_sum x2, other arithmetic, denoise(): average = jnp.mean(convolved, axis=0)  17.7 us
    dot_general x2, matrix products, denoise(): jnp.dot(out_weight.T, block_out, preferred_element_type=jnp.float32)  8.2 us
    dot_general x2, matrix products, denoise(): jnp.dot(up_weight.T, normed, preferred_element_type=jnp.float32)  7.09 us
  transfers between devices with their start and end apart: 7, of which 5 were waited for; matrix products, arithmetic and copies ran while one was open for 1% of the time, Pallas kernels for 0%

commit v1 on v0

v1 whole, which is shorter than its diff:
```python
import functools
import math

import jax
import jax.numpy as jnp
from jax import lax
from jax.experimental import pallas as pl
from jax.experimental.pallas import tpu as pltpu
from jax.sharding import PartitionSpec as P

ITERS = 2
LEVELS = 1000
LANES = 128
LEAD = 8


def noise_levels(step_index):
    log_ratio = math.log(0.1) / (LEVELS - 1)
    return 2.0 * jnp.exp(step_index.astype(jnp.float32) * log_ratio)


def conditions(noise_level, time_weight):
    half_width = time_weight.shape[0] // 2
    frequency = jnp.exp(jnp.arange(half_width, dtype=jnp.float32) * (-math.log(100.0) / half_width))
    angles = jnp.log(noise_level)[:, None] * frequency[None, :]
    features = jnp.concatenate([jnp.cos(angles), jnp.sin(angles)], axis=1)
    return jax.nn.silu(jnp.dot(features, time_weight, precision=lax.Precision.HIGHEST))


def denoise_kernel(
    sizes, scal_ref, flag_ref, *refs
):
    pieces, half, lon, chunks = sizes
    states = refs[:pieces]
    (cond_ref, emb_ref, dw_ref, gain_ref, up_ref, down_ref, out_ref,
     g0_ref, g1_ref, inc0_ref, inc1_ref, act_ref, conv_ref, bo_ref) = refs[pieces:]
    h = flag_ref[0]
    edge = flag_ref[1]
    width = chunks * LANES

    emb = emb_ref[...]
    for slot in range(2):
        cond = cond_ref[slot : slot + 1, :]
        for kind, ref in (("own", states[slot]), ("outer", states[2 + slot])):
            rows = ref.shape[1] // lon
            if kind == "own":
                base = 2 * (1 - h)
                scale = None
            else:
                base = 5 * h
                scale = edge.astype(jnp.float32)
            turned = ref[...].T
            for r in range(rows):
                z = jnp.dot(turned[r * lon : (r + 1) * lon, :], emb, preferred_element_type=jnp.float32)
                a = (z + cond).astype(jnp.bfloat16).astype(jnp.float32)
                if scale is not None:
                    a = a * scale
                for c in range(chunks):
                    piece = a[:, c * LANES : (c + 1) * LANES]
                    act_ref[slot, c, base + r, LEAD : LEAD + lon, :] = piece
                    act_ref[slot, c, base + r, 0:LEAD, :] = piece[lon - LEAD : lon, :]
                    act_ref[slot, c, base + r, LEAD + lon : 2 * LEAD + lon, :] = piece[0:LEAD, :]

    def conv_chunk(i, carry):
        slot = i // chunks
        c = i % chunks
        taps = [jnp.broadcast_to(dw_ref[c, k : k + 1, :], (8, LANES)) for k in range(25)]

        def conv_block(b, carry):
            col = pl.multiple_of(b * 8, 8)
            sums = [None] * half
            for rr in range(half + 4):
                for j in range(5):
                    x = act_ref[slot, c, rr, pl.ds(col + LEAD - 2 + j, 8), :]
                    for o in range(half):
                        k = rr - o
                        if 0 <= k < 5:
                            t = taps[k * 5 + j] * x
                            sums[o] = t if sums[o] is None else sums[o] + t
            for o in range(half):
                conv_ref[slot, o, c, pl.ds(col, 8), :] = sums[o]
            return carry

        return lax.fori_loop(0, lon // 8, conv_block, carry)

    lax.fori_loop(0, 2 * chunks, conv_chunk, 0)

    def mix(i, carry):
        slot = i // half
        o = i % half
        x = [conv_ref[slot, o, c] for c in range(chunks)]
        mean = sum(jnp.sum(v, axis=1, keepdims=True) for v in x) * (1.0 / width)
        x = [v - mean for v in x]
        var = sum(jnp.sum(v * v, axis=1, keepdims=True) for v in x) * (1.0 / width)
        inv = lax.rsqrt(var + 1e-06)
        n = jnp.concatenate(
            [(v * inv * gain_ref[:, c * LANES : (c + 1) * LANES]).astype(jnp.bfloat16) for c, v in enumerate(x)], axis=1
        )
        u = jnp.dot(n, up_ref[...], preferred_element_type=jnp.float32)
        hid = jax.nn.gelu(u, approximate=True).astype(jnp.bfloat16)
        d = jnp.dot(hid, down_ref[...], preferred_element_type=jnp.float32)
        a = jnp.concatenate([act_ref[slot, c, 2 + o, LEAD : LEAD + lon, :] for c in range(chunks)], axis=1)
        bo_ref[slot, pl.ds(pl.multiple_of(o * lon, 16), lon), :] = (a + d).astype(jnp.bfloat16)
        return carry

    lax.fori_loop(0, 2 * half, mix, 0)

    for slot, (g_ref, inc_ref) in enumerate(((g0_ref, inc0_ref), (g1_ref, inc1_ref))):
        drift = lax.dot_general(
            out_ref[...], bo_ref[slot], (((1,), (1,)), ((), ())), preferred_element_type=jnp.float32
        )
        inc_ref[...] = scal_ref[slot] * drift + g_ref[...]


def denoise(states, cond, coef, flags, weights, g_own, g_part, half, lon):
    channels = g_own.shape[0]
    width = cond.shape[1]
    chunks = width // LANES
    emb, dw, gain, up, down, out = weights
    vmem = pl.BlockSpec(memory_space=pltpu.VMEM)
    smem = pl.BlockSpec(memory_space=pltpu.SMEM)
    points = half * lon
    shape = jax.ShapeDtypeStruct((channels, points), jnp.float32)
    flops = 2 * 2 * points * width * (channels * 2 + 2 * up.shape[1] + 25)
    return pl.pallas_call(
        functools.partial(denoise_kernel, (len(states), half, lon, chunks)),
        out_shape=(shape, shape),
        in_specs=[smem, smem] + [vmem] * (len(states) + 9),
        out_specs=(vmem, vmem),
        scratch_shapes=[
            pltpu.VMEM((2, chunks, half + 4, lon + 2 * LEAD, LANES), jnp.float32),
            pltpu.VMEM((2, half, chunks, lon, LANES), jnp.float32),
            pltpu.VMEM((2, points, width), jnp.bfloat16),
        ],
        cost_estimate=pl.CostEstimate(flops=flops, bytes_accessed=4 << 20, transcendentals=2 * points * up.shape[1]),
        compiler_params=pltpu.CompilerParams(vmem_limit_bytes=48 << 20),
    )(coef, flags, *states, cond, emb, dw, gain, up, down, out, g_own, g_part)


def pair_sums(total, groups, swap, memory):
    earlier = None
    kept = []
    unit = 1
    stage = 0
    cur = total
    while unit < groups:
        before = memory[stage] if memory else None
        sent = (cur - before[0] if before else cur).astype(jnp.bfloat16)
        known = sent.astype(jnp.float32) + (before[0] if before else 0.0)
        got = before[1] if before else jnp.zeros_like(total)
        for step in (3, 2, 1):
            if step * unit < groups:
                shift = 2 * step * unit
                perm = [(i, i + shift) for i in range(2 * groups - shift)]
                got = got + lax.ppermute(sent, "tm", perm).astype(jnp.float32)
        kept.append((known, got))
        earlier = got if earlier is None else earlier + got
        cur = cur + got
        unit *= 4
        stage += 1
    return earlier, kept


def shards(
    traj, noise, step_index, embed_weight, time_weight, dw_weight, ln_gain, up_weight, down_weight, out_weight,
):
    times, bands = lax.axis_size("tm"), lax.axis_size("lat")
    t, l = lax.axis_index("tm"), lax.axis_index("lat")
    y = t % 2
    h = (y + l) % 2
    first = t // 2 == 0
    groups = times // 2
    channels, rows, lon = traj.shape[1:]
    half = rows // 2
    width = embed_weight.shape[1]
    both = ("tm", "lat")

    def at(a, b):
        return a * bands + b

    cells = [(a, b, (a + b) % 2) for a in range(times) for b in range(bands)]
    swap = [(at(a, b), at(a ^ 1, b)) for a, b, _ in cells]
    side = [(at(a, b), at(a, b + (1 if c else -1))) for a, b, c in cells if 0 <= b + (1 if c else -1) < bands]
    cross = [(at(a, b), at(a ^ 1, b + (-1 if c else 1))) for a, b, c in cells if 0 <= b + (-1 if c else 1) < bands]

    def cut(x, start, count):
        return lax.dynamic_slice_in_dim(x, start, count, axis=1).reshape(channels, count * lon)

    root = traj[0]
    v = root.astype(jnp.bfloat16)
    part5 = lax.ppermute(cut(v, 1 - h, half + 2), both, swap)
    own_out = lax.ppermute(cut(v, (rows - 2) * h, 2), both, side)
    part_out = lax.ppermute(cut(v, (rows - 2) * (1 - h), 2), both, cross)
    own5 = cut(v, h, half + 2)
    index2 = jnp.concatenate([step_index, lax.ppermute(step_index, both, swap)])

    level = noise_levels(step_index)[0]
    fixed = 0.125 * jnp.sqrt(level) * noise[0] + jnp.where(t == 0, root, 0.0)
    g_own = cut(fixed, half * h, half)
    g_part = lax.ppermute(cut(fixed, half * (1 - h), half), both, swap)

    levels2 = noise_levels(index2)
    cond = conditions(levels2, time_weight)
    coef = 0.125 * levels2
    edge = jnp.where(jnp.where(h == 0, l > 0, l < bands - 1), 1, 0)
    flags = jnp.stack([h, edge]).astype(jnp.int32)
    chunks = width // LANES
    dw = dw_weight.T.reshape(25, chunks, LANES).transpose(1, 0, 2)
    weights = (embed_weight, dw, ln_gain.reshape(1, width), up_weight, down_weight, out_weight.T)

    states = (own5, part5, own_out, part_out)
    memory = None
    for picard_step in range(ITERS):
        inc_own, inc_part = denoise(states, cond, coef, flags, weights, g_own, g_part, half, lon)
        earlier, memory = pair_sums(inc_own + inc_part, groups, swap, memory)
        inc_even = jnp.where(y == 0, inc_own, inc_part)
        now_own = earlier + jnp.where(y == 1, inc_even, 0.0)
        now_part = earlier + jnp.where(y == 0, inc_even, 0.0)
        if picard_step + 1 < ITERS:
            start_own = cut(v, half * h, half)
            start_part = jnp.where(h == 0, part5[:, : half * lon], part5[:, 2 * lon :])
            s_own = jnp.where(first & (y == 0), start_own, now_own.astype(jnp.bfloat16))
            s_part = jnp.where(first & (y == 1), start_part, now_part.astype(jnp.bfloat16))
            s = jnp.stack([s_own, s_part])
            low, high = s[:, :, : 2 * lon], s[:, :, (half - 2) * lon :]
            inner = lax.ppermute(jnp.where(h == 0, high, low), both, swap)
            outer = lax.ppermute(jnp.where(h == 0, low, high), both, side)
            inner = inner[::-1]
            s5 = jnp.where(
                h == 0, jnp.concatenate([s, inner], axis=2), jnp.concatenate([inner, s], axis=2)
            )
            states = (s5[0], s5[1], outer[0], outer[1])
    other = lax.ppermute(now_part, both, swap)
    mine = now_own
    upper = jnp.where(h == 0, mine, other).reshape(channels, half, lon)
    lower = jnp.where(h == 0, other, mine).reshape(channels, half, lon)
    result = jnp.concatenate([upper, lower], axis=1)
    return jnp.where(t == 0, root, result)[None]


def solution(mesh):
    in_specs = (P("tm", None, "lat", None), P("tm", None, "lat", None), P("tm")) + (P(),) * 7
    out_specs = P("tm", None, "lat", None)
    return jax.shard_map(shards, mesh=mesh, in_specs=in_specs, out_specs=out_specs, check_vma=False)
```

time: 320 us -> 111 us (0.35); the launches traced: 314 us -> 110 us
  waiting for transfers between devices: 238 us -> 14.2 us
  Pallas kernels: 0 us -> 28.1 us
  starting transfers between devices: 6.4 us -> 32.5 us
  matrix products: 18.1 us -> 0.62 us
  other arithmetic: 25.8 us -> 9.49 us
  between operations: 14.9 us -> 1.15 us
  local copies, waits for them, and re-layouts: 9.97 us -> 23.7 us
    all_gather x2 -> x0, waiting for transfers between devices: 158 us -> none  [entering(): gathered = lax.all_gather(part, axis)]
    psum x1 -> x0, waiting for transfers between devices: 74.6 us -> none  [spread(): return lax.psum(kept, axis)]
    pallas_call x0 -> x2, Pallas kernels: none -> 28.1 us  [denoise(): pl.pallas_call(functools.partial(denoise_kernel, (len(states), half, lon,...]
    ppermute x4 -> x14, starting transfers between devices: 6.32 us -> 32.5 us  [the longest x6 20.4 us: pair_sums(): got = got + lax.ppermute(sent, 'tm', perm).astype(jnp.float32)]
    reduce_sum x4 -> x0, other arithmetic: 18.7 us -> none  [the longest x2 17.7 us: denoise(): average = jnp.mean(convolved, axis=0)]
    dot_general x6 -> x0, matrix products: 16.3 us -> none  [the longest x2 8.2 us: denoise(): jnp.dot(out_weight.T, block_out, preferred_element_type=jnp.float32)]
    ppermute x4 -> x14, waiting for transfers between devices: 6.04 us -> 14.2 us  [the longest x1 6.53 us: shards(): other = lax.ppermute(now_part, both, swap)]
    unnamed x98 -> x46, local copies, waits for them, and re-layouts: 1.23 us -> 8.11 us
  transfers between devices with their start and end apart: 7 -> 14, of which waited for: 5 -> 5; matrix products, arithmetic and copies ran while one was open for 1% -> 17% of each run, Pallas kernels for 0% -> 0%
where the time goes in v1:
time: 111 us; the launch traced here: 110 us
  starting transfers between devices  32.5 us (29%)
  Pallas kernels  28.1 us (25%)
  local copies, waits for them, and re-layouts  23.7 us (21%)
  waiting for transfers between devices  14.2 us (13%)
  other arithmetic  9.49 us (9%)
  between operations  1.15 us (1%)
    pallas_call x2, Pallas kernels, denoise(): pl.pallas_call(functools.partial(denoise_kernel, (len(states), half, lon,...  28.1 us
    ppermute x6, starting transfers between devices, pair_sums(): got = got + lax.ppermute(sent, 'tm', perm).astype(jnp.float32)  20.4 us
    unnamed x46, local copies, waits for them, and re-layouts  8.11 us
    reshape x7, local copies, waits for them, and re-layouts, cut(): lax.dynamic_slice_in_dim(x, start, count, axis=1)  6.59 us
    ppermute x1, waiting for transfers between devices, shards(): other = lax.ppermute(now_part, both, swap)  6.53 us
    dynamic_slice x4, local copies, waits for them, and re-layouts, cut(): lax.dynamic_slice_in_dim(x, start, count, axis=1)  5.86 us
    ppermute x6, waiting for transfers between devices, pair_sums(): got = got + lax.ppermute(sent, 'tm', perm).astype(jnp.float32)  3.59 us
    ppermute x1, starting transfers between devices, shards(): part_out = lax.ppermute(cut(v, (rows - 2) * (1 - h), 2), both, cross)  3.38 us
  transfers between devices with their start and end apart: 14, of which 5 were waited for; matrix products, arithmetic and copies ran while one was open for 17% of the time, Pallas kernels for 0%

profile of v1, /device:TPU:0, one launch (start us, length us, event | category | flops | bytes accessed | tf_op | source)
XLA Modules:
  0.0 109.7 jit_solution(16656376839077370457)
XLA Ops:
  0.0 3.0 %collective-permute-start = (s32[1]{0:T(128)}, s32[1]{0:T(128)}, u32[]{:S(2)}, u32[]{:S(2)}) collective-permute-start(s32[1]{0:T(128)} %param.12), channel_id=1, source_target_pairs={{0,4},{1,5},{2,6},{3,7},{4,0},{5,1},{6,2},{7,3},{8,12},{9,13},{10,... | collective-permute-start | bytes 20 | tf_op jit(solution)/shard_map/ppermute | solution.py:195
  3.0 1.4 %convert_element_type.48 = bf16[1,83,6,192]{3,0,2,1:T(2,128)(2,1)S(1)} convert(f32[1,83,6,192]{3,0,2,1:T(1,128)} %param.10) | non-fusion elementwise | flops 95616 | bytes 573696 | tf_op jit(solution)/shard_map/convert_element_type | solution.py:190
  7.6 3.4 %collective-permute-start.3 = (bf16[83,384]{1,0:T(8,128)(2,1)}, bf16[83,384]{1,0:T(8,128)(2,1)S(1)}, u32[]{:S(2)}, u32[]{:S(2)}) collective-permute-start(bf16[83,384]{1,0:T(8,128)(2,1)} %reshape.84), channel_id=1, source_target_pairs={{0,5},{1,4},{2,7},{3,6},{5,2},{6,1},{8,13},{9,12},{10,15},{11,14},... | collective-permute-start | bytes 191240 | tf_op jit(solution)/shard_map/ppermute | solution.py:193
  11.0 2.5 %dynamic-slice_reduce_fusion.1 = (bf16[83,5,192]{2,1,0:T(8,128)(2,1)}, bf16[83,5,192]{2,1,0:T(8,128)(2,1)S(1)}) fusion(bf16[1,83,6,192]{3,0,2,1:T(2,128)(2,1)S(1)} %convert_element_type.48, s32[]{:T(128)S(6)} %select_n.144, s32[]{:T(128)S(6)} %select_n.145), kind=kLoop, calls=%fused_computation.3 | loop fusion | bytes 637448 | tf_op jit(solution)/shard_map/dynamic_slice | solution.py:187
  13.5 0.9 reshape.82
  17.6 2.0 %collective-permute-start.4 = (f32[83,576]{1,0:T(8,128)}, f32[83,576]{1,0:T(8,128)S(1)}, u32[]{:S(2)}, u32[]{:S(2)}) collective-permute-start(f32[83,576]{1,0:T(8,128)} %copy.25), channel_id=1, source_target_pairs={{0,4},{1,5},{2,6},{3,7},{4,0},{5,1},{6,2},{7,3},{8,12},{9,13},{10,... | collective-permute-start | bytes 573704 | tf_op jit(solution)/shard_map/ppermute | solution.py:200
  19.7 1.3 %reshape.81.refs_0_ = bf16[83,960]{1,0:T(8,128)(2,1)S(1)} reshape(bf16[83,5,192]{2,1,0:T(8,128)(2,1)} %get-tuple-element.15) | data formatting | bytes 318720 | tf_op jit(solution)/shard_map/reshape | solution.py:187
  24.2 1.8 %collective-permute-done.4.refs_12_ = f32[83,576]{1,0:T(8,128)S(1)} collective-permute-done((f32[83,576]{1,0:T(8,128)}, f32[83,576]{1,0:T(8,128)S(1)}, u32[]{:S(2)}, u32[]{:S(2)}) %collective-permute-start.4) | collective-permute-done | bytes 191264 | tf_op jit(solution)/shard_map/ppermute | solution.py:200
  29.3 14.0 %shard_map.100 = (f32[83,576]{1,0:T(8,128)S(1)}, f32[83,576]{1,0:T(8,128)S(1)}) custom-call(f32[2]{0:T(128)S(1)} %broadcast_multiply_fusion.scal_ref, s32[2]{0:T(128)S(1)} %pad_add_fusion.flag_ref, bf16[83,960]{1,0:T(8,128)(2,1)S(1)} %reshape.81.refs_0_, bf16[83,960]{1,0:T(8,128)(2,1)S(1)} %collective-permute-done.1.refs_1_, bf16[83,384]{1,0:T(8,128)(2,1)S(1)} %copy-done.8, ...), custom_call_target="tpu_custom_call" | custom-call | flops 2641231872 | bytes 4194304 | tf_op jit(solution)/shard_map/pallas_call | solution.py:125
  44.0 4.2 %collective-permute-start.7 = (bf16[83,576]{1,0:T(8,128)(2,1)}, bf16[83,576]{1,0:T(8,128)(2,1)S(1)}, u32[]{:S(2)}, u32[]{:S(2)}) collective-permute-start(bf16[83,576]{1,0:T(8,128)(2,1)} %add_convert_fusion.2), channel_id=1, source_target_pairs={{0,8},{4,12},{8,16},{12,20},{16,24},{20,28},{1,9},{5,13},{9,17},{1... | collective-permute-start | bytes 286856 | tf_op jit(solution)/shard_map/ppermute | solution.py:155
  48.3 5.1 %collective-permute-start.6 = (bf16[83,576]{1,0:T(8,128)(2,1)}, bf16[83,576]{1,0:T(8,128)(2,1)}, u32[]{:S(2)}, u32[]{:S(2)}) collective-permute-start(bf16[83,576]{1,0:T(8,128)(2,1)} %add_convert_fusion.2), channel_id=1, source_target_pairs={{0,16},{4,20},{8,24},{12,28},{1,17},{5,21},{9,25},{13,29},{2,18},{... | collective-permute-start | bytes 286856 | tf_op jit(solution)/shard_map/ppermute | solution.py:155
  53.4 1.9 %collective-permute-start.5 = (bf16[83,576]{1,0:T(8,128)(2,1)}, bf16[83,576]{1,0:T(8,128)(2,1)}, u32[]{:S(2)}, u32[]{:S(2)}) collective-permute-start(bf16[83,576]{1,0:T(8,128)(2,1)} %add_convert_fusion.2), channel_id=1, source_target_pairs={{0,24},{4,28},{1,25},{5,29},{2,26},{6,30},{3,27},{7,31}} | collective-permute-start | bytes 286856 | tf_op jit(solution)/shard_map/ppermute | solution.py:155
  55.3 2.4 %dynamic-slice_reduce_fusion.2 = bf16[83,3,192]{2,1,0:T(4,128)(2,1)} fusion(bf16[1,83,6,192]{3,0,2,1:T(2,128)(2,1)} %copy-done.12, s32[]{:T(128)S(6)} %select_n.149), kind=kLoop, calls=%fused_computation.5 | loop fusion | bytes 191236 | tf_op jit(solution)/shard_map/dynamic_slice | solution.py:187
  57.8 1.7 %reshape.89 = bf16[83,576]{1,0:T(8,128)(2,1)} reshape(bf16[83,3,192]{2,1,0:T(4,128)(2,1)} %dynamic-slice_reduce_fusion.2) | data formatting | bytes 191232 | tf_op jit(solution)/shard_map/reshape | solution.py:187
  59.5 1.2 %fusion.2 = (bf16[1,83,576]{2,1,0:T(8,128)(2,1)S(1)}, bf16[1,83,576]{2,1,0:T(8,128)(2,1)S(1)}) fusion(bf16[83,576]{1,0:T(8,128)(2,1)} %reshape.89, pred[]{:T(512)S(6)} %eq.17, pred[]{:T(512)S(6)} %and.25, f32[83,576]{1,0:T(8,128)S(1)} %get-tuple-element.9, f32[83,576]{1,0:T(8,128)S(1)} %get-tuple-element.10, pred[]{:T(512)S(6)} %eq.16, ...), kind=kLoop, calls=%fused_computation.25 | loop fusion | flops 717120 | bytes 1147397 | tf_op jit(solution)/shard_map/stack | solution.py:224
  61.5 1.6 %collective-permute-start.8 = (bf16[2,83,384]{2,1,0:T(8,128)(2,1)S(1)}, bf16[2,83,384]{2,1,0:T(8,128)(2,1)S(1)}, u32[]{:S(2)}, u32[]{:S(2)}) collective-permute-start(bf16[2,83,384]{2,1,0:T(8,128)(2,1)S(1)} %get-tuple-element.28), channel_id=1, source_target_pairs={{0,4},{1,5},{2,6},{3,7},{4,0},{5,1},{6,2},{7,3},{8,12},{9,13},{10,... | collective-permute-start | bytes 382472 | tf_op jit(solution)/shard_map/ppermute | solution.py:226
  63.1 1.4 %collective-permute-start.9 = (bf16[2,83,384]{2,1,0:T(8,128)(2,1)}, bf16[2,83,384]{2,1,0:T(8,128)(2,1)}, u32[]{:S(2)}, u32[]{:S(2)}) collective-permute-start(bf16[2,83,384]{2,1,0:T(8,128)(2,1)} %get-tuple-element.27), channel_id=1, source_target_pairs={{1,2},{2,1},{4,5},{5,4},{6,7},{7,6},{9,10},{10,9},{12,13},{13,12},... | collective-permute-start | bytes 382472 | tf_op jit(solution)/shard_map/ppermute | solution.py:227
  64.5 2.2 %collective-permute-done.8 = bf16[2,83,384]{2,1,0:T(8,128)(2,1)S(1)} collective-permute-done((bf16[2,83,384]{2,1,0:T(8,128)(2,1)S(1)}, bf16[2,83,384]{2,1,0:T(8,128)(2,1)S(1)}, u32[]{:S(2)}, u32[]{:S(2)}) %collective-permute-start.8) | collective-permute-done | bytes 127520 | tf_op jit(solution)/shard_map/ppermute | solution.py:226
  67.5 1.1 %maximum_select_fusion.1 = bf16[2,83,960]{2,1,0:T(8,128)(2,1)S(1)} fusion(bf16[2,83,384]{2,1,0:T(8,128)(2,1)} %rev.3, bf16[1,83,576]{2,1,0:T(8,128)(2,1)S(1)} %copy-done.19, bf16[1,83,576]{2,1,0:T(8,128)(2,1)S(1)} %copy-done.17, pred[]{:T(512)S(6)} %eq.14), kind=kLoop, calls=%fused_computation.4 | loop fusion | flops 2071680 | bytes 637441 | tf_op jit(solution)/shard_map/jit(_where)/select_n | solution.py:229
  68.6 1.0 slice_bitcast_fusion.2
  69.6 1.2 %copy-done.3 = bf16[1024,512]{1,0:T(8,128)(2,1)S(1)} copy-done((bf16[1024,512]{1,0:T(8,128)(2,1)S(1)}, bf16[1024,512]{1,0:T(8,128)(2,1)}, u32[]{:S(2)}) %copy-start.3) | copy-done | bytes 1048600
  70.8 14.0 %shard_map.101 = (f32[83,576]{1,0:T(8,128)S(1)}, f32[83,576]{1,0:T(8,128)S(1)}) custom-call(f32[2]{0:T(128)S(1)} %broadcast_multiply_fusion.scal_ref, s32[2]{0:T(128)S(1)} %pad_add_fusion.flag_ref, bf16[83,960]{1,0:T(8,128)(2,1)S(1)} %get-tuple-element.26.refs_0_, bf16[83,960]{1,0:T(8,128)(2,1)S(1)} %get-tuple-element.25.refs_1_, ...), custom_call_target="tpu_custom_call" | custom-call | flops 2641231872 | bytes 4194304 | tf_op jit(solution)/shard_map/pallas_call | solution.py:125
  84.9 0.9 subtract_convert_fusion
  85.8 2.4 %collective-permute-start.12 = (bf16[83,576]{1,0:T(8,128)(2,1)S(1)}, bf16[83,576]{1,0:T(8,128)(2,1)S(1)}, u32[]{:S(2)}, u32[]{:S(2)}) collective-permute-start(bf16[83,576]{1,0:T(8,128)(2,1)S(1)} %subtract_convert_fusion), channel_id=1, source_target_pairs={{0,8},{4,12},{8,16},{12,20},{16,24},{20,28},{1,9},{5,13},{9,17},{1... | collective-permute-start | bytes 286856 | tf_op jit(solution)/shard_map/ppermute | solution.py:155
  88.2 5.4 %collective-permute-start.11 = (bf16[83,576]{1,0:T(8,128)(2,1)S(1)}, bf16[83,576]{1,0:T(8,128)(2,1)S(1)}, u32[]{:S(2)}, u32[]{:S(2)}) collective-permute-start(bf16[83,576]{1,0:T(8,128)(2,1)S(1)} %subtract_convert_fusion), channel_id=1, source_target_pairs={{0,16},{4,20},{8,24},{12,28},{1,17},{5,21},{9,25},{13,29},{2,18},{... | collective-permute-start | bytes 286856 | tf_op jit(solution)/shard_map/ppermute | solution.py:155
  93.6 1.3 %collective-permute-start.10 = (bf16[83,576]{1,0:T(8,128)(2,1)S(1)}, bf16[83,576]{1,0:T(8,128)(2,1)S(1)}, u32[]{:S(2)}, u32[]{:S(2)}) collective-permute-start(bf16[83,576]{1,0:T(8,128)(2,1)S(1)} %subtract_convert_fusion), channel_id=1, source_target_pairs={{0,24},{4,28},{1,25},{5,29},{2,26},{6,30},{3,27},{7,31}} | collective-permute-start | bytes 286856 | tf_op jit(solution)/shard_map/ppermute | solution.py:155
  94.9 2.2 %collective-permute-done.11 = bf16[83,576]{1,0:T(8,128)(2,1)S(1)} collective-permute-done((bf16[83,576]{1,0:T(8,128)(2,1)S(1)}, bf16[83,576]{1,0:T(8,128)(2,1)S(1)}, u32[]{:S(2)}, u32[]{:S(2)}) %collective-permute-start.11) | collective-permute-done | bytes 95648 | tf_op jit(solution)/shard_map/ppermute | solution.py:155
  97.1 1.4 %collective-permute-done.10 = bf16[83,576]{1,0:T(8,128)(2,1)S(1)} collective-permute-done((bf16[83,576]{1,0:T(8,128)(2,1)S(1)}, bf16[83,576]{1,0:T(8,128)(2,1)S(1)}, u32[]{:S(2)}, u32[]{:S(2)}) %collective-permute-start.10) | collective-permute-done | bytes 95648 | tf_op jit(solution)/shard_map/ppermute | solution.py:155
  98.5 1.1 select_add_fusion.1
  99.7 6.5 %collective-permute-done.13 = f32[83,576]{1,0:T(8,128)S(1)} collective-permute-done((f32[83,576]{1,0:T(8,128)S(1)}, f32[83,576]{1,0:T(8,128)S(1)}, u32[]{:S(2)}, u32[]{:S(2)}) %collective-permute-start.13) | collective-permute-done | bytes 191264 | tf_op jit(solution)/shard_map/ppermute | solution.py:233
  106.2 1.1 %broadcast_select_fusion.5 = (f32[83,576]{1,0:T(8,128)S(1)}, f32[83,576]{1,0:T(8,128)S(1)}) fusion(f32[83,576]{1,0:T(8,128)S(1)} %collective-permute-done.13, pred[]{:T(512)S(6)} %eq.14, f32[83,576]{1,0:T(8,128)S(1)} %get-tuple-element.11, f32[83,576]{1,0:T(8,128)S(1)} %get-tuple-element.12, pred[]{:T(512)S(6)} %eq.16, pred[]{:T(512)S(6)} %eq.17, ...), kind=kLoop, calls=%fused_computation.32 | loop fusion | flops 717120 | bytes 1529859 | tf_op jit(solution)/shard_map/jit(_where)/select_n | solution.py:235
  108.6 1.1 %copy.31 = f32[1,83,6,192]{3,0,2,1:T(1,128)} copy(f32[1,83,6,192]{1,3,2,0:T(8,128)S(1)} %maximum_select_fusion) | data formatting | bytes 764928 | tf_op jit(solution)/shard_map/jit(_where)/select_n | solution.py:238
  (80 shorter events, 15.6 us)
Async XLA Ops:
  0.0 22.3 %copy-start = (f32[512,512]{1,0:T(8,128)S(1)}, f32[512,512]{1,0:T(8,128)}, u32[]{:S(2)}) copy-start(f32[512,512]{1,0:T(8,128)} %param.14) | copy-start | bytes 3145732
  0.0 21.3 %collective-permute-start = (s32[1]{0:T(128)}, s32[1]{0:T(128)}, u32[]{:S(2)}, u32[]{:S(2)}) collective-permute-start(s32[1]{0:T(128)} %param.12), channel_id=1, source_target_pairs={{0,4},{1,5},{2,6},{3,7},{4,0},{5,1},{6,2},{7,3},{8,12},{9,13},{10,... | collective-permute-start | bytes 20 | tf_op jit(solution)/shard_map/ppermute | solution.py:195
  4.4 9.1 %copy-start.12 = (bf16[1,83,6,192]{3,0,2,1:T(2,128)(2,1)}, bf16[1,83,6,192]{3,0,2,1:T(2,128)(2,1)S(1)}, u32[]{:S(2)}) copy-start(bf16[1,83,6,192]{3,0,2,1:T(2,128)(2,1)S(1)} %convert_element_type.48) | copy-start | bytes 573700
  6.1 16.8 %collective-permute-start.2 = (bf16[83,384]{1,0:T(8,128)(2,1)}, bf16[83,384]{1,0:T(8,128)(2,1)S(1)}, u32[]{:S(2)}, u32[]{:S(2)}) collective-permute-start(bf16[83,384]{1,0:T(8,128)(2,1)} %reshape.83), channel_id=1, source_target_pairs={{1,2},{2,1},{4,5},{5,4},{6,7},{7,6},{9,10},{10,9},{12,13},{13,12},... | collective-permute-start | bytes 191240 | tf_op jit(solution)/shard_map/ppermute | solution.py:192
  7.6 16.0 %collective-permute-start.3 = (bf16[83,384]{1,0:T(8,128)(2,1)}, bf16[83,384]{1,0:T(8,128)(2,1)S(1)}, u32[]{:S(2)}, u32[]{:S(2)}) collective-permute-start(bf16[83,384]{1,0:T(8,128)(2,1)} %reshape.84), channel_id=1, source_target_pairs={{0,5},{1,4},{2,7},{3,6},{5,2},{6,1},{8,13},{9,12},{10,15},{11,14},... | collective-permute-start | bytes 191240 | tf_op jit(solution)/shard_map/ppermute | solution.py:193
  13.5 1.6 %copy-start.15 = (f32[1,83,6,192]{3,0,2,1:T(1,128)S(1)}, f32[1,83,6,192]{3,0,2,1:T(1,128)}, u32[]{:S(2)}) copy-start(f32[1,83,6,192]{3,0,2,1:T(1,128)} %param.10) | copy-start | bytes 1147396
  14.4 9.8 %collective-permute-start.1 = (bf16[83,960]{1,0:T(8,128)(2,1)}, bf16[83,960]{1,0:T(8,128)(2,1)S(1)}, u32[]{:S(2)}, u32[]{:S(2)}) collective-permute-start(bf16[83,960]{1,0:T(8,128)(2,1)} %reshape.82), channel_id=1, source_target_pairs={{0,4},{1,5},{2,6},{3,7},{4,0},{5,1},{6,2},{7,3},{8,12},{9,13},{10,... | collective-permute-start | bytes 478088 | tf_op jit(solution)/shard_map/ppermute | solution.py:191
  15.1 1.0 copy-start.20
  15.6 1.1 %copy-start.13 = (f32[1,83,6,192]{1,3,2,0:T(8,128)}, f32[1,83,6,192]{1,3,2,0:T(8,128)S(1)}, u32[]{:S(2)}) copy-start(f32[1,83,6,192]{1,3,2,0:T(8,128)S(1)} %copy.30) | copy-start | bytes 1147396
  16.8 2.9 %copy-start.21 = (f32[512,25]{0,1:T(8,128)S(1)}, f32[512,25]{0,1:T(8,128)}, u32[]{:S(2)}) copy-start(f32[512,25]{0,1:T(8,128)} %param.15) | copy-start | bytes 153604
  17.6 8.3 %collective-permute-start.4 = (f32[83,576]{1,0:T(8,128)}, f32[83,576]{1,0:T(8,128)S(1)}, u32[]{:S(2)}, u32[]{:S(2)}) collective-permute-start(f32[83,576]{1,0:T(8,128)} %copy.25), channel_id=1, source_target_pairs={{0,4},{1,5},{2,6},{3,7},{4,0},{5,1},{6,2},{7,3},{8,12},{9,13},{10,... | collective-permute-start | bytes 573704 | tf_op jit(solution)/shard_map/ppermute | solution.py:200
  19.7 6.3 %copy-start.4 = (bf16[83,512]{1,0:T(8,128)(2,1)S(1)}, bf16[83,512]{1,0:T(8,128)(2,1)}, u32[]{:S(2)}) copy-start(bf16[83,512]{1,0:T(8,128)(2,1)} %refs_5_.3) | copy-start | bytes 254980
  19.7 6.3 %copy-start.1 = (bf16[512,1024]{1,0:T(8,128)(2,1)S(1)}, bf16[512,1024]{1,0:T(8,128)(2,1)}, u32[]{:S(2)}) copy-start(bf16[512,1024]{1,0:T(8,128)(2,1)} %refs_8_.3) | copy-start | bytes 3145732
  21.2 4.8 %copy-start.2 = (bf16[1024,512]{1,0:T(8,128)(2,1)S(1)}, bf16[1024,512]{1,0:T(8,128)(2,1)}, u32[]{:S(2)}) copy-start(bf16[1024,512]{1,0:T(8,128)(2,1)} %refs_9_.3) | copy-start | bytes 3145732
  26.7 0.9 copy-start.5
  27.6 0.9 copy-start.8
  28.4 0.9 copy-start.10
  44.0 15.4 %collective-permute-start.7 = (bf16[83,576]{1,0:T(8,128)(2,1)}, bf16[83,576]{1,0:T(8,128)(2,1)S(1)}, u32[]{:S(2)}, u32[]{:S(2)}) collective-permute-start(bf16[83,576]{1,0:T(8,128)(2,1)} %add_convert_fusion.2), channel_id=1, source_target_pairs={{0,8},{4,12},{8,16},{12,20},{16,24},{20,28},{1,9},{5,13},{9,17},{1... | collective-permute-start | bytes 286856 | tf_op jit(solution)/shard_map/ppermute | solution.py:155
  48.3 11.2 %collective-permute-start.6 = (bf16[83,576]{1,0:T(8,128)(2,1)}, bf16[83,576]{1,0:T(8,128)(2,1)}, u32[]{:S(2)}, u32[]{:S(2)}) collective-permute-start(bf16[83,576]{1,0:T(8,128)(2,1)} %add_convert_fusion.2), channel_id=1, source_target_pairs={{0,16},{4,20},{8,24},{12,28},{1,17},{5,21},{9,25},{13,29},{2,18},{... | collective-permute-start | bytes 286856 | tf_op jit(solution)/shard_map/ppermute | solution.py:155
  53.4 6.1 %collective-permute-start.5 = (bf16[83,576]{1,0:T(8,128)(2,1)}, bf16[83,576]{1,0:T(8,128)(2,1)}, u32[]{:S(2)}, u32[]{:S(2)}) collective-permute-start(bf16[83,576]{1,0:T(8,128)(2,1)} %add_convert_fusion.2), channel_id=1, source_target_pairs={{0,24},{4,28},{1,25},{5,29},{2,26},{6,30},{3,27},{7,31}} | collective-permute-start | bytes 286856 | tf_op jit(solution)/shard_map/ppermute | solution.py:155
  60.7 0.8 copy-start.16
  61.5 5.3 %collective-permute-start.8 = (bf16[2,83,384]{2,1,0:T(8,128)(2,1)S(1)}, bf16[2,83,384]{2,1,0:T(8,128)(2,1)S(1)}, u32[]{:S(2)}, u32[]{:S(2)}) collective-permute-start(bf16[2,83,384]{2,1,0:T(8,128)(2,1)S(1)} %get-tuple-element.28), channel_id=1, source_target_pairs={{0,4},{1,5},{2,6},{3,7},{4,0},{5,1},{6,2},{7,3},{8,12},{9,13},{10,... | collective-permute-start | bytes 382472 | tf_op jit(solution)/shard_map/ppermute | solution.py:226
  63.1 4.4 %copy-start.17 = (bf16[1,83,576]{2,1,0:T(8,128)(2,1)S(1)}, bf16[1,83,576]{2,1,0:T(8,128)(2,1)}, u32[]{:S(2)}) copy-start(bf16[1,83,576]{2,1,0:T(8,128)(2,1)} %copy-done.16) | copy-start | bytes 286852
  63.1 4.4 %copy-start.19 = (bf16[1,83,576]{2,1,0:T(8,128)(2,1)S(1)}, bf16[1,83,576]{2,1,0:T(8,128)(2,1)}, u32[]{:S(2)}) copy-start(bf16[1,83,576]{2,1,0:T(8,128)(2,1)} %copy-done.18) | copy-start | bytes 286852
  63.1 5.5 %collective-permute-start.9 = (bf16[2,83,384]{2,1,0:T(8,128)(2,1)}, bf16[2,83,384]{2,1,0:T(8,128)(2,1)}, u32[]{:S(2)}, u32[]{:S(2)}) collective-permute-start(bf16[2,83,384]{2,1,0:T(8,128)(2,1)} %get-tuple-element.27), channel_id=1, source_target_pairs={{1,2},{2,1},{4,5},{5,4},{6,7},{7,6},{9,10},{10,9},{12,13},{13,12},... | collective-permute-start | bytes 382472 | tf_op jit(solution)/shard_map/ppermute | solution.py:227
  68.6 1.0 copy-start.6
  69.6 1.2 %copy-start.3 = (bf16[1024,512]{1,0:T(8,128)(2,1)S(1)}, bf16[1024,512]{1,0:T(8,128)(2,1)}, u32[]{:S(2)}) copy-start(bf16[1024,512]{1,0:T(8,128)(2,1)} %refs_9_.3) | copy-start | bytes 3145732
  85.8 9.1 %collective-permute-start.12 = (bf16[83,576]{1,0:T(8,128)(2,1)S(1)}, bf16[83,576]{1,0:T(8,128)(2,1)S(1)}, u32[]{:S(2)}, u32[]{:S(2)}) collective-permute-start(bf16[83,576]{1,0:T(8,128)(2,1)S(1)} %subtract_convert_fusion), channel_id=1, source_target_pairs={{0,8},{4,12},{8,16},{12,20},{16,24},{20,28},{1,9},{5,13},{9,17},{1... | collective-permute-start | bytes 286856 | tf_op jit(solution)/shard_map/ppermute | solution.py:155
  88.2 8.9 %collective-permute-start.11 = (bf16[83,576]{1,0:T(8,128)(2,1)S(1)}, bf16[83,576]{1,0:T(8,128)(2,1)S(1)}, u32[]{:S(2)}, u32[]{:S(2)}) collective-permute-start(bf16[83,576]{1,0:T(8,128)(2,1)S(1)} %subtract_convert_fusion), channel_id=1, source_target_pairs={{0,16},{4,20},{8,24},{12,28},{1,17},{5,21},{9,25},{13,29},{2,18},{... | collective-permute-start | bytes 286856 | tf_op jit(solution)/shard_map/ppermute | solution.py:155
  93.6 4.9 %collective-permute-start.10 = (bf16[83,576]{1,0:T(8,128)(2,1)S(1)}, bf16[83,576]{1,0:T(8,128)(2,1)S(1)}, u32[]{:S(2)}, u32[]{:S(2)}) collective-permute-start(bf16[83,576]{1,0:T(8,128)(2,1)S(1)} %subtract_convert_fusion), channel_id=1, source_target_pairs={{0,24},{4,28},{1,25},{5,29},{2,26},{6,30},{3,27},{7,31}} | collective-permute-start | bytes 286856 | tf_op jit(solution)/shard_map/ppermute | solution.py:155
  99.6 6.6 %collective-permute-start.13 = (f32[83,576]{1,0:T(8,128)S(1)}, f32[83,576]{1,0:T(8,128)S(1)}, u32[]{:S(2)}, u32[]{:S(2)}) collective-permute-start(f32[83,576]{1,0:T(8,128)S(1)} %select_add_fusion.1), channel_id=1, source_target_pairs={{0,4},{1,5},{2,6},{3,7},{4,0},{5,1},{6,2},{7,3},{8,12},{9,13},{10,... | collective-permute-start | bytes 573704 | tf_op jit(solution)/shard_map/ppermute | solution.py:233
  107.5 1.1 copy-start.14
  (4 other events, 2.8 us)

commit v2 on v0

v2 whole, which is shorter than its diff:
```python
import functools
import math

import jax
import jax.numpy as jnp
from jax import lax
from jax.experimental import pallas as pl
from jax.experimental.pallas import tpu as pltpu
from jax.sharding import PartitionSpec as P

ITERS = 2
LEVELS = 1000
LANES = 128
LEAD = 8
RADIX = 4
BF16 = jnp.bfloat16
F32 = jnp.float32
VMEM = pl.BlockSpec(memory_space=pltpu.VMEM)
SMEM = pl.BlockSpec(memory_space=pltpu.SMEM)
ANY = pl.BlockSpec(memory_space=pl.ANY)
LIMIT = pltpu.CompilerParams(vmem_limit_bytes=48 << 20)


def place():
    t, l = lax.axis_index("tm"), lax.axis_index("lat")
    return t, l, t % 2, (t + l) % 2


def level_of(index):
    return 2.0 * jnp.exp(index * (math.log(0.1) / (LEVELS - 1)))


def prep_kernel(idx_ref, traj_ref, own_ref, swap_ref, side_ref, cross_ref, v_ref):
    channels, rows, _, lon = traj_ref.shape
    half = rows // 2
    _, _, _, h = place()
    for r in range(rows):
        v_ref[:, r * lon : (r + 1) * lon] = traj_ref[:, r, 0, :].astype(BF16)
    span, near = (half + 2) * lon, 2 * lon

    def cut(upper):
        low, high = v_ref[:, :span], v_ref[:, lon : lon + span]
        first, last = v_ref[:, :near], v_ref[:, (rows - 2) * lon :]
        own_ref[...] = low if upper else high
        swap_ref[:channels, :] = high if upper else low
        side_ref[...] = first if upper else last
        cross_ref[...] = last if upper else first

    @pl.when(h == 0)
    def _():
        cut(True)

    @pl.when(h == 1)
    def _():
        cut(False)

    index = idx_ref[0]
    swap_ref[channels : channels + 1, :] = jnp.full((1, span), index // 32, F32).astype(BF16)
    swap_ref[channels + 1 : channels + 2, :] = jnp.full((1, span), index % 32, F32).astype(BF16)


def noise_kernel(idx_ref, traj_ref, noise_ref, own_ref, send_ref):
    channels, rows, _, lon = traj_ref.shape
    half = rows // 2
    t, _, _, h = place()
    scale = 0.125 * jnp.sqrt(level_of(jnp.full((1, lon), idx_ref[0], F32)))
    anchor = jnp.where(t == 0, 1.0, 0.0)
    for r in range(rows):
        value = scale * noise_ref[:, r, 0, :] + anchor * traj_ref[:, r, 0, :]
        here = h == r // half
        cols = slice((r % half) * lon, (r % half + 1) * lon)

        @pl.when(here)
        def _():
            own_ref[:, cols] = value

        @pl.when(jnp.logical_not(here))
        def _():
            send_ref[:, cols] = value


def denoise_kernel(first, sizes, *refs):
    half, lon, chunks, ff = sizes
    width = chunks * LANES
    channels = None
    refs = list(refs)

    def take(n):
        got = refs[:n]
        del refs[:n]
        return got

    (idx_ref,) = take(1)
    if first:
        own5, part5, outer_own, outer_part = take(4)
        (time_hbm,) = take(1)
    else:
        s_own, s_part, inner, outer = take(4)
        cond_in, coef_in, sent_in = take(3)
    hbm = take(8)
    sent_ref, even_ref, total_ref = take(3)
    if first:
        cond_ref, coef_ref = take(2)
    else:
        cond_ref, coef_ref = cond_in, coef_in
    bufs = take(8)
    if first:
        (time_buf,) = take(1)
    act_ref, conv_ref, norm_ref, hid_ref, bo_ref, sems = take(6)
    emb_ref, dw_ref, gain_ref, up_ref, down_ref, out_ref, g0_ref, g1_ref = bufs

    t, l, y, h = place()
    bands = lax.axis_size("lat")
    copies = [pltpu.make_async_copy(s, d, sems.at[i]) for i, (s, d) in enumerate(zip(hbm, bufs))]
    if first:
        copies.append(pltpu.make_async_copy(time_hbm, time_buf, sems.at[8]))
        copies[8].start()
    for c in copies[:8]:
        c.start()
    emb_c, dw_c, gain_c, up_c, down_c, out_c, g0_c, g1_c = copies[:8]

    if first:
        quarter = width // 2
        mine = jnp.full((1, quarter), idx_ref[0], F32)
        rows = part5.shape[0]
        theirs = part5[83:84, :quarter].astype(F32) * 32.0 + part5[84:85, :quarter].astype(F32)
        index = jnp.concatenate([mine, theirs, jnp.zeros((6, quarter), F32)], axis=0)
        level = level_of(index)
        coef_ref[...] = 0.125 * level[:, :LANES]
        step = lax.broadcasted_iota(jnp.int32, (8, quarter), 1).astype(F32)
        angle = jnp.log(level) * jnp.exp(step * (-math.log(100.0) / quarter))
        features = jnp.concatenate([jnp.cos(angle), jnp.sin(angle)], axis=1)
        copies[8].wait()
        z = jnp.dot(features, time_buf[...], precision=lax.Precision.HIGHEST, preferred_element_type=F32)
        cond_ref[...] = z / (1.0 + jnp.exp(-z))

    emb_c.wait()
    emb = emb_ref[...]
    channels = emb.shape[0]
    border = jnp.where(jnp.where(h == 0, l > 0, l < bands - 1), 1.0, 0.0)
    inside = 5 * (1 - h)
    outside = 5 * h
    for slot in range(2):
        cond = cond_ref[slot : slot + 1, :]
        if first:
            pieces = (
                ((own5, part5)[slot][:channels, :], 2 * (1 - h), None),
                ((outer_own, outer_part)[slot][...], outside, border),
            )
        else:
            near = 2 * lon
            back = slice((1 - slot) * near, (2 - slot) * near)
            pieces = (
                ((s_own, s_part)[slot][...], 2, None),
                (inner[:, back], inside, None),
                (outer[:, slot * near : (slot + 1) * near], outside, border),
            )
        for value, base, scale in pieces:
            turned = value.T
            for r in range(value.shape[1] // lon):
                z = jnp.dot(turned[r * lon : (r + 1) * lon, :], emb, preferred_element_type=F32)
                a = (z + cond).astype(BF16).astype(F32)
                if scale is not None:
                    a = a * scale
                for c in range(chunks):
                    piece = a[:, c * LANES : (c + 1) * LANES]
                    act_ref[slot, c, base + r, LEAD : LEAD + lon, :] = piece
                    act_ref[slot, c, base + r, 0:LEAD, :] = piece[lon - LEAD : lon, :]
                    act_ref[slot, c, base + r, LEAD + lon : 2 * LEAD + lon, :] = piece[0:LEAD, :]

    part = lon // 2

    def conv(i):
        slot, o, flip = i // half, i % half, i % 2
        for c in range(chunks):
            for p in range(2):
                total = None
                for rr in range(5):
                    for j in range(5):
                        x = act_ref[slot, c, o + rr, LEAD - 2 + j + p * part : LEAD - 2 + j + (p + 1) * part, :]
                        x = x * dw_ref[rr * 5 + j : rr * 5 + j + 1, c * LANES : (c + 1) * LANES]
                        total = x if total is None else total + x
                conv_ref[c, p * part : (p + 1) * part, :] = total
        for p in range(2):
            x = [conv_ref[c, p * part : (p + 1) * part, :] for c in range(chunks)]
            mean = jnp.sum(functools.reduce(jnp.add, x), axis=1, keepdims=True) * (1.0 / width)
            x = [v - mean for v in x]
            var = jnp.sum(functools.reduce(jnp.add, [v * v for v in x]), axis=1, keepdims=True) * (1.0 / width)
            inv = lax.rsqrt(var + 1e-06)
            for c, v in enumerate(x):
                lane = slice(c * LANES, (c + 1) * LANES)
                norm_ref[flip, p * part : (p + 1) * part, lane] = (v * inv * gain_ref[:, lane]).astype(BF16)

    def mix(i):
        slot, o, flip = i // half, i % half, i % 2
        n = norm_ref[flip]
        k0 = math.sqrt(2.0 / math.pi)
        for b in range(0, ff, 256):
            u = jnp.dot(n, up_ref[:, b : b + 256], preferred_element_type=F32)
            hid_ref[:, b : b + 256] = (u + u * jnp.tanh(u * (k0 + (k0 * 0.044715) * (u * u)))).astype(BF16)
        for b in range(0, width, 256):
            d = jnp.dot(hid_ref[...], down_ref[:, b : b + 256], preferred_element_type=F32)
            for k in range(2):
                a = act_ref[slot, b // LANES + k, 2 + o, LEAD : LEAD + lon, :]
                lane = slice(b + k * LANES, b + (k + 1) * LANES)
                value = (a + 0.5 * d[:, k * LANES : (k + 1) * LANES]).astype(BF16)
                bo_ref[slot, pl.ds(pl.multiple_of(o * lon, 16), lon), lane] = value

    dw_c.wait()
    gain_c.wait()
    conv(0)
    up_c.wait()
    down_c.wait()

    def both(i, carry):
        conv(i)
        mix(i - 1)
        return carry

    lax.fori_loop(1, 2 * half, both, 0)
    mix(2 * half - 1)

    out_c.wait()
    g0_c.wait()
    g1_c.wait()
    incs = []
    for slot, g_ref in enumerate((g0_ref, g1_ref)):
        drift = lax.dot_general(out_ref[...], bo_ref[slot], (((1,), (1,)), ((), ())), preferred_element_type=F32)
        inc = coef_ref[slot : slot + 1, 0:1] * drift + g_ref[...]
        incs.append(inc)

        @pl.when(y == slot)
        def _():
            even_ref[...] = inc

    total = incs[0] + incs[1]
    if not first:
        total = total - sent_in[...].astype(F32)
    total_ref[...] = total
    sent_ref[...] = total.astype(BF16)


def denoise(first, head, weights, half, lon):
    emb, dw, gain, up, down, out, g_own, g_part = weights
    channels, points = g_own.shape
    width, ff = up.shape
    chunks = width // LANES
    grid = jax.ShapeDtypeStruct((channels, points), F32)
    outs = [jax.ShapeDtypeStruct((channels, points), BF16), grid, grid]
    if first:
        outs += [jax.ShapeDtypeStruct((8, width), F32), jax.ShapeDtypeStruct((8, LANES), F32)]
        specs = [SMEM] + [VMEM] * 4 + [ANY]
    else:
        specs = [SMEM] + [VMEM] * 7
    scratch = [pltpu.VMEM(w.shape, w.dtype) for w in weights]
    if first:
        scratch.append(pltpu.VMEM(head[-1].shape, F32))
    scratch += [
        pltpu.VMEM((2, chunks, half + 4, lon + 2 * LEAD, LANES), F32),
        pltpu.VMEM((chunks, lon, LANES), F32),
        pltpu.VMEM((2, lon, width), BF16),
        pltpu.VMEM((lon, ff), BF16),
        pltpu.VMEM((2, points, width), BF16),
        pltpu.SemaphoreType.DMA((9,)),
    ]
    flops = 2 * 2 * points * width * (channels * 2 + 2 * ff + 25)
    return pl.pallas_call(
        functools.partial(denoise_kernel, first, (half, lon, chunks, ff)),
        out_shape=tuple(outs),
        in_specs=specs + [ANY] * 8,
        out_specs=tuple([VMEM] * len(outs)),
        scratch_shapes=scratch,
        cost_estimate=pl.CostEstimate(flops=flops, bytes_accessed=4 << 20, transcendentals=2 * points * ff),
        compiler_params=LIMIT,
        name="denoise_first" if first else "denoise_later",
    )(*head, *weights)


def middle_kernel(count, lon, *refs):
    gots, refs = refs[:count], refs[count:]
    even, own5, part5, sum_ref, own_ref, part_ref, inner_ref, outer_ref = refs
    channels, points = even.shape
    t, _, y, h = place()
    near = 2 * lon
    total = gots[0][...].astype(F32)
    for g in gots[1:]:
        total = total + g[...].astype(F32)
    sum_ref[...] = total
    odd = (total + even[...]).astype(BF16)
    flat = total.astype(BF16)

    def emit(parity, upper):
        shift = 0 if upper else near
        start = (own5 if parity == 0 else part5)[:channels, shift : shift + points]
        state = jnp.where(t < 2, start.astype(F32), flat.astype(F32)).astype(BF16)
        pair = (state, odd) if parity == 0 else (odd, state)
        own_ref[...] = pair[0]
        part_ref[...] = pair[1]
        for k, s in enumerate(pair):
            cols = slice(k * near, (k + 1) * near)
            low, high = s[:, :near], s[:, points - near :]
            inner_ref[:, cols] = high if upper else low
            outer_ref[:, cols] = low if upper else high

    for parity in range(2):
        for half_at in range(2):

            @pl.when((y == parity) & (h == half_at))
            def _():
                emit(parity, half_at == 0)


def ending_kernel(count, *refs):
    gots, (before, even, mine_ref, send_ref) = refs[:count], refs[count:]
    _, _, y, _ = place()
    total = before[...]
    for g in gots:
        total = total + g[...].astype(F32)
    odd = total + even[...]
    mine_ref[...] = jnp.where(y == 0, total, odd)
    send_ref[...] = jnp.where(y == 0, odd, total)


def output_kernel(mine, other, traj_ref, out_ref):
    channels, rows, _, lon = out_ref.shape
    half = rows // 2
    t, _, _, h = place()
    for r in range(rows):
        cols = slice((r % half) * lon, (r % half + 1) * lon)
        value = jnp.where(h == r // half, mine[:, cols], other[:, cols])
        out_ref[:, r, 0, :] = jnp.where(t == 0, traj_ref[:, r, 0, :], value)


def call(body, outs, ins, specs=None, scratch=(), name=None):
    return pl.pallas_call(
        body,
        out_shape=tuple(jax.ShapeDtypeStruct(s, d) for s, d in outs),
        in_specs=specs or [VMEM] * len(ins),
        out_specs=tuple([VMEM] * len(outs)),
        scratch_shapes=list(scratch),
        compiler_params=LIMIT,
        name=name,
    )(*ins)


def exchange(sent, total, groups, memory):
    gots, kept = [], []
    base, moved, unit = sent, None, 1
    while unit < groups:
        if unit > 1:
            rest = memory[len(kept)] if memory else 0.0
            sent = (total + moved + rest).astype(BF16)
            kept.append(base.astype(F32) + moved + rest - sent.astype(F32))
        for step in range(RADIX - 1, 0, -1):
            shift = 2 * step * unit
            if shift < 2 * groups:
                gots.append(lax.ppermute(sent, "tm", [(i, i + shift) for i in range(2 * groups - shift)]))
        unit *= RADIX
        if groups > RADIX:
            moved = functools.reduce(jnp.add, [g.astype(F32) for g in gots])
    return gots, kept


def shards(
    traj, noise, step_index, embed_weight, time_weight, dw_weight, ln_gain, up_weight, down_weight, out_weight,
):
    times, bands = lax.axis_size("tm"), lax.axis_size("lat")
    groups = times // 2
    channels, rows, lon = traj.shape[1:]
    half = rows // 2
    width = embed_weight.shape[1]
    points, span, near = half * lon, (half + 2) * lon, 2 * lon
    axes = ("tm", "lat")

    def at(a, b):
        return a * bands + b

    cells = [(a, b, (a + b) % 2) for a in range(times) for b in range(bands)]
    swap = [(at(a, b), at(a ^ 1, b)) for a, b, _ in cells]
    side = [(at(a, b), at(a, b + (1 if c else -1))) for a, b, c in cells if 0 <= b + (1 if c else -1) < bands]
    cross = [(at(a, b), at(a ^ 1, b + (-1 if c else 1))) for a, b, c in cells if 0 <= b + (-1 if c else 1) < bands]

    root = traj.reshape(channels, rows, 1, lon)
    draws = noise.reshape(channels, rows, 1, lon)
    own5, to_swap, to_side, to_cross = call(
        prep_kernel,
        [((channels, span), BF16), ((88, span), BF16), ((channels, near), BF16), ((channels, near), BF16)],
        (step_index, root),
        [SMEM, VMEM],
        [pltpu.VMEM((channels, rows * lon), BF16)],
        "prep",
    )
    part5 = lax.ppermute(to_swap, axes, swap)
    outer_part = lax.ppermute(to_cross, axes, cross)
    outer_own = lax.ppermute(to_side, axes, side)
    g_own, g_send = call(
        noise_kernel, [((channels, points), F32)] * 2, (step_index, root, draws), [SMEM, VMEM, VMEM], name="noise"
    )
    g_part = lax.ppermute(g_send, axes, swap)
    weights = (
        embed_weight, dw_weight.T, ln_gain.reshape(1, width), up_weight, down_weight, out_weight.T, g_own, g_part,
    )

    sent, even, total, cond, coef = denoise(
        True, (step_index, own5, part5, outer_own, outer_part, time_weight), weights, half, lon
    )
    gots, memory = exchange(sent, total, groups, None)
    before = None
    for picard_step in range(1, ITERS):
        before, s_own, s_part, inner, outer = call(
            functools.partial(middle_kernel, len(gots), lon),
            [((channels, points), F32)] + [((channels, points), BF16)] * 2 + [((channels, 2 * near), BF16)] * 2,
            (*gots, even, own5, part5),
            name="middle",
        )
        inner = lax.ppermute(inner, axes, swap)
        outer = lax.ppermute(outer, axes, side)
        known = sent
        sent, even, total = denoise(False, (step_index, s_own, s_part, inner, outer, cond, coef, known), weights, half, lon)
        gots, memory = exchange(sent, total, groups, memory)
    mine, send = call(
        functools.partial(ending_kernel, len(gots)),
        [((channels, points), F32)] * 2,
        (*gots, before, even),
        name="ending",
    )
    other = lax.ppermute(send, axes, swap)
    (result,) = call(output_kernel, [((channels, rows, 1, lon), F32)], (mine, other, root), name="output")
    return result.reshape(1, channels, rows, lon)


def solution(mesh):
    in_specs = (P("tm", None, "lat", None), P("tm", None, "lat", None), P("tm")) + (P(),) * 7
    out_specs = P("tm", None, "lat", None)
    return jax.shard_map(shards, mesh=mesh, in_specs=in_specs, out_specs=out_specs, check_vma=False)
```

time: 320 us -> 94.2 us (0.29); the launches traced: 314 us -> 93.7 us
  waiting for transfers between devices: 238 us -> 23.7 us
  Pallas kernels: 0 us -> 33.3 us
  other arithmetic: 25.8 us -> 0 us
  starting transfers between devices: 6.4 us -> 30.7 us
  matrix products: 18.1 us -> 0 us
  between operations: 14.9 us -> 0.88 us
  local copies, waits for them, and re-layouts: 9.97 us -> 5.2 us
    all_gather x2 -> x0, waiting for transfers between devices: 158 us -> none  [entering(): gathered = lax.all_gather(part, axis)]
    psum x1 -> x0, waiting for transfers between devices: 74.6 us -> none  [spread(): return lax.psum(kept, axis)]
    pallas_call x0 -> x7, Pallas kernels: none -> 33.3 us  [the longest x2 30.2 us: denoise(): pl.pallas_call(functools.partial(denoise_kernel, first, (half, lon, chunk...]
    ppermute x4 -> x13, starting transfers between devices: 6.32 us -> 30.7 us  [the longest x6 19.5 us: exchange(): lax.ppermute(sent, 'tm', [(i, i + shift) for i in range(2 * groups - shif...]
    reduce_sum x4 -> x0, other arithmetic: 18.7 us -> none  [the longest x2 17.7 us: denoise(): average = jnp.mean(convolved, axis=0)]
    dot_general x7 -> x0, matrix products: 18.1 us -> none  [the longest x2 8.2 us: denoise(): jnp.dot(out_weight.T, block_out, preferred_element_type=jnp.float32)]
    ppermute x4 -> x13, waiting for transfers between devices: 6.04 us -> 23.7 us  [the longest x1 8.36 us: shards(): other = lax.ppermute(send, axes, swap)]
    convert_element_type x6 -> x0, other arithmetic: 5.68 us -> none  [the longest x2 3.63 us: denoise(): current.astype(jnp.bfloat16).reshape(channels, lat_rows * lon_cols)]
  transfers between devices with their start and end apart: 7 -> 13, of which waited for: 5 -> 7; matrix products, arithmetic and copies ran while one was open for 1% -> 0% of each run, Pallas kernels for 0% -> 1%
where the time goes in v2:
time: 94.2 us; the launch traced here: 93.7 us
  Pallas kernels  33.3 us (35%)
  starting transfers between devices  30.7 us (33%)
  waiting for transfers between devices  23.7 us (25%)
  local copies, waits for them, and re-layouts  5.2 us (6%)
    pallas_call x2, Pallas kernels, denoise(): pl.pallas_call(functools.partial(denoise_kernel, first, (half, lon, chunk...  30.2 us
    ppermute x6, starting transfers between devices, exchange(): lax.ppermute(sent, 'tm', [(i, i + shift) for i in range(2 * groups - shif...  19.5 us
    ppermute x1, waiting for transfers between devices, shards(): other = lax.ppermute(send, axes, swap)  8.36 us
    ppermute x6, waiting for transfers between devices, exchange(): lax.ppermute(sent, 'tm', [(i, i + shift) for i in range(2 * groups - shif...  8.29 us
    ppermute x1, starting transfers between devices, shards(): outer_part = lax.ppermute(to_cross, axes, cross)  5.27 us
    unnamed x24, local copies, waits for them, and re-layouts  5.2 us
    ppermute x1, waiting for transfers between devices, shards(): inner = lax.ppermute(inner, axes, swap)  3.78 us
    ppermute x1, waiting for transfers between devices, shards(): outer_part = lax.ppermute(to_cross, axes, cross)  3.22 us
  transfers between devices with their start and end apart: 13, of which 7 were waited for; matrix products, arithmetic and copies ran while one was open for 0% of the time, Pallas kernels for 1%

profile of v2, /device:TPU:0, one launch (start us, length us, event | category | flops | bytes accessed | tf_op | source)
XLA Modules:
  0.0 93.7 jit_solution(15486531083864622967)
XLA Ops:
  0.7 1.0 %copy-done = f32[1,83,6,192]{3,0,2,1:T(1,128)S(1)} copy-done((f32[1,83,6,192]{3,0,2,1:T(1,128)S(1)}, f32[1,83,6,192]{3,0,2,1:T(1,128)}, u32[]{:S(2)}) %copy-start) | copy-done | bytes 382488
  1.7 1.0 %copy-done.2 = f32[1,83,6,192]{3,0,2,1:T(1,128)S(1)} copy-done((f32[1,83,6,192]{3,0,2,1:T(1,128)S(1)}, f32[1,83,6,192]{3,0,2,1:T(1,128)}, u32[]{:S(2)}) %copy-start.2) | copy-done | bytes 382488
  2.7 0.7 noise.1
  3.4 3.1 %collective-permute-start.3 = (f32[83,576]{1,0:T(8,128)S(1)}, f32[83,576]{1,0:T(8,128)S(1)}, u32[]{:S(2)}, u32[]{:S(2)}) collective-permute-start(f32[83,576]{1,0:T(8,128)S(1)} %get-tuple-element.29), channel_id=1, source_target_pairs={{0,4},{1,5},{2,6},{3,7},{4,0},{5,1},{6,2},{7,3},{8,12},{9,13},{10,... | collective-permute-start | bytes 573704 | tf_op jit(solution)/shard_map/ppermute | solution.py:399
  6.5 0.8 prep.1
  7.3 0.1 collective-permute-start
  7.4 0.7 collective-permute-start.1
  8.1 5.3 %collective-permute-start.2 = (bf16[83,384]{1,0:T(8,128)(2,1)S(1)}, bf16[83,384]{1,0:T(8,128)(2,1)S(1)}, u32[]{:S(2)}, u32[]{:S(2)}) collective-permute-start(bf16[83,384]{1,0:T(8,128)(2,1)S(1)} %get-tuple-element.27), channel_id=1, source_target_pairs={{0,5},{1,4},{2,7},{3,6},{5,2},{6,1},{8,13},{9,12},{10,15},{11,14},... | collective-permute-start | bytes 191240 | tf_op jit(solution)/shard_map/ppermute | solution.py:394
  13.4 3.2 %collective-permute-done.2.refs_4_ = bf16[83,384]{1,0:T(8,128)(2,1)S(1)} collective-permute-done((bf16[83,384]{1,0:T(8,128)(2,1)S(1)}, bf16[83,384]{1,0:T(8,128)(2,1)S(1)}, u32[]{:S(2)}, u32[]{:S(2)}) %collective-permute-start.2) | collective-permute-done | bytes 63776 | tf_op jit(solution)/shard_map/ppermute | solution.py:394
  16.6 0.6 copy-done.11
  17.3 1.2 %copy-done.4 = bf16[512,1024]{1,0:T(8,128)(2,1)S(1)} copy-done((bf16[512,1024]{1,0:T(8,128)(2,1)S(1)}, bf16[512,1024]{1,0:T(8,128)(2,1)}, u32[]{:S(2)}) %copy-start.4) | copy-done | bytes 1048600
  18.5 1.2 %copy-done.6 = bf16[1024,512]{1,0:T(8,128)(2,1)S(1)} copy-done((bf16[1024,512]{1,0:T(8,128)(2,1)S(1)}, bf16[1024,512]{1,0:T(8,128)(2,1)}, u32[]{:S(2)}) %copy-start.6) | copy-done | bytes 1048600
  19.7 15.4 %denoise_first.1 = (bf16[83,576]{1,0:T(8,128)(2,1)S(1)}, f32[83,576]{1,0:T(8,128)S(1)}, f32[83,576]{1,0:T(8,128)}, f32[8,512]{1,0:T(8,128)S(1)}, f32[8,128]{1,0:T(8,128)S(1)}) custom-call(s32[1]{0:T(128)S(6)} %copy.11.idx_ref.refs_0_, bf16[83,960]{1,0:T(8,128)(2,1)S(1)} %get-tuple-element.24.refs_1_.refs_4_, ...), custom_call_target="tpu_custom_call" | custom-call | flops 2641231872 | bytes 4194304 | tf_op jit(solution)/shard_map/denoise_first/pallas_call | solution.py:267
  35.2 3.5 %collective-permute-start.6 = (bf16[83,576]{1,0:T(8,128)(2,1)S(1)}, bf16[83,576]{1,0:T(8,128)(2,1)S(1)}, u32[]{:S(2)}, u32[]{:S(2)}) collective-permute-start(bf16[83,576]{1,0:T(8,128)(2,1)S(1)} %get-tuple-element.30.refs_7_), channel_id=1, source_target_pairs={{0,8},{4,12},{8,16},{12,20},{16,24},{20,28},{1,9},{5,13},{9,17},{1... | collective-permute-start | bytes 286856 | tf_op jit(solution)/shard_map/ppermute | solution.py:357
  38.7 4.5 %collective-permute-start.5 = (bf16[83,576]{1,0:T(8,128)(2,1)S(1)}, bf16[83,576]{1,0:T(8,128)(2,1)S(1)}, u32[]{:S(2)}, u32[]{:S(2)}) collective-permute-start(bf16[83,576]{1,0:T(8,128)(2,1)S(1)} %get-tuple-element.30.refs_7_), channel_id=1, source_target_pairs={{0,16},{4,20},{8,24},{12,28},{1,17},{5,21},{9,25},{13,29},{2,18},{... | collective-permute-start | bytes 286856 | tf_op jit(solution)/shard_map/ppermute | solution.py:357
  43.2 1.3 %collective-permute-start.4 = (bf16[83,576]{1,0:T(8,128)(2,1)S(1)}, bf16[83,576]{1,0:T(8,128)(2,1)S(1)}, u32[]{:S(2)}, u32[]{:S(2)}) collective-permute-start(bf16[83,576]{1,0:T(8,128)(2,1)S(1)} %get-tuple-element.30.refs_7_), channel_id=1, source_target_pairs={{0,24},{4,28},{1,25},{5,29},{2,26},{6,30},{3,27},{7,31}} | collective-permute-start | bytes 286856 | tf_op jit(solution)/shard_map/ppermute | solution.py:357
  44.5 2.1 %collective-permute-done.5.refs_1_ = bf16[83,576]{1,0:T(8,128)(2,1)S(1)} collective-permute-done((bf16[83,576]{1,0:T(8,128)(2,1)S(1)}, bf16[83,576]{1,0:T(8,128)(2,1)S(1)}, u32[]{:S(2)}, u32[]{:S(2)}) %collective-permute-start.5) | collective-permute-done | bytes 95648 | tf_op jit(solution)/shard_map/ppermute | solution.py:357
  46.6 2.4 %collective-permute-done.4.refs_0_ = bf16[83,576]{1,0:T(8,128)(2,1)S(1)} collective-permute-done((bf16[83,576]{1,0:T(8,128)(2,1)S(1)}, bf16[83,576]{1,0:T(8,128)(2,1)S(1)}, u32[]{:S(2)}, u32[]{:S(2)}) %collective-permute-start.4) | collective-permute-done | bytes 95648 | tf_op jit(solution)/shard_map/ppermute | solution.py:357
  49.0 0.2 middle.1
  49.2 1.2 %collective-permute-start.7 = (bf16[83,768]{1,0:T(8,128)(2,1)S(1)}, bf16[83,768]{1,0:T(8,128)(2,1)S(1)}, u32[]{:S(2)}, u32[]{:S(2)}) collective-permute-start(bf16[83,768]{1,0:T(8,128)(2,1)S(1)} %get-tuple-element.34), channel_id=1, source_target_pairs={{0,4},{1,5},{2,6},{3,7},{4,0},{5,1},{6,2},{7,3},{8,12},{9,13},{10,... | collective-permute-start | bytes 382472 | tf_op jit(solution)/shard_map/ppermute | solution.py:416
  50.4 0.8 collective-permute-start.8
  51.2 3.8 %collective-permute-done.7.refs_3_ = bf16[83,768]{1,0:T(8,128)(2,1)S(1)} collective-permute-done((bf16[83,768]{1,0:T(8,128)(2,1)S(1)}, bf16[83,768]{1,0:T(8,128)(2,1)S(1)}, u32[]{:S(2)}, u32[]{:S(2)}) %collective-permute-start.7) | collective-permute-done | bytes 127520 | tf_op jit(solution)/shard_map/ppermute | solution.py:416
  55.0 14.7 %denoise_later.1 = (bf16[83,576]{1,0:T(8,128)(2,1)S(1)}, f32[83,576]{1,0:T(8,128)S(1)}, f32[83,576]{1,0:T(8,128)}) custom-call(s32[1]{0:T(128)S(6)} %copy.11.idx_ref.refs_0_, bf16[83,576]{1,0:T(8,128)(2,1)S(1)} %get-tuple-element.32.refs_1_, bf16[83,576]{1,0:T(8,128)(2,1)S(1)} %get-tuple-element.33.refs_2_, ...), custom_call_target="tpu_custom_call" | custom-call | flops 2641231872 | bytes 4194304 | tf_op jit(solution)/shard_map/denoise_later/pallas_call | solution.py:267
  69.8 3.9 %collective-permute-start.11 = (bf16[83,576]{1,0:T(8,128)(2,1)S(1)}, bf16[83,576]{1,0:T(8,128)(2,1)S(1)}, u32[]{:S(2)}, u32[]{:S(2)}) collective-permute-start(bf16[83,576]{1,0:T(8,128)(2,1)S(1)} %get-tuple-element.38), channel_id=1, source_target_pairs={{0,8},{4,12},{8,16},{12,20},{16,24},{20,28},{1,9},{5,13},{9,17},{1... | collective-permute-start | bytes 286856 | tf_op jit(solution)/shard_map/ppermute | solution.py:357
  73.7 5.0 %collective-permute-start.10 = (bf16[83,576]{1,0:T(8,128)(2,1)S(1)}, bf16[83,576]{1,0:T(8,128)(2,1)S(1)}, u32[]{:S(2)}, u32[]{:S(2)}) collective-permute-start(bf16[83,576]{1,0:T(8,128)(2,1)S(1)} %get-tuple-element.38), channel_id=1, source_target_pairs={{0,16},{4,20},{8,24},{12,28},{1,17},{5,21},{9,25},{13,29},{2,18},{... | collective-permute-start | bytes 286856 | tf_op jit(solution)/shard_map/ppermute | solution.py:357
  78.7 1.3 %collective-permute-start.9 = (bf16[83,576]{1,0:T(8,128)(2,1)S(1)}, bf16[83,576]{1,0:T(8,128)(2,1)S(1)}, u32[]{:S(2)}, u32[]{:S(2)}) collective-permute-start(bf16[83,576]{1,0:T(8,128)(2,1)S(1)} %get-tuple-element.38), channel_id=1, source_target_pairs={{0,24},{4,28},{1,25},{5,29},{2,26},{6,30},{3,27},{7,31}} | collective-permute-start | bytes 286856 | tf_op jit(solution)/shard_map/ppermute | solution.py:357
  80.1 1.3 %collective-permute-done.10.refs_1_ = bf16[83,576]{1,0:T(8,128)(2,1)S(1)} collective-permute-done((bf16[83,576]{1,0:T(8,128)(2,1)S(1)}, bf16[83,576]{1,0:T(8,128)(2,1)S(1)}, u32[]{:S(2)}, u32[]{:S(2)}) %collective-permute-start.10) | collective-permute-done | bytes 95648 | tf_op jit(solution)/shard_map/ppermute | solution.py:357
  81.4 2.4 %collective-permute-done.9.refs_0_ = bf16[83,576]{1,0:T(8,128)(2,1)S(1)} collective-permute-done((bf16[83,576]{1,0:T(8,128)(2,1)S(1)}, bf16[83,576]{1,0:T(8,128)(2,1)S(1)}, u32[]{:S(2)}, u32[]{:S(2)}) %collective-permute-start.9) | collective-permute-done | bytes 95648 | tf_op jit(solution)/shard_map/ppermute | solution.py:357
  83.8 0.1 ending.1
  83.9 0.1 collective-permute-start.12
  84.0 8.4 %collective-permute-done.12.other = f32[83,576]{1,0:T(8,128)S(1)} collective-permute-done((f32[83,576]{1,0:T(8,128)S(1)}, f32[83,576]{1,0:T(8,128)S(1)}, u32[]{:S(2)}, u32[]{:S(2)}) %collective-permute-start.12) | collective-permute-done | bytes 191264 | tf_op jit(solution)/shard_map/ppermute | solution.py:427
  92.3 1.4 %output.1 = f32[83,6,1,192]{3,2,1,0:T(1,128)} custom-call(f32[83,576]{1,0:T(8,128)S(1)} %get-tuple-element.41.mine, f32[83,576]{1,0:T(8,128)S(1)} %collective-permute-done.12.other, f32[83,6,1,192]{3,2,1,0:T(1,128)S(1)} %bitcast.8), custom_call_target="tpu_custom_call" | custom-call | tf_op jit(solution)/shard_map/output/pallas_call | solution.py:335
  (25 shorter events, 0.1 us)
Async XLA Ops:
  0.7 1.0 %copy-start = (f32[1,83,6,192]{3,0,2,1:T(1,128)S(1)}, f32[1,83,6,192]{3,0,2,1:T(1,128)}, u32[]{:S(2)}) copy-start(f32[1,83,6,192]{3,0,2,1:T(1,128)} %param.10) | copy-start | bytes 1147396
  1.7 1.0 %copy-start.2 = (f32[1,83,6,192]{3,0,2,1:T(1,128)S(1)}, f32[1,83,6,192]{3,0,2,1:T(1,128)}, u32[]{:S(2)}) copy-start(f32[1,83,6,192]{3,0,2,1:T(1,128)} %param.11) | copy-start | bytes 1147396
  2.7 13.9 %copy-start.3 = (f32[512,512]{1,0:T(8,128)S(1)}, f32[512,512]{1,0:T(8,128)}, u32[]{:S(2)}) copy-start(f32[512,512]{1,0:T(8,128)} %refs_5_.1) | copy-start | bytes 3145732
  3.4 13.2 %copy-start.8 = (bf16[83,512]{1,0:T(8,128)(2,1)S(1)}, bf16[83,512]{1,0:T(8,128)(2,1)}, u32[]{:S(2)}) copy-start(bf16[83,512]{1,0:T(8,128)(2,1)} %refs_8_.1) | copy-start | bytes 254980
  3.4 13.2 %copy-start.9 = (bf16[512,83]{0,1:T(8,128)(2,1)S(1)}, bf16[512,83]{0,1:T(8,128)(2,1)}, u32[]{:S(2)}) copy-start(bf16[512,83]{0,1:T(8,128)(2,1)} %param.19) | copy-start | bytes 254980
  3.4 13.2 %copy-start.10 = (f32[512,25]{0,1:T(8,128)S(1)}, f32[512,25]{0,1:T(8,128)}, u32[]{:S(2)}) copy-start(f32[512,25]{0,1:T(8,128)} %param.15) | copy-start | bytes 153604
  3.4 13.2 %collective-permute-start.3 = (f32[83,576]{1,0:T(8,128)S(1)}, f32[83,576]{1,0:T(8,128)S(1)}, u32[]{:S(2)}, u32[]{:S(2)}) collective-permute-start(f32[83,576]{1,0:T(8,128)S(1)} %get-tuple-element.29), channel_id=1, source_target_pairs={{0,4},{1,5},{2,6},{3,7},{4,0},{5,1},{6,2},{7,3},{8,12},{9,13},{10,... | collective-permute-start | bytes 573704 | tf_op jit(solution)/shard_map/ppermute | solution.py:399
  7.3 9.3 %collective-permute-start = (bf16[88,960]{1,0:T(8,128)(2,1)S(1)}, bf16[88,960]{1,0:T(8,128)(2,1)S(1)}, u32[]{:S(2)}, u32[]{:S(2)}) collective-permute-start(bf16[88,960]{1,0:T(8,128)(2,1)S(1)} %get-tuple-element.25), channel_id=1, source_target_pairs={{0,4},{1,5},{2,6},{3,7},{4,0},{5,1},{6,2},{7,3},{8,12},{9,13},{10,... | collective-permute-start | bytes 506888 | tf_op jit(solution)/shard_map/ppermute | solution.py:393
  7.4 6.0 %collective-permute-start.1 = (bf16[83,384]{1,0:T(8,128)(2,1)S(1)}, bf16[83,384]{1,0:T(8,128)(2,1)S(1)}, u32[]{:S(2)}, u32[]{:S(2)}) collective-permute-start(bf16[83,384]{1,0:T(8,128)(2,1)S(1)} %get-tuple-element.26), channel_id=1, source_target_pairs={{1,2},{2,1},{4,5},{5,4},{6,7},{7,6},{9,10},{10,9},{12,13},{13,12},... | collective-permute-start | bytes 191240 | tf_op jit(solution)/shard_map/ppermute | solution.py:395
  8.1 8.5 %collective-permute-start.2 = (bf16[83,384]{1,0:T(8,128)(2,1)S(1)}, bf16[83,384]{1,0:T(8,128)(2,1)S(1)}, u32[]{:S(2)}, u32[]{:S(2)}) collective-permute-start(bf16[83,384]{1,0:T(8,128)(2,1)S(1)} %get-tuple-element.27), channel_id=1, source_target_pairs={{0,5},{1,4},{2,7},{3,6},{5,2},{6,1},{8,13},{9,12},{10,15},{11,14},... | collective-permute-start | bytes 191240 | tf_op jit(solution)/shard_map/ppermute | solution.py:394
  16.6 0.7 copy-start.11
  17.3 1.2 %copy-start.4 = (bf16[512,1024]{1,0:T(8,128)(2,1)S(1)}, bf16[512,1024]{1,0:T(8,128)(2,1)}, u32[]{:S(2)}) copy-start(bf16[512,1024]{1,0:T(8,128)(2,1)} %refs_11_.1) | copy-start | bytes 3145732
  18.5 1.2 %copy-start.6 = (bf16[1024,512]{1,0:T(8,128)(2,1)S(1)}, bf16[1024,512]{1,0:T(8,128)(2,1)}, u32[]{:S(2)}) copy-start(bf16[1024,512]{1,0:T(8,128)(2,1)} %refs_12_.1) | copy-start | bytes 3145732
  19.7 35.3 %copy-start.5 = (bf16[512,1024]{1,0:T(8,128)(2,1)S(1)}, bf16[512,1024]{1,0:T(8,128)(2,1)}, u32[]{:S(2)}) copy-start(bf16[512,1024]{1,0:T(8,128)(2,1)} %refs_11_.1) | copy-start | bytes 3145732
  19.7 35.3 %copy-start.7 = (bf16[1024,512]{1,0:T(8,128)(2,1)S(1)}, bf16[1024,512]{1,0:T(8,128)(2,1)}, u32[]{:S(2)}) copy-start(bf16[1024,512]{1,0:T(8,128)(2,1)} %refs_12_.1) | copy-start | bytes 3145732
  35.2 9.3 %collective-permute-start.6 = (bf16[83,576]{1,0:T(8,128)(2,1)S(1)}, bf16[83,576]{1,0:T(8,128)(2,1)S(1)}, u32[]{:S(2)}, u32[]{:S(2)}) collective-permute-start(bf16[83,576]{1,0:T(8,128)(2,1)S(1)} %get-tuple-element.30.refs_7_), channel_id=1, source_target_pairs={{0,8},{4,12},{8,16},{12,20},{16,24},{20,28},{1,9},{5,13},{9,17},{1... | collective-permute-start | bytes 286856 | tf_op jit(solution)/shard_map/ppermute | solution.py:357
  38.7 7.9 %collective-permute-start.5 = (bf16[83,576]{1,0:T(8,128)(2,1)S(1)}, bf16[83,576]{1,0:T(8,128)(2,1)S(1)}, u32[]{:S(2)}, u32[]{:S(2)}) collective-permute-start(bf16[83,576]{1,0:T(8,128)(2,1)S(1)} %get-tuple-element.30.refs_7_), channel_id=1, source_target_pairs={{0,16},{4,20},{8,24},{12,28},{1,17},{5,21},{9,25},{13,29},{2,18},{... | collective-permute-start | bytes 286856 | tf_op jit(solution)/shard_map/ppermute | solution.py:357
  43.2 5.9 %collective-permute-start.4 = (bf16[83,576]{1,0:T(8,128)(2,1)S(1)}, bf16[83,576]{1,0:T(8,128)(2,1)S(1)}, u32[]{:S(2)}, u32[]{:S(2)}) collective-permute-start(bf16[83,576]{1,0:T(8,128)(2,1)S(1)} %get-tuple-element.30.refs_7_), channel_id=1, source_target_pairs={{0,24},{4,28},{1,25},{5,29},{2,26},{6,30},{3,27},{7,31}} | collective-permute-start | bytes 286856 | tf_op jit(solution)/shard_map/ppermute | solution.py:357
  49.2 5.8 %collective-permute-start.7 = (bf16[83,768]{1,0:T(8,128)(2,1)S(1)}, bf16[83,768]{1,0:T(8,128)(2,1)S(1)}, u32[]{:S(2)}, u32[]{:S(2)}) collective-permute-start(bf16[83,768]{1,0:T(8,128)(2,1)S(1)} %get-tuple-element.34), channel_id=1, source_target_pairs={{0,4},{1,5},{2,6},{3,7},{4,0},{5,1},{6,2},{7,3},{8,12},{9,13},{10,... | collective-permute-start | bytes 382472 | tf_op jit(solution)/shard_map/ppermute | solution.py:416
  50.4 4.6 %collective-permute-start.8 = (bf16[83,768]{1,0:T(8,128)(2,1)S(1)}, bf16[83,768]{1,0:T(8,128)(2,1)S(1)}, u32[]{:S(2)}, u32[]{:S(2)}) collective-permute-start(bf16[83,768]{1,0:T(8,128)(2,1)S(1)} %get-tuple-element.35), channel_id=1, source_target_pairs={{1,2},{2,1},{4,5},{5,4},{6,7},{7,6},{9,10},{10,9},{12,13},{13,12},... | collective-permute-start | bytes 382472 | tf_op jit(solution)/shard_map/ppermute | solution.py:417
  69.8 22.5 %copy-start.1 = (f32[1,83,6,192]{3,0,2,1:T(1,128)S(1)}, f32[1,83,6,192]{3,0,2,1:T(1,128)}, u32[]{:S(2)}) copy-start(f32[1,83,6,192]{3,0,2,1:T(1,128)} %param.10) | copy-start | bytes 1147396
  69.8 10.2 %collective-permute-start.11 = (bf16[83,576]{1,0:T(8,128)(2,1)S(1)}, bf16[83,576]{1,0:T(8,128)(2,1)S(1)}, u32[]{:S(2)}, u32[]{:S(2)}) collective-permute-start(bf16[83,576]{1,0:T(8,128)(2,1)S(1)} %get-tuple-element.38), channel_id=1, source_target_pairs={{0,8},{4,12},{8,16},{12,20},{16,24},{20,28},{1,9},{5,13},{9,17},{1... | collective-permute-start | bytes 286856 | tf_op jit(solution)/shard_map/ppermute | solution.py:357
  73.7 7.7 %collective-permute-start.10 = (bf16[83,576]{1,0:T(8,128)(2,1)S(1)}, bf16[83,576]{1,0:T(8,128)(2,1)S(1)}, u32[]{:S(2)}, u32[]{:S(2)}) collective-permute-start(bf16[83,576]{1,0:T(8,128)(2,1)S(1)} %get-tuple-element.38), channel_id=1, source_target_pairs={{0,16},{4,20},{8,24},{12,28},{1,17},{5,21},{9,25},{13,29},{2,18},{... | collective-permute-start | bytes 286856 | tf_op jit(solution)/shard_map/ppermute | solution.py:357
  78.7 5.1 %collective-permute-start.9 = (bf16[83,576]{1,0:T(8,128)(2,1)S(1)}, bf16[83,576]{1,0:T(8,128)(2,1)S(1)}, u32[]{:S(2)}, u32[]{:S(2)}) collective-permute-start(bf16[83,576]{1,0:T(8,128)(2,1)S(1)} %get-tuple-element.38), channel_id=1, source_target_pairs={{0,24},{4,28},{1,25},{5,29},{2,26},{6,30},{3,27},{7,31}} | collective-permute-start | bytes 286856 | tf_op jit(solution)/shard_map/ppermute | solution.py:357
  83.9 8.4 %collective-permute-start.12 = (f32[83,576]{1,0:T(8,128)S(1)}, f32[83,576]{1,0:T(8,128)S(1)}, u32[]{:S(2)}, u32[]{:S(2)}) collective-permute-start(f32[83,576]{1,0:T(8,128)S(1)} %get-tuple-element.42), channel_id=1, source_target_pairs={{0,4},{1,5},{2,6},{3,7},{4,0},{5,1},{6,2},{7,3},{8,12},{9,13},{10,... | collective-permute-start | bytes 573704 | tf_op jit(solution)/shard_map/ppermute | solution.py:427

commit v3 on v2

v3 whole, which is shorter than its diff:
```python
import functools
import math

import jax
import jax.numpy as jnp
from jax import lax
from jax.experimental import pallas as pl
from jax.experimental.pallas import tpu as pltpu
from jax.sharding import PartitionSpec as P

ITERS = 2
LEVELS = 1000
LANES = 128
LEAD = 8
RADIX = 4
BF16 = jnp.bfloat16
F32 = jnp.float32
VMEM = pl.BlockSpec(memory_space=pltpu.VMEM)
SMEM = pl.BlockSpec(memory_space=pltpu.SMEM)
HBM = pl.BlockSpec(memory_space=pltpu.HBM)
VMEM_OR_HBM = pl.BlockSpec(memory_space=pl.ANY)
PAD = 88
LIMIT = pltpu.CompilerParams(vmem_limit_bytes=48 << 20)


def place():
    t, l = lax.axis_index("tm"), lax.axis_index("lat")
    return t, l, t % 2, (t + l) % 2


def level_of(index):
    return 2.0 * jnp.exp(index * (math.log(0.1) / (LEVELS - 1)))


def prep_kernel(idx_ref, traj_hbm, own_ref, swap_ref, side_ref, cross_ref, traj_ref, v_ref, sem):
    channels, rows, _, lon = traj_ref.shape
    half = rows // 2
    _, _, _, h = place()
    copy = pltpu.make_async_copy(traj_hbm, traj_ref, sem)
    copy.start()
    v_ref[channels:, :] = jnp.ones((PAD - channels, rows * lon), BF16)
    copy.wait()
    for r in range(rows):
        v_ref[:channels, r * lon : (r + 1) * lon] = traj_ref[:, r, 0, :].astype(BF16)
    span, near = (half + 2) * lon, 2 * lon

    def cut(upper):
        low, high = v_ref[:, :span], v_ref[:, lon : lon + span]
        first, last = v_ref[:, :near], v_ref[:, (rows - 2) * lon :]
        own_ref[...] = low if upper else high
        swap_ref[...] = high if upper else low
        side_ref[...] = first if upper else last
        cross_ref[...] = last if upper else first

    @pl.when(h == 0)
    def _():
        cut(True)

    @pl.when(h == 1)
    def _():
        cut(False)

    index = idx_ref[0]
    swap_ref[PAD - 2 : PAD - 1, :] = jnp.full((1, span), index // 32, F32).astype(BF16)
    swap_ref[PAD - 1 : PAD, :] = jnp.full((1, span), index % 32, F32).astype(BF16)


def noise_kernel(idx_ref, after_ref, traj_hbm, noise_hbm, own_ref, send_ref, traj_ref, noise_ref, sems):
    channels, rows, _, lon = traj_ref.shape
    half = rows // 2
    t, _, _, h = place()
    copy = pltpu.make_async_copy(noise_hbm, noise_ref, sems.at[0])
    copy.start()
    scale = 0.125 * jnp.sqrt(level_of(jnp.full((1, lon), idx_ref[0], F32)))

    def emit(upper, anchored):
        for r in range(rows):
            value = scale * noise_ref[:, r, 0, :]
            if anchored:
                value = value + traj_ref[:, r, 0, :]
            cols = slice((r % half) * lon, (r % half + 1) * lon)
            target = own_ref if (r < half) == upper else send_ref
            target[:, cols] = value

    @pl.when(t == 0)
    def _():
        root = pltpu.make_async_copy(traj_hbm, traj_ref, sems.at[1])
        root.start()
        root.wait()

    copy.wait()
    for upper in (True, False):
        for anchored in (True, False):

            @pl.when((h == (0 if upper else 1)) & ((t == 0) == anchored))
            def _():
                emit(upper, anchored)


def spread_out(main, extra):
    done = 0
    for i, unit in enumerate(main):
        unit()
        while done < len(extra) and done * len(main) < (i + 1) * len(extra):
            extra[done]()
            done += 1
    for unit in extra[done:]:
        unit()


def denoise_kernel(first, sizes, *refs):
    half, lon, chunks, ff, channels = sizes
    width = chunks * LANES
    refs = list(refs)

    def take(n):
        got = refs[:n]
        del refs[:n]
        return got

    (idx_ref,) = take(1)
    if first:
        own5, part5, outer_own, outer_part = take(4)
        (time_hbm,) = take(1)
    else:
        s_own, s_part, inner, outer = take(4)
        emb_in, coef_ref, sent_in = take(3)
    hbm = take(8)
    sent_ref, even_ref, total_ref = take(3)
    if first:
        emb_all, coef_ref = take(2)
    else:
        emb_all = emb_in
    bufs = take(8)
    if first:
        (time_buf,) = take(1)
    act_ref, conv_ref, norm_ref, up_out, hid_ref, bo_ref, sems = take(7)
    emb_ref, dw_ref, gain_ref, up_ref, down_ref, out_ref, g0_ref, g1_ref = bufs

    t, l, y, h = place()
    copies = [pltpu.make_async_copy(s, d, sems.at[i]) for i, (s, d) in enumerate(zip(hbm, bufs))]
    emb_c, dw_c, gain_c, up_c, down_c, out_c, g0_c, g1_c = copies
    if first:
        time_c = pltpu.make_async_copy(time_hbm, time_buf, sems.at[8])
        time_c.start()
    for c in copies:
        c.start()

    if first:
        quarter = width // 2
        mine = jnp.full((1, quarter), idx_ref[0], F32)
        theirs = part5[PAD - 2 : PAD - 1, :quarter].astype(F32) * 32.0 + part5[PAD - 1 : PAD, :quarter].astype(F32)
        index = jnp.concatenate([mine, theirs, jnp.zeros((6, quarter), F32)], axis=0)
        level = level_of(index)
        coef_ref[...] = 0.125 * level[:, :LANES]
        step = lax.broadcasted_iota(jnp.int32, (8, quarter), 1).astype(F32)
        angle = jnp.log(level) * jnp.exp(step * (-math.log(100.0) / quarter))
        features = jnp.concatenate([jnp.cos(angle), jnp.sin(angle)], axis=1)
        time_c.wait()
        z = jnp.dot(features, time_buf[...], precision=lax.Precision.HIGHEST, preferred_element_type=F32)
        cond = z / (1.0 + jnp.exp(-z))
        emb_c.wait()
        for slot in range(2):
            emb_all[slot, :channels, :] = emb_ref[...]
            emb_all[slot, channels:, :] = jnp.zeros((PAD - channels, width), BF16)
            rest = cond[slot : slot + 1, :]
            for k in range(3):
                piece = rest.astype(BF16)
                emb_all[slot, channels + k : channels + k + 1, :] = piece
                rest = rest - piece.astype(F32)
    else:
        emb_c.wait()

    inside = 5 * (1 - h)
    outside = 5 * h

    def embed_units(slot):
        units = []
        if first:
            pieces = (((own5, part5)[slot], None, 2 * (1 - h)), ((outer_own, outer_part)[slot], None, outside))
        else:
            near = 2 * lon
            pieces = (
                ((s_own, s_part)[slot], None, 2),
                (inner, slice((1 - slot) * near, (2 - slot) * near), inside),
                (outer, slice(slot * near, (slot + 1) * near), outside),
            )
        for ref, cols, base in pieces:
            count = (ref.shape[1] if cols is None else cols.stop - cols.start) // lon
            held = []

            def unit(r, ref=ref, cols=cols, base=base, held=held):
                if not held:
                    held.append((ref[...] if cols is None else ref[:, cols]).T)
                rows = held[0][r * lon : (r + 1) * lon, :]
                a = jnp.dot(rows, emb_all[slot], preferred_element_type=F32).astype(BF16).astype(F32)
                for c in range(chunks):
                    piece = a[:, c * LANES : (c + 1) * LANES]
                    act_ref[slot, c, base + r, LEAD : LEAD + lon, :] = piece
                    act_ref[slot, c, base + r, 0:LEAD, :] = piece[lon - LEAD : lon, :]
                    act_ref[slot, c, base + r, LEAD + lon : 2 * LEAD + lon, :] = piece[0:LEAD, :]

            units += [functools.partial(unit, r) for r in range(count)]
        return units

    part = lon // 2
    tile = 24

    def conv_units(b):
        slot, p = b // 2, b % 2
        flip = b % 2

        def tile_unit(c, k):
            col = p * part + k * tile
            taps = [dw_ref[q : q + 1, c * LANES : (c + 1) * LANES] for q in range(25)]
            sums = [None] * half
            for rr in range(half + 4):
                for j in range(5):
                    at = LEAD - 2 + j + col
                    x = act_ref[slot, c, rr, at : at + tile, :]
                    for o in range(half):
                        if 0 <= rr - o < 5:
                            v = x * taps[(rr - o) * 5 + j]
                            sums[o] = v if sums[o] is None else sums[o] + v
            for o in range(half):
                conv_ref[flip, c, o, k * tile : (k + 1) * tile, :] = sums[o]

        def norm_unit(o, k):
            span = slice(k * 48, (k + 1) * 48)
            x = [conv_ref[flip, c, o, span, :] for c in range(chunks)]
            mean = jnp.sum(functools.reduce(jnp.add, x), axis=1, keepdims=True) * (1.0 / width)
            x = [v - mean for v in x]
            var = jnp.sum(functools.reduce(jnp.add, [v * v for v in x]), axis=1, keepdims=True) * (1.0 / width)
            inv = lax.rsqrt(var + 1e-06)
            for c, v in enumerate(x):
                lane = slice(c * LANES, (c + 1) * LANES)
                value = (v * inv * gain_ref[:, lane]).astype(BF16)
                norm_ref[flip, o * part + k * 48 : o * part + (k + 1) * 48, lane] = value

        return [functools.partial(tile_unit, c, k) for c in range(chunks) for k in range(part // tile)] + [
            functools.partial(norm_unit, o, k) for o in range(half) for k in range(part // 48)
        ]

    k0 = math.sqrt(2.0 / math.pi)

    def mix_units(b):
        slot, p = b // 2, b % 2
        flip = b % 2
        count = half * part

        def up_unit(n):
            up_out[n % 2] = jnp.dot(norm_ref[flip], up_ref[:, n * 256 : (n + 1) * 256], preferred_element_type=F32)

        def gelu_unit(n, o):
            u = up_out[n % 2, o * part : (o + 1) * part, :]
            value = (u + u * jnp.tanh(u * (k0 + (k0 * 0.044715) * (u * u)))).astype(BF16)
            hid_ref[flip, o * part : (o + 1) * part, n * 256 : (n + 1) * 256] = value

        def down_unit(m):
            d = jnp.dot(hid_ref[flip], down_ref[:, m * 256 : (m + 1) * 256], preferred_element_type=F32)
            for o in range(half):
                for k in range(2):
                    c = 2 * m + k
                    a = act_ref[slot, c, 2 + o, LEAD + p * part : LEAD + (p + 1) * part, :]
                    value = (a + 0.5 * d[o * part : (o + 1) * part, k * LANES : (k + 1) * LANES]).astype(BF16)
                    start = o * lon + p * part
                    bo_ref[slot, start : start + part, c * LANES : (c + 1) * LANES] = value

        steps = ff // 256
        units = [functools.partial(up_unit, 0)]
        for n in range(steps):
            if n + 1 < steps:
                units.append(functools.partial(up_unit, n + 1))
            units += [functools.partial(gelu_unit, n, o) for o in range(half)]
        return units + [functools.partial(down_unit, m) for m in range(width // 256)]

    incs = []

    def out_unit(slot):
        drift = lax.dot_general(out_ref[...], bo_ref[slot], (((1,), (1,)), ((), ())), preferred_element_type=F32)
        incs.append(coef_ref[slot : slot + 1, 0:1] * drift + (g0_ref, g1_ref)[slot][...])

    for unit in embed_units(0):
        unit()
    dw_c.wait()
    gain_c.wait()
    spread_out(conv_units(0), embed_units(1))
    up_c.wait()
    down_c.wait()
    spread_out(conv_units(1), mix_units(0))
    spread_out(conv_units(2), mix_units(1))
    out_c.wait()
    g0_c.wait()
    g1_c.wait()
    spread_out(conv_units(3), mix_units(2) + [functools.partial(out_unit, 0)])
    for unit in mix_units(3):
        unit()
    out_unit(1)

    for slot in range(2):

        @pl.when(y == slot)
        def _():
            even_ref[...] = incs[slot]

    total = incs[0] + incs[1]
    if not first:
        total = total - sent_in[...].astype(F32)
    total_ref[...] = total
    sent_ref[...] = total.astype(BF16)


def denoise(first, head, weights, half, lon):
    emb, dw, gain, up, down, out, g_own, g_part = weights
    channels, points = g_own.shape
    width, ff = up.shape
    chunks = width // LANES
    grid = jax.ShapeDtypeStruct((channels, points), F32)
    outs = [jax.ShapeDtypeStruct((channels, points), BF16), grid, grid]
    if first:
        outs += [jax.ShapeDtypeStruct((2, PAD, width), BF16), jax.ShapeDtypeStruct((8, LANES), F32)]
        specs = [SMEM] + [VMEM] * 4 + [HBM]
    else:
        specs = [SMEM] + [VMEM] * 7
    scratch = [pltpu.VMEM(w.shape, w.dtype) for w in weights]
    if first:
        scratch.append(pltpu.VMEM(head[-1].shape, F32))
    block = points // 2
    scratch += [
        pltpu.VMEM((2, chunks, half + 4, lon + 2 * LEAD, LANES), F32),
        pltpu.VMEM((2, chunks, half, lon // 2, LANES), F32),
        pltpu.VMEM((2, block, width), BF16),
        pltpu.VMEM((2, block, 256), F32),
        pltpu.VMEM((2, block, ff), BF16),
        pltpu.VMEM((2, points, width), BF16),
        pltpu.SemaphoreType.DMA((9,)),
    ]
    flops = 2 * 2 * points * width * (channels * 2 + 2 * ff + 25)
    return pl.pallas_call(
        functools.partial(denoise_kernel, first, (half, lon, chunks, ff, channels)),
        out_shape=tuple(outs),
        in_specs=specs + [HBM] * 6 + [VMEM_OR_HBM] * 2,
        out_specs=tuple([VMEM] * len(outs)),
        scratch_shapes=scratch,
        cost_estimate=pl.CostEstimate(flops=flops, bytes_accessed=4 << 20, transcendentals=2 * points * ff),
        compiler_params=LIMIT,
        name="denoise_first" if first else "denoise_later",
    )(*head, *weights)


def middle_kernel(count, lon, *refs):
    gots, refs = refs[:count], refs[count:]
    even, own5, part5, sum_ref, own_ref, part_ref, inner_ref, outer_ref = refs
    channels, points = even.shape
    t, _, y, h = place()
    near = 2 * lon
    total = gots[0][...].astype(F32)
    for g in gots[1:]:
        total = total + g[...].astype(F32)
    sum_ref[...] = total
    odd = (total + even[...]).astype(BF16)
    flat = total.astype(BF16)
    for ref in (own_ref, part_ref, inner_ref, outer_ref):
        ref[channels:, :] = jnp.ones((PAD - channels, ref.shape[1]), BF16)

    def emit(parity, upper):
        shift = 0 if upper else near
        start = (own5 if parity == 0 else part5)[:channels, shift : shift + points]
        state = jnp.where(t < 2, start.astype(F32), flat.astype(F32)).astype(BF16)
        pair = (state, odd) if parity == 0 else (odd, state)
        own_ref[:channels, :] = pair[0]
        part_ref[:channels, :] = pair[1]
        for k, s in enumerate(pair):
            cols = slice(k * near, (k + 1) * near)
            low, high = s[:, :near], s[:, points - near :]
            inner_ref[:channels, cols] = high if upper else low
            outer_ref[:channels, cols] = low if upper else high

    for parity in range(2):
        for half_at in range(2):

            @pl.when((y == parity) & (h == half_at))
            def _():
                emit(parity, half_at == 0)


def ending_kernel(count, *refs):
    gots, (before, even, mine_ref, send_ref) = refs[:count], refs[count:]
    _, _, y, _ = place()
    total = before[...]
    for g in gots:
        total = total + g[...].astype(F32)
    odd = total + even[...]
    mine_ref[...] = jnp.where(y == 0, total, odd)
    send_ref[...] = jnp.where(y == 0, odd, total)


def output_kernel(mine, other, traj_hbm, out_ref, sem):
    channels, rows, _, lon = out_ref.shape
    half = rows // 2
    t, _, _, h = place()

    def emit(upper):
        for r in range(rows):
            cols = slice((r % half) * lon, (r % half + 1) * lon)
            out_ref[:, r, 0, :] = (mine if (r < half) == upper else other)[:, cols]

    @pl.when((h == 0) & (t > 0))
    def _():
        emit(True)

    @pl.when((h == 1) & (t > 0))
    def _():
        emit(False)

    @pl.when(t == 0)
    def _():
        copy = pltpu.make_async_copy(traj_hbm, out_ref, sem)
        copy.start()
        copy.wait()


def call(body, outs, ins, specs=None, scratch=(), name=None):
    return pl.pallas_call(
        body,
        out_shape=tuple(jax.ShapeDtypeStruct(s, d) for s, d in outs),
        in_specs=specs or [VMEM] * len(ins),
        out_specs=tuple([VMEM] * len(outs)),
        scratch_shapes=list(scratch),
        compiler_params=LIMIT,
        name=name,
    )(*ins)


def exchange(sent, total, groups, memory):
    gots, kept = [], []
    base, moved, unit = sent, None, 1
    while unit < groups:
        if unit > 1:
            rest = memory[len(kept)] if memory else 0.0
            sent = (total + moved + rest).astype(BF16)
            kept.append(base.astype(F32) + moved + rest - sent.astype(F32))
        for step in range(1, RADIX):
            shift = 2 * step * unit
            if shift < 2 * groups:
                gots.append(lax.ppermute(sent, "tm", [(i, i + shift) for i in range(2 * groups - shift)]))
        unit *= RADIX
        if groups > RADIX:
            moved = functools.reduce(jnp.add, [g.astype(F32) for g in gots])
    return gots, kept


def shards(
    traj, noise, step_index, embed_weight, time_weight, dw_weight, ln_gain, up_weight, down_weight, out_weight,
):
    times, bands = lax.axis_size("tm"), lax.axis_size("lat")
    groups = times // 2
    channels, rows, lon = traj.shape[1:]
    half = rows // 2
    width = embed_weight.shape[1]
    points, span, near = half * lon, (half + 2) * lon, 2 * lon
    axes = ("tm", "lat")

    def at(a, b):
        return a * bands + b

    cells = [(a, b, (a + b) % 2) for a in range(times) for b in range(bands)]
    swap = [(at(a, b), at(a ^ 1, b)) for a, b, _ in cells]
    side = [(at(a, b), at(a, b + (1 if c else -1))) for a, b, c in cells if 0 <= b + (1 if c else -1) < bands]
    cross = [(at(a, b), at(a ^ 1, b + (-1 if c else 1))) for a, b, c in cells if 0 <= b + (-1 if c else 1) < bands]

    root = traj.reshape(channels, rows, 1, lon)
    draws = noise.reshape(channels, rows, 1, lon)
    band = (channels, rows, 1, lon)
    own5, to_swap, to_side, to_cross = call(
        prep_kernel,
        [((PAD, span), BF16), ((PAD, span), BF16), ((PAD, near), BF16), ((PAD, near), BF16)],
        (step_index, root),
        [SMEM, HBM],
        [pltpu.VMEM(band, F32), pltpu.VMEM((PAD, rows * lon), BF16), pltpu.SemaphoreType.DMA],
        "prep",
    )
    part5 = lax.ppermute(to_swap, axes, swap)
    outer_part = lax.ppermute(to_cross, axes, cross)
    outer_own = lax.ppermute(to_side, axes, side)
    g_own, g_send = call(
        noise_kernel,
        [((channels, points), F32)] * 2,
        (step_index, own5, root, draws),
        [SMEM, VMEM, HBM, HBM],
        [pltpu.VMEM(band, F32), pltpu.VMEM(band, F32), pltpu.SemaphoreType.DMA((2,))],
        "noise",
    )
    g_part = lax.ppermute(g_send, axes, swap)
    weights = (
        embed_weight, dw_weight.T, ln_gain.reshape(1, width), up_weight, down_weight, out_weight.T, g_own, g_part,
    )

    sent, even, total, emb_all, coef = denoise(
        True, (step_index, own5, part5, outer_own, outer_part, time_weight), weights, half, lon
    )
    gots, memory = exchange(sent, total, groups, None)
    before = None
    for picard_step in range(1, ITERS):
        before, s_own, s_part, inner, outer = call(
            functools.partial(middle_kernel, len(gots), lon),
            [((channels, points), F32)] + [((PAD, points), BF16)] * 2 + [((PAD, 2 * near), BF16)] * 2,
            (*gots, even, own5, part5),
            name="middle",
        )
        inner = lax.ppermute(inner, axes, swap)
        outer = lax.ppermute(outer, axes, side)
        known = sent
        sent, even, total = denoise(False, (step_index, s_own, s_part, inner, outer, emb_all, coef, known), weights, half, lon)
        gots, memory = exchange(sent, total, groups, memory)
    mine, send = call(
        functools.partial(ending_kernel, len(gots)),
        [((channels, points), F32)] * 2,
        (*gots, before, even),
        name="ending",
    )
    other = lax.ppermute(send, axes, swap)
    (result,) = call(
        output_kernel, [(band, F32)], (mine, other, root), [VMEM, VMEM, HBM], [pltpu.SemaphoreType.DMA], "output"
    )
    return result.reshape(1, channels, rows, lon)


def solution(mesh):
    in_specs = (P("tm", None, "lat", None), P("tm", None, "lat", None), P("tm")) + (P(),) * 7
    out_specs = P("tm", None, "lat", None)
    return jax.shard_map(shards, mesh=mesh, in_specs=in_specs, out_specs=out_specs, check_vma=False)
```

time: 94.2 us -> 87.7 us (0.931)
  the two profiles are of different devices: /device:TPU:0 before, /device:TPU:16 now
where the time goes in v3:
time: 87.7 us; the launch traced here: 87.2 us
  waiting for transfers between devices  35.7 us (41%)
  Pallas kernels  25.1 us (29%)
  starting transfers between devices  20.3 us (23%)
  local copies, waits for them, and re-layouts  5.06 us (6%)
  between operations  1.03 us (1%)
    pallas_call x2, Pallas kernels, denoise(): pl.pallas_call(functools.partial(denoise_kernel, first, (half, lon, chunk...  21.9 us
    ppermute x6, waiting for transfers between devices, exchange(): lax.ppermute(sent, 'tm', [(i, i + shift) for i in range(2 * groups - shif...  20.9 us
    ppermute x6, starting transfers between devices, exchange(): lax.ppermute(sent, 'tm', [(i, i + shift) for i in range(2 * groups - shif...  10.1 us
    ppermute x1, waiting for transfers between devices, shards(): other = lax.ppermute(send, axes, swap)  7.5 us
    unnamed x24, local copies, waits for them, and re-layouts  5.06 us
    ppermute x1, starting transfers between devices, shards(): outer_part = lax.ppermute(to_cross, axes, cross)  4.78 us
    ppermute x1, waiting for transfers between devices, shards(): outer_part = lax.ppermute(to_cross, axes, cross)  4.12 us
    pallas_call x5, Pallas kernels, call(): pl.pallas_call(body, out_shape=tuple((jax.ShapeDtypeStruct(s, d) for s, d...  3.21 us
  transfers between devices with their start and end apart: 13, of which 7 were waited for; matrix products, arithmetic and copies ran while one was open for 0% of the time, Pallas kernels for 0%

profile of v3, /device:TPU:16, one launch (start us, length us, event | category | flops | bytes accessed | tf_op | source)
XLA Modules:
  0.0 87.2 jit_solution(10509606401999984358)
XLA Ops:
  0.7 1.0 %copy-done = f32[1,83,6,192]{3,0,2,1:T(1,128)S(1)} copy-done((f32[1,83,6,192]{3,0,2,1:T(1,128)S(1)}, f32[1,83,6,192]{3,0,2,1:T(1,128)}, u32[]{:S(2)}) %copy-start) | copy-done | bytes 382488
  1.7 1.1 %prep.1 = (bf16[88,960]{1,0:T(8,128)(2,1)S(1)}, bf16[88,960]{1,0:T(8,128)(2,1)S(1)}, bf16[88,384]{1,0:T(8,128)(2,1)S(1)}, bf16[88,384]{1,0:T(8,128)(2,1)S(1)}) custom-call(s32[1]{0:T(128)S(6)} %copy.11.idx_ref.refs_0_, f32[83,6,1,192]{3,2,1,0:T(1,128)S(1)} %bitcast.6), custom_call_target="tpu_custom_call" | custom-call | tf_op jit(solution)/shard_map/prep/pallas_call | solution.py:424
  2.8 0.6 noise.1
  3.4 1.6 %collective-permute-start.3 = (f32[83,576]{1,0:T(8,128)S(1)}, f32[83,576]{1,0:T(8,128)S(1)}, u32[]{:S(2)}, u32[]{:S(2)}) collective-permute-start(f32[83,576]{1,0:T(8,128)S(1)} %get-tuple-element.29), channel_id=1, source_target_pairs={{0,4},{1,5},{2,6},{3,7},{4,0},{5,1},{6,2},{7,3},{8,12},{9,13},{10,... | collective-permute-start | bytes 573704 | tf_op jit(solution)/shard_map/ppermute | solution.py:494
  5.0 0.5 collective-permute-start
  5.5 0.7 collective-permute-start.1
  6.2 4.8 %collective-permute-start.2 = (bf16[88,384]{1,0:T(8,128)(2,1)S(1)}, bf16[88,384]{1,0:T(8,128)(2,1)S(1)}, u32[]{:S(2)}, u32[]{:S(2)}) collective-permute-start(bf16[88,384]{1,0:T(8,128)(2,1)S(1)} %get-tuple-element.27), channel_id=1, source_target_pairs={{0,5},{1,4},{2,7},{3,6},{5,2},{6,1},{8,13},{9,12},{10,15},{11,14},... | collective-permute-start | bytes 202760 | tf_op jit(solution)/shard_map/ppermute | solution.py:484
  11.0 4.1 %collective-permute-done.2.refs_4_ = bf16[88,384]{1,0:T(8,128)(2,1)S(1)} collective-permute-done((bf16[88,384]{1,0:T(8,128)(2,1)S(1)}, bf16[88,384]{1,0:T(8,128)(2,1)S(1)}, u32[]{:S(2)}, u32[]{:S(2)}) %collective-permute-start.2) | collective-permute-done | bytes 67616 | tf_op jit(solution)/shard_map/ppermute | solution.py:484
  15.1 0.7 copy-done.11
  15.8 1.2 %copy-done.4 = bf16[512,1024]{1,0:T(8,128)(2,1)S(1)} copy-done((bf16[512,1024]{1,0:T(8,128)(2,1)S(1)}, bf16[512,1024]{1,0:T(8,128)(2,1)}, u32[]{:S(2)}) %copy-start.4) | copy-done | bytes 1048600
  17.0 1.2 %copy-done.6 = bf16[1024,512]{1,0:T(8,128)(2,1)S(1)} copy-done((bf16[1024,512]{1,0:T(8,128)(2,1)S(1)}, bf16[1024,512]{1,0:T(8,128)(2,1)}, u32[]{:S(2)}) %copy-start.6) | copy-done | bytes 1048600
  18.2 0.9 %copy-done.9 = bf16[512,83]{0,1:T(8,128)(2,1)S(1)} copy-done((bf16[512,83]{0,1:T(8,128)(2,1)S(1)}, bf16[512,83]{0,1:T(8,128)(2,1)}, u32[]{:S(2)}) %copy-start.9) | copy-done | bytes 85016
  19.1 11.3 %denoise_first.1 = (bf16[83,576]{1,0:T(8,128)(2,1)S(1)}, f32[83,576]{1,0:T(8,128)S(1)}, f32[83,576]{1,0:T(8,128)}, bf16[2,88,512]{2,1,0:T(8,128)(2,1)S(1)}, f32[8,128]{1,0:T(8,128)S(1)}) custom-call(s32[1]{0:T(128)S(6)} %copy.11.idx_ref.refs_0_, bf16[88,960]{1,0:T(8,128)(2,1)S(1)} %get-tuple-element.24.after_ref.refs_1_.refs_4_, ...), custom_call_target="tpu_custom_call" | custom-call | flops 2641231872 | bytes 4194304 | tf_op jit(solution)/shard_map/denoise_first/pallas_call | solution.py:339
  30.5 0.7 collective-permute-start.6
  31.2 1.3 %collective-permute-start.5 = (bf16[83,576]{1,0:T(8,128)(2,1)S(1)}, bf16[83,576]{1,0:T(8,128)(2,1)S(1)}, u32[]{:S(2)}, u32[]{:S(2)}) collective-permute-start(bf16[83,576]{1,0:T(8,128)(2,1)S(1)} %get-tuple-element.30.refs_7_), channel_id=1, source_target_pairs={{0,16},{4,20},{8,24},{12,28},{1,17},{5,21},{9,25},{13,29},{2,18},{... | collective-permute-start | bytes 286856 | tf_op jit(solution)/shard_map/ppermute | solution.py:446
  32.5 4.1 %collective-permute-start.4 = (bf16[83,576]{1,0:T(8,128)(2,1)S(1)}, bf16[83,576]{1,0:T(8,128)(2,1)S(1)}, u32[]{:S(2)}, u32[]{:S(2)}) collective-permute-start(bf16[83,576]{1,0:T(8,128)(2,1)S(1)} %get-tuple-element.30.refs_7_), channel_id=1, source_target_pairs={{0,8},{4,12},{8,16},{12,20},{16,24},{20,28},{1,9},{5,13},{9,17},{1... | collective-permute-start | bytes 286856 | tf_op jit(solution)/shard_map/ppermute | solution.py:446
  36.6 6.1 %collective-permute-done.5.refs_1_ = bf16[83,576]{1,0:T(8,128)(2,1)S(1)} collective-permute-done((bf16[83,576]{1,0:T(8,128)(2,1)S(1)}, bf16[83,576]{1,0:T(8,128)(2,1)S(1)}, u32[]{:S(2)}, u32[]{:S(2)}) %collective-permute-start.5) | collective-permute-done | bytes 95648 | tf_op jit(solution)/shard_map/ppermute | solution.py:446
  42.7 4.3 %collective-permute-done.4.refs_0_ = bf16[83,576]{1,0:T(8,128)(2,1)S(1)} collective-permute-done((bf16[83,576]{1,0:T(8,128)(2,1)S(1)}, bf16[83,576]{1,0:T(8,128)(2,1)S(1)}, u32[]{:S(2)}, u32[]{:S(2)}) %collective-permute-start.4) | collective-permute-done | bytes 95648 | tf_op jit(solution)/shard_map/ppermute | solution.py:446
  47.0 0.4 middle.1
  47.4 1.9 %collective-permute-start.7 = (bf16[88,768]{1,0:T(8,128)(2,1)S(1)}, bf16[88,768]{1,0:T(8,128)(2,1)S(1)}, u32[]{:S(2)}, u32[]{:S(2)}) collective-permute-start(bf16[88,768]{1,0:T(8,128)(2,1)S(1)} %get-tuple-element.34), channel_id=1, source_target_pairs={{0,4},{1,5},{2,6},{3,7},{4,0},{5,1},{6,2},{7,3},{8,12},{9,13},{10,... | collective-permute-start | bytes 405512 | tf_op jit(solution)/shard_map/ppermute | solution.py:511
  49.3 0.7 collective-permute-start.8
  50.0 3.2 %collective-permute-done.7.refs_3_ = bf16[88,768]{1,0:T(8,128)(2,1)S(1)} collective-permute-done((bf16[88,768]{1,0:T(8,128)(2,1)S(1)}, bf16[88,768]{1,0:T(8,128)(2,1)S(1)}, u32[]{:S(2)}, u32[]{:S(2)}) %collective-permute-start.7) | collective-permute-done | bytes 135200 | tf_op jit(solution)/shard_map/ppermute | solution.py:511
  53.1 10.6 %denoise_later.1 = (bf16[83,576]{1,0:T(8,128)(2,1)S(1)}, f32[83,576]{1,0:T(8,128)S(1)}, f32[83,576]{1,0:T(8,128)}) custom-call(s32[1]{0:T(128)S(6)} %copy.11.idx_ref.refs_0_, bf16[88,576]{1,0:T(8,128)(2,1)S(1)} %get-tuple-element.32.refs_1_, bf16[88,576]{1,0:T(8,128)(2,1)S(1)} %get-tuple-element.33.refs_2_, ...), custom_call_target="tpu_custom_call" | custom-call | flops 2641231872 | bytes 4194304 | tf_op jit(solution)/shard_map/denoise_later/pallas_call | solution.py:339
  63.7 0.8 collective-permute-start.11
  64.5 1.3 %collective-permute-start.10 = (bf16[83,576]{1,0:T(8,128)(2,1)S(1)}, bf16[83,576]{1,0:T(8,128)(2,1)S(1)}, u32[]{:S(2)}, u32[]{:S(2)}) collective-permute-start(bf16[83,576]{1,0:T(8,128)(2,1)S(1)} %get-tuple-element.38), channel_id=1, source_target_pairs={{0,16},{4,20},{8,24},{12,28},{1,17},{5,21},{9,25},{13,29},{2,18},{... | collective-permute-start | bytes 286856 | tf_op jit(solution)/shard_map/ppermute | solution.py:446
  65.8 1.9 %collective-permute-start.9 = (bf16[83,576]{1,0:T(8,128)(2,1)S(1)}, bf16[83,576]{1,0:T(8,128)(2,1)S(1)}, u32[]{:S(2)}, u32[]{:S(2)}) collective-permute-start(bf16[83,576]{1,0:T(8,128)(2,1)S(1)} %get-tuple-element.38), channel_id=1, source_target_pairs={{0,8},{4,12},{8,16},{12,20},{16,24},{20,28},{1,9},{5,13},{9,17},{1... | collective-permute-start | bytes 286856 | tf_op jit(solution)/shard_map/ppermute | solution.py:446
  67.7 4.9 %collective-permute-done.10.refs_1_ = bf16[83,576]{1,0:T(8,128)(2,1)S(1)} collective-permute-done((bf16[83,576]{1,0:T(8,128)(2,1)S(1)}, bf16[83,576]{1,0:T(8,128)(2,1)S(1)}, u32[]{:S(2)}, u32[]{:S(2)}) %collective-permute-start.10) | collective-permute-done | bytes 95648 | tf_op jit(solution)/shard_map/ppermute | solution.py:446
  72.7 5.6 %collective-permute-done.9.refs_0_ = bf16[83,576]{1,0:T(8,128)(2,1)S(1)} collective-permute-done((bf16[83,576]{1,0:T(8,128)(2,1)S(1)}, bf16[83,576]{1,0:T(8,128)(2,1)S(1)}, u32[]{:S(2)}, u32[]{:S(2)}) %collective-permute-start.9) | collective-permute-done | bytes 95648 | tf_op jit(solution)/shard_map/ppermute | solution.py:446
  78.3 0.1 ending.1
  78.3 0.1 collective-permute-start.12
  78.4 7.5 %collective-permute-done.12.other = f32[83,576]{1,0:T(8,128)S(1)} collective-permute-done((f32[83,576]{1,0:T(8,128)S(1)}, f32[83,576]{1,0:T(8,128)S(1)}, u32[]{:S(2)}, u32[]{:S(2)}) %collective-permute-start.12) | collective-permute-done | bytes 191264 | tf_op jit(solution)/shard_map/ppermute | solution.py:522
  85.9 1.1 %output.1 = f32[83,6,1,192]{3,2,1,0:T(1,128)} custom-call(f32[83,576]{1,0:T(8,128)S(1)} %get-tuple-element.41.mine, f32[83,576]{1,0:T(8,128)S(1)} %collective-permute-done.12.other, f32[83,6,1,192]{3,2,1,0:T(1,128)S(1)} %bitcast.8), custom_call_target="tpu_custom_call" | custom-call | tf_op jit(solution)/shard_map/output/pallas_call | solution.py:424
  (25 shorter events, 0.1 us)
Async XLA Ops:
  0.7 1.0 %copy-start = (f32[1,83,6,192]{3,0,2,1:T(1,128)S(1)}, f32[1,83,6,192]{3,0,2,1:T(1,128)}, u32[]{:S(2)}) copy-start(f32[1,83,6,192]{3,0,2,1:T(1,128)} %param.10) | copy-start | bytes 1147396
  1.7 1.1 %copy-start.2 = (f32[1,83,6,192]{3,0,2,1:T(1,128)S(1)}, f32[1,83,6,192]{3,0,2,1:T(1,128)}, u32[]{:S(2)}) copy-start(f32[1,83,6,192]{3,0,2,1:T(1,128)} %param.11) | copy-start | bytes 1147396
  1.7 13.4 %copy-start.3 = (f32[512,512]{1,0:T(8,128)S(1)}, f32[512,512]{1,0:T(8,128)}, u32[]{:S(2)}) copy-start(f32[512,512]{1,0:T(8,128)} %refs_5_.1) | copy-start | bytes 3145732
  2.8 12.3 %copy-start.8 = (bf16[83,512]{1,0:T(8,128)(2,1)S(1)}, bf16[83,512]{1,0:T(8,128)(2,1)}, u32[]{:S(2)}) copy-start(bf16[83,512]{1,0:T(8,128)(2,1)} %refs_8_.1) | copy-start | bytes 254980
  2.8 12.3 %copy-start.10 = (f32[512,25]{0,1:T(8,128)S(1)}, f32[512,25]{0,1:T(8,128)}, u32[]{:S(2)}) copy-start(f32[512,25]{0,1:T(8,128)} %param.15) | copy-start | bytes 153604
  3.4 11.7 %collective-permute-start.3 = (f32[83,576]{1,0:T(8,128)S(1)}, f32[83,576]{1,0:T(8,128)S(1)}, u32[]{:S(2)}, u32[]{:S(2)}) collective-permute-start(f32[83,576]{1,0:T(8,128)S(1)} %get-tuple-element.29), channel_id=1, source_target_pairs={{0,4},{1,5},{2,6},{3,7},{4,0},{5,1},{6,2},{7,3},{8,12},{9,13},{10,... | collective-permute-start | bytes 573704 | tf_op jit(solution)/shard_map/ppermute | solution.py:494
  5.0 10.1 %collective-permute-start = (bf16[88,960]{1,0:T(8,128)(2,1)S(1)}, bf16[88,960]{1,0:T(8,128)(2,1)S(1)}, u32[]{:S(2)}, u32[]{:S(2)}) collective-permute-start(bf16[88,960]{1,0:T(8,128)(2,1)S(1)} %get-tuple-element.25), channel_id=1, source_target_pairs={{0,4},{1,5},{2,6},{3,7},{4,0},{5,1},{6,2},{7,3},{8,12},{9,13},{10,... | collective-permute-start | bytes 506888 | tf_op jit(solution)/shard_map/ppermute | solution.py:483
  5.5 5.5 %collective-permute-start.1 = (bf16[88,384]{1,0:T(8,128)(2,1)S(1)}, bf16[88,384]{1,0:T(8,128)(2,1)S(1)}, u32[]{:S(2)}, u32[]{:S(2)}) collective-permute-start(bf16[88,384]{1,0:T(8,128)(2,1)S(1)} %get-tuple-element.26), channel_id=1, source_target_pairs={{1,2},{2,1},{4,5},{5,4},{6,7},{7,6},{9,10},{10,9},{12,13},{13,12},... | collective-permute-start | bytes 202760 | tf_op jit(solution)/shard_map/ppermute | solution.py:485
  6.2 8.9 %collective-permute-start.2 = (bf16[88,384]{1,0:T(8,128)(2,1)S(1)}, bf16[88,384]{1,0:T(8,128)(2,1)S(1)}, u32[]{:S(2)}, u32[]{:S(2)}) collective-permute-start(bf16[88,384]{1,0:T(8,128)(2,1)S(1)} %get-tuple-element.27), channel_id=1, source_target_pairs={{0,5},{1,4},{2,7},{3,6},{5,2},{6,1},{8,13},{9,12},{10,15},{11,14},... | collective-permute-start | bytes 202760 | tf_op jit(solution)/shard_map/ppermute | solution.py:484
  15.1 0.7 copy-start.11
  15.8 1.2 %copy-start.4 = (bf16[512,1024]{1,0:T(8,128)(2,1)S(1)}, bf16[512,1024]{1,0:T(8,128)(2,1)}, u32[]{:S(2)}) copy-start(bf16[512,1024]{1,0:T(8,128)(2,1)} %refs_11_.1) | copy-start | bytes 3145732
  17.0 1.2 %copy-start.6 = (bf16[1024,512]{1,0:T(8,128)(2,1)S(1)}, bf16[1024,512]{1,0:T(8,128)(2,1)}, u32[]{:S(2)}) copy-start(bf16[1024,512]{1,0:T(8,128)(2,1)} %refs_12_.1) | copy-start | bytes 3145732
  18.2 0.9 %copy-start.9 = (bf16[512,83]{0,1:T(8,128)(2,1)S(1)}, bf16[512,83]{0,1:T(8,128)(2,1)}, u32[]{:S(2)}) copy-start(bf16[512,83]{0,1:T(8,128)(2,1)} %param.19) | copy-start | bytes 254980
  19.1 34.0 %copy-start.5 = (bf16[512,1024]{1,0:T(8,128)(2,1)S(1)}, bf16[512,1024]{1,0:T(8,128)(2,1)}, u32[]{:S(2)}) copy-start(bf16[512,1024]{1,0:T(8,128)(2,1)} %refs_11_.1) | copy-start | bytes 3145732
  19.1 34.0 %copy-start.7 = (bf16[1024,512]{1,0:T(8,128)(2,1)S(1)}, bf16[1024,512]{1,0:T(8,128)(2,1)}, u32[]{:S(2)}) copy-start(bf16[1024,512]{1,0:T(8,128)(2,1)} %refs_12_.1) | copy-start | bytes 3145732
  30.5 6.1 %collective-permute-start.6 = (bf16[83,576]{1,0:T(8,128)(2,1)S(1)}, bf16[83,576]{1,0:T(8,128)(2,1)S(1)}, u32[]{:S(2)}, u32[]{:S(2)}) collective-permute-start(bf16[83,576]{1,0:T(8,128)(2,1)S(1)} %get-tuple-element.30.refs_7_), channel_id=1, source_target_pairs={{0,24},{4,28},{1,25},{5,29},{2,26},{6,30},{3,27},{7,31}} | collective-permute-start | bytes 286856 | tf_op jit(solution)/shard_map/ppermute | solution.py:446
  31.2 11.6 %collective-permute-start.5 = (bf16[83,576]{1,0:T(8,128)(2,1)S(1)}, bf16[83,576]{1,0:T(8,128)(2,1)S(1)}, u32[]{:S(2)}, u32[]{:S(2)}) collective-permute-start(bf16[83,576]{1,0:T(8,128)(2,1)S(1)} %get-tuple-element.30.refs_7_), channel_id=1, source_target_pairs={{0,16},{4,20},{8,24},{12,28},{1,17},{5,21},{9,25},{13,29},{2,18},{... | collective-permute-start | bytes 286856 | tf_op jit(solution)/shard_map/ppermute | solution.py:446
  32.5 14.5 %collective-permute-start.4 = (bf16[83,576]{1,0:T(8,128)(2,1)S(1)}, bf16[83,576]{1,0:T(8,128)(2,1)S(1)}, u32[]{:S(2)}, u32[]{:S(2)}) collective-permute-start(bf16[83,576]{1,0:T(8,128)(2,1)S(1)} %get-tuple-element.30.refs_7_), channel_id=1, source_target_pairs={{0,8},{4,12},{8,16},{12,20},{16,24},{20,28},{1,9},{5,13},{9,17},{1... | collective-permute-start | bytes 286856 | tf_op jit(solution)/shard_map/ppermute | solution.py:446
  47.4 5.8 %collective-permute-start.7 = (bf16[88,768]{1,0:T(8,128)(2,1)S(1)}, bf16[88,768]{1,0:T(8,128)(2,1)S(1)}, u32[]{:S(2)}, u32[]{:S(2)}) collective-permute-start(bf16[88,768]{1,0:T(8,128)(2,1)S(1)} %get-tuple-element.34), channel_id=1, source_target_pairs={{0,4},{1,5},{2,6},{3,7},{4,0},{5,1},{6,2},{7,3},{8,12},{9,13},{10,... | collective-permute-start | bytes 405512 | tf_op jit(solution)/shard_map/ppermute | solution.py:511
  49.3 3.8 %collective-permute-start.8 = (bf16[88,768]{1,0:T(8,128)(2,1)S(1)}, bf16[88,768]{1,0:T(8,128)(2,1)S(1)}, u32[]{:S(2)}, u32[]{:S(2)}) collective-permute-start(bf16[88,768]{1,0:T(8,128)(2,1)S(1)} %get-tuple-element.35), channel_id=1, source_target_pairs={{1,2},{2,1},{4,5},{5,4},{6,7},{7,6},{9,10},{10,9},{12,13},{13,12},... | collective-permute-start | bytes 405512 | tf_op jit(solution)/shard_map/ppermute | solution.py:512
  63.7 22.3 %copy-start.1 = (f32[1,83,6,192]{3,0,2,1:T(1,128)S(1)}, f32[1,83,6,192]{3,0,2,1:T(1,128)}, u32[]{:S(2)}) copy-start(f32[1,83,6,192]{3,0,2,1:T(1,128)} %param.10) | copy-start | bytes 1147396
  63.7 4.0 %collective-permute-start.11 = (bf16[83,576]{1,0:T(8,128)(2,1)S(1)}, bf16[83,576]{1,0:T(8,128)(2,1)S(1)}, u32[]{:S(2)}, u32[]{:S(2)}) collective-permute-start(bf16[83,576]{1,0:T(8,128)(2,1)S(1)} %get-tuple-element.38), channel_id=1, source_target_pairs={{0,24},{4,28},{1,25},{5,29},{2,26},{6,30},{3,27},{7,31}} | collective-permute-start | bytes 286856 | tf_op jit(solution)/shard_map/ppermute | solution.py:446
  64.5 8.2 %collective-permute-start.10 = (bf16[83,576]{1,0:T(8,128)(2,1)S(1)}, bf16[83,576]{1,0:T(8,128)(2,1)S(1)}, u32[]{:S(2)}, u32[]{:S(2)}) collective-permute-start(bf16[83,576]{1,0:T(8,128)(2,1)S(1)} %get-tuple-element.38), channel_id=1, source_target_pairs={{0,16},{4,20},{8,24},{12,28},{1,17},{5,21},{9,25},{13,29},{2,18},{... | collective-permute-start | bytes 286856 | tf_op jit(solution)/shard_map/ppermute | solution.py:446
  65.8 12.4 %collective-permute-start.9 = (bf16[83,576]{1,0:T(8,128)(2,1)S(1)}, bf16[83,576]{1,0:T(8,128)(2,1)S(1)}, u32[]{:S(2)}, u32[]{:S(2)}) collective-permute-start(bf16[83,576]{1,0:T(8,128)(2,1)S(1)} %get-tuple-element.38), channel_id=1, source_target_pairs={{0,8},{4,12},{8,16},{12,20},{16,24},{20,28},{1,9},{5,13},{9,17},{1... | collective-permute-start | bytes 286856 | tf_op jit(solution)/shard_map/ppermute | solution.py:446
  78.3 7.6 %collective-permute-start.12 = (f32[83,576]{1,0:T(8,128)S(1)}, f32[83,576]{1,0:T(8,128)S(1)}, u32[]{:S(2)}, u32[]{:S(2)}) collective-permute-start(f32[83,576]{1,0:T(8,128)S(1)} %get-tuple-element.42), channel_id=1, source_target_pairs={{0,4},{1,5},{2,6},{3,7},{4,0},{5,1},{6,2},{7,3},{8,12},{9,13},{10,... | collective-permute-start | bytes 573704 | tf_op jit(solution)/shard_map/ppermute | solution.py:522

commit v4 on v3

v4 whole, which is shorter than its diff:
```python
import functools
import math

import jax
import jax.numpy as jnp
from jax import lax
from jax.experimental import pallas as pl
from jax.experimental.pallas import tpu as pltpu
from jax.sharding import PartitionSpec as P


ITERS = 2
LEVELS = 1000
LANES = 128
LEAD = 8
RADIX = 4
TILE = 24
BF16 = jnp.bfloat16
F32 = jnp.float32
VMEM = pl.BlockSpec(memory_space=pltpu.VMEM)
SMEM = pl.BlockSpec(memory_space=pltpu.SMEM)
HBM = pl.BlockSpec(memory_space=pltpu.HBM)
VMEM_OR_HBM = pl.BlockSpec(memory_space=pl.ANY)
PAD = 88
LIMIT = pltpu.CompilerParams(vmem_limit_bytes=24 << 20)


def place():
    t, l = lax.axis_index("tm"), lax.axis_index("lat")
    return t, l, t % 2, (t + l) % 2


def level_of(index):
    return 2.0 * jnp.exp(index * (math.log(0.1) / (LEVELS - 1)))


def prep_kernel(idx_ref, traj_hbm, own_ref, inner_ref, swap_ref, side_ref, cross_ref, traj_ref, v_ref, sem):
    channels, rows, _, lon = traj_ref.shape
    half = rows // 2
    _, _, _, h = place()
    copy = pltpu.make_async_copy(traj_hbm, traj_ref, sem)
    copy.start()
    v_ref[channels:, :] = jnp.ones((PAD - channels, rows * lon), BF16)
    copy.wait()
    for r in range(rows):
        v_ref[:channels, r * lon : (r + 1) * lon] = traj_ref[:, r, 0, :].astype(BF16)
    span, near = (half + 2) * lon, 2 * lon

    def cut(upper):
        low, high = v_ref[:, :span], v_ref[:, lon : lon + span]
        first, last = v_ref[:, :near], v_ref[:, (rows - 2) * lon :]
        own_ref[...] = v_ref[:, : half * lon] if upper else v_ref[:, half * lon :]
        inner_ref[...] = v_ref[:, half * lon : span] if upper else v_ref[:, lon : half * lon]
        swap_ref[...] = high if upper else low
        side_ref[...] = first if upper else last
        cross_ref[...] = last if upper else first

    @pl.when(h == 0)
    def _():
        cut(True)

    @pl.when(h == 1)
    def _():
        cut(False)

    index = idx_ref[0]
    swap_ref[PAD - 2 : PAD - 1, :] = jnp.full((1, span), index // 32, F32).astype(BF16)
    swap_ref[PAD - 1 : PAD, :] = jnp.full((1, span), index % 32, F32).astype(BF16)


def condition_of(index, time_weight):
    half_width = index.shape[1]
    level = level_of(index)
    step = lax.broadcasted_iota(jnp.int32, index.shape, 1).astype(F32)
    angle = jnp.log(level) * jnp.exp(step * (-math.log(100.0) / half_width))
    features = jnp.concatenate([jnp.cos(angle), jnp.sin(angle)], axis=1)
    z = jnp.dot(features, time_weight, precision=lax.Precision.HIGHEST, preferred_element_type=F32)
    return z / (1.0 + jnp.exp(-z)), level


def fill_embedding(all_ref, emb, cond):
    channels, width = emb.shape
    all_ref[:channels, :] = emb
    all_ref[channels:, :] = jnp.zeros((PAD - channels, width), BF16)
    rest = cond
    for k in range(3):
        piece = rest.astype(BF16)
        all_ref[channels + k : channels + k + 1, :] = piece
        rest = rest - piece.astype(F32)


def embed_row(turned, r, lon, emb_all):
    return jnp.dot(turned[r * lon : (r + 1) * lon, :], emb_all, preferred_element_type=F32).astype(BF16)


def store_row(act_ref, row, a, lon):
    a = a.astype(F32)
    for c in range(a.shape[1] // LANES):
        piece = a[:, c * LANES : (c + 1) * LANES]
        act_ref[c, row, LEAD : LEAD + lon, :] = piece
        act_ref[c, row, 0:LEAD, :] = piece[lon - LEAD : lon, :]
        act_ref[c, row, LEAD + lon : 2 * LEAD + lon, :] = piece[0:LEAD, :]


def conv_tile(act_ref, dw_ref, c, col, tile, half, rows, shift, sums):
    taps = {}
    for rr in rows:
        for j in range(5):
            at = LEAD - 2 + j + col
            x = act_ref[c, rr - shift, at : at + tile, :]
            for o in range(half):
                q = (rr - o) * 5 + j
                if 0 <= rr - o < 5:
                    if q not in taps:
                        taps[q] = dw_ref[q : q + 1, c * LANES : (c + 1) * LANES]
                    v = x * taps[q]
                    sums[o] = v if sums[o] is None else sums[o] + v
    return sums


def near_body(states, emb_alls, dw_ref, act_refs, keep_ref, partial_ref, half, lon):
    for slot, (state, emb_all, act_ref) in enumerate(zip(states, emb_alls, act_refs)):
        chunks = emb_all.shape[1] // LANES
        turned = state[...].T
        for r in range(half):
            a = embed_row(turned, r, lon, emb_all[...])
            keep_ref[slot, r * lon : (r + 1) * lon, :] = a
            store_row(act_ref, r, a, lon)
    for slot, act_ref in enumerate(act_refs):
        for c in range(chunks):
            for k in range(lon // TILE):
                rows = range(2, 2 + half)
                sums = conv_tile(act_ref, dw_ref, c, k * TILE, TILE, half, rows, 2, [None] * half)
                for o in range(half):
                    partial_ref[slot, c, o, k * TILE : (k + 1) * TILE, :] = sums[o]


def near_first_kernel(
    half, idx_ref, own_ref, emb_ref, dw_ref, time_hbm, noise_hbm, traj_hbm,
    emb_all, coef_ref, keep_ref, partial_ref, g_own, g_send,
    act_ref, time_ref, noise_ref, traj_ref, sems,
):
    _, rows, _, lon = noise_ref.shape
    t, _, _, h = place()
    time_c = pltpu.make_async_copy(time_hbm, time_ref, sems.at[0])
    noise_c = pltpu.make_async_copy(noise_hbm, noise_ref, sems.at[1])
    time_c.start()
    noise_c.start()
    index = jnp.full((8, time_ref.shape[0] // 2), idx_ref[0], F32)
    time_c.wait()
    cond, level = condition_of(index, time_ref[...])
    coef_ref[...] = 0.125 * level[:, :LANES]
    fill_embedding(emb_all, emb_ref[...], cond[0:1, :])
    near_body((own_ref,), (emb_all,), dw_ref, (act_ref,), keep_ref, partial_ref, half, lon)
    noise_c.wait()
    scale = 0.125 * jnp.sqrt(level_of(jnp.full((1, lon), idx_ref[0], F32)))

    def emit(upper, anchored):
        for r in range(rows):
            value = scale * noise_ref[:, r, 0, :]
            if anchored:
                value = value + traj_ref[:, r, 0, :]
            cols = slice((r % half) * lon, (r % half + 1) * lon)
            target = g_own if (r < half) == upper else g_send
            target[:, cols] = value

    @pl.when(t == 0)
    def _():
        root = pltpu.make_async_copy(traj_hbm, traj_ref, sems.at[2])
        root.start()
        root.wait()

    for upper in (True, False):
        for anchored in (True, False):

            @pl.when((h == (0 if upper else 1)) & ((t == 0) == anchored))
            def _():
                emit(upper, anchored)


def near_later_kernel(half, lon, own_ref, part_ref, emb_own, emb_part, dw_ref, keep_ref, partial_ref, act0, act1):
    near_body((own_ref, part_ref), (emb_own, emb_part), dw_ref, (act0, act1), keep_ref, partial_ref, half, lon)


def spread_out(main, extra):
    done = 0
    for i, unit in enumerate(main):
        unit()
        while done < len(extra) and done * len(main) < (i + 1) * len(extra):
            extra[done]()
            done += 1
    for unit in extra[done:]:
        unit()


def finish(first_sum, second_sum, known, sent_ref, even_ref, rest):
    _, _, y, _ = place()
    even_ref[...] = jnp.where(y == 0, first_sum, second_sum)
    total = first_sum + second_sum
    if known is not None:
        total = total - known.astype(F32)
    sent_ref[...] = total.astype(BF16)
    for total_ref in rest:
        total_ref[...] = total


def finish_kernel(inc_own, drift_part, g_part, sent_ref, even_ref, *rest):
    finish(inc_own[...], drift_part[...] + g_part[...], None, sent_ref, even_ref, rest)


def far_kernel(first, staged, sizes, *refs):
    half, lon, chunks, ff, _ = sizes
    width = chunks * LANES
    refs = list(refs)

    def take(n):
        got = refs[:n]
        del refs[:n]
        return got

    if first:
        inner_own, outer_own, part5, outer_part = take(4)
        emb_own, coef_own, keep_in, partial, emb_ref, time_hbm = take(6)
    else:
        inner, outer = take(2)
        emb_own, emb_part, coef_own, coef_part, keep_in, partial, sent_in = take(7)
    dw_ref, gain_ref, up_ref, down_ref, out_ref, g_own = take(6)
    if first:
        inc_own, drift_part, emb_part, coef_part = take(4)
    else:
        (g_part,) = take(1)
        sent_ref, even_ref = take(2)
        rest = take(1) if staged else []
    act0, act1, conv_ref, norm_ref, up_out, hid_ref, bo_ref = take(7)
    if first:
        time_ref, time_sem = take(2)

    _, _, _, h = place()
    acts = (act0, act1)
    inside = 5 * (1 - h)
    outside = 5 * h
    near = 2 * lon
    whole = (False, first)
    if first:
        time_c = pltpu.make_async_copy(time_hbm, time_ref, time_sem)
        time_c.start()

    def condition_unit():
        quarter = width // 2
        row = lambda k: part5[PAD - k : PAD - k + 1, :quarter].astype(F32)
        index = jnp.broadcast_to(row(2) * 32.0 + row(1), (8, quarter))
        cond, level = condition_of(index, time_ref[...])
        coef_part[...] = 0.125 * level[:, :LANES]
        fill_embedding(emb_part, emb_ref[...], cond[0:1, :])

    def embed_units(slot):
        emb_all = (emb_own, emb_part)[slot]
        if not first:
            pieces = (
                (inner, slice((1 - slot) * near, (2 - slot) * near), inside),
                (outer, slice(slot * near, (slot + 1) * near), outside),
            )
        elif slot == 0:
            pieces = ((inner_own, slice(0, near), inside), (outer_own, slice(0, near), outside))
        else:
            pieces = ((part5, slice(0, (half + 2) * lon), 2 * (1 - h)), (outer_part, slice(0, near), outside))
        units = []
        for ref, cols, base in pieces:
            held = []

            def unit(r, ref=ref, cols=cols, base=base, held=held):
                if not held:
                    held.append(ref[:, cols].T)
                store_row(acts[slot], base + r, embed_row(held[0], r, lon, emb_all[...]), lon)

            units += [functools.partial(unit, r) for r in range((cols.stop - cols.start) // lon)]
        return units

    part = lon // 2

    def conv_units(b):
        slot, p = b // 2, b % 2
        flip = b % 2
        rows = range(half + 4) if whole[slot] else (0, 1, half + 2, half + 3)

        def tile_unit(c, k):
            col = p * part + k * TILE
            sums = [None if whole[slot] else partial[slot, c, o, col : col + TILE, :] for o in range(half)]
            sums = conv_tile(acts[slot], dw_ref, c, col, TILE, half, rows, 0, sums)
            for o in range(half):
                conv_ref[flip, c, o, k * TILE : (k + 1) * TILE, :] = sums[o]

        def norm_unit(o, k):
            span = slice(k * 48, (k + 1) * 48)
            x = [conv_ref[flip, c, o, span, :] for c in range(chunks)]
            mean = jnp.sum(functools.reduce(jnp.add, x), axis=1, keepdims=True) * (1.0 / width)
            x = [v - mean for v in x]
            var = jnp.sum(functools.reduce(jnp.add, [v * v for v in x]), axis=1, keepdims=True) * (1.0 / width)
            inv = lax.rsqrt(var + 1e-06)
            for c, v in enumerate(x):
                lane = slice(c * LANES, (c + 1) * LANES)
                value = (v * inv * gain_ref[:, lane]).astype(BF16)
                norm_ref[flip, o * part + k * 48 : o * part + (k + 1) * 48, lane] = value

        return [functools.partial(tile_unit, c, k) for c in range(chunks) for k in range(part // TILE)] + [
            functools.partial(norm_unit, o, k) for o in range(half) for k in range(part // 48)
        ]

    k0 = math.sqrt(2.0 / math.pi)

    def mix_units(b):
        slot, p = b // 2, b % 2
        flip = b % 2

        def up_unit(n):
            up_out[n % 2] = jnp.dot(norm_ref[flip], up_ref[:, n * 256 : (n + 1) * 256], preferred_element_type=F32)

        def gelu_unit(n, o):
            u = up_out[n % 2, o * part : (o + 1) * part, :]
            value = (u + u * jnp.tanh(u * (k0 + (k0 * 0.044715) * (u * u)))).astype(BF16)
            hid_ref[flip, o * part : (o + 1) * part, n * 256 : (n + 1) * 256] = value

        def down_unit(m):
            d = jnp.dot(hid_ref[flip], down_ref[:, m * 256 : (m + 1) * 256], preferred_element_type=F32)
            lane = slice(m * 256, (m + 1) * 256)
            for o in range(half):
                span = slice(o * lon + p * part, o * lon + (p + 1) * part)
                if whole[slot]:
                    c = 2 * m
                    at = slice(LEAD + p * part, LEAD + (p + 1) * part)
                    a = jnp.concatenate([acts[slot][c, 2 + o, at, :], acts[slot][c + 1, 2 + o, at, :]], axis=1)
                else:
                    a = keep_in[slot, span, lane].astype(F32)
                bo_ref[slot, span, lane] = (a + 0.5 * d[o * part : (o + 1) * part, :]).astype(BF16)

        steps = ff // 256
        units = [functools.partial(up_unit, 0)]
        for n in range(steps):
            if n + 1 < steps:
                units.append(functools.partial(up_unit, n + 1))
            units += [functools.partial(gelu_unit, n, o) for o in range(half)]
        return units + [functools.partial(down_unit, m) for m in range(width // 256)]

    incs = []

    def out_unit(slot):
        drift = lax.dot_general(out_ref[...], bo_ref[slot], (((1,), (1,)), ((), ())), preferred_element_type=F32)
        drift = (coef_own, coef_part)[slot][0:1, 0:1] * drift
        if slot == 0:
            drift = drift + g_own[...]
        elif not first:
            drift = drift + g_part[...]
        if first:
            (inc_own, drift_part)[slot][...] = drift
        else:
            incs.append(drift)

    for unit in embed_units(0):
        unit()
    if first:
        spread_out(conv_units(0), [])
        time_c.wait()
        condition_unit()
        spread_out(conv_units(1), embed_units(1) + mix_units(0))
    else:
        spread_out(conv_units(0), embed_units(1))
        spread_out(conv_units(1), mix_units(0))
    spread_out(conv_units(2), mix_units(1))
    spread_out(conv_units(3), mix_units(2) + [functools.partial(out_unit, 0)])
    for unit in mix_units(3):
        unit()
    out_unit(1)
    if not first:
        finish(incs[0], incs[1], sent_in[...], sent_ref, even_ref, rest)


def cost(flops, nbytes=1 << 20):
    return pl.CostEstimate(flops=int(flops), bytes_accessed=nbytes, transcendentals=0)


def act_scratch(chunks, rows, lon):
    return pltpu.VMEM((chunks, rows, lon + 2 * LEAD, LANES), F32)


def far(first, staged, head, weights, half, lon):
    _, _, up, _, _, g_own = weights[:6]
    channels, points = g_own.shape
    width, ff = up.shape
    chunks = width // LANES
    block = points // 2
    grid = ((channels, points), F32)
    outs = [grid, grid] if first else [((channels, points), BF16), grid] + [grid] * staged
    specs = [VMEM] * (len(head) + len(weights))
    scratch = [act_scratch(chunks, half + 4, lon)] * 2 + [
        pltpu.VMEM((2, chunks, half, lon // 2, LANES), F32),
        pltpu.VMEM((2, block, width), BF16),
        pltpu.VMEM((2, block, 256), F32),
        pltpu.VMEM((2, block, ff), BF16),
        pltpu.VMEM((2, points, width), BF16),
    ]
    if first:
        outs += [((PAD, width), BF16), ((8, LANES), F32)]
        specs[len(head) - 1] = HBM
        scratch += [pltpu.VMEM(head[-1].shape, F32), pltpu.SemaphoreType.DMA]
    return call(
        functools.partial(far_kernel, first, staged, (half, lon, chunks, ff, channels)),
        outs,
        (*head, *weights),
        specs,
        scratch,
        cost(2 * 2 * points * width * (channels * 2 + 2 * ff + 25)),
    )


def middle_kernel(count, lon, *refs):
    gots, refs = refs[:count], refs[count:]
    even, own3, part5, sum_ref, own_ref, part_ref, inner_ref, outer_ref = refs
    channels, points = even.shape
    t, _, y, h = place()
    near = 2 * lon
    total = gots[0][...].astype(F32)
    for g in gots[1:]:
        total = total + g[...].astype(F32)
    sum_ref[...] = total
    odd = (total + even[...]).astype(BF16)
    flat = total.astype(BF16)
    for ref in (own_ref, part_ref, inner_ref, outer_ref):
        ref[channels:, :] = jnp.ones((PAD - channels, ref.shape[1]), BF16)

    def emit(parity, upper):
        shift = 0 if upper else near
        start = own3[:channels, :] if parity == 0 else part5[:channels, shift : shift + points]
        state = jnp.where(t < 2, start.astype(F32), flat.astype(F32)).astype(BF16)
        pair = (state, odd) if parity == 0 else (odd, state)
        own_ref[:channels, :] = pair[0]
        part_ref[:channels, :] = pair[1]
        for k, s in enumerate(pair):
            cols = slice(k * near, (k + 1) * near)
            low, high = s[:, :near], s[:, points - near :]
            inner_ref[:channels, cols] = high if upper else low
            outer_ref[:channels, cols] = low if upper else high

    for parity in range(2):
        for half_at in range(2):

            @pl.when((y == parity) & (h == half_at))
            def _():
                emit(parity, half_at == 0)


def ending_kernel(count, *refs):
    gots, (before, even, mine_ref, send_ref) = refs[:count], refs[count:]
    _, _, y, _ = place()
    total = before[...]
    for g in gots:
        total = total + g[...].astype(F32)
    odd = total + even[...]
    mine_ref[...] = jnp.where(y == 0, total, odd)
    send_ref[...] = jnp.where(y == 0, odd, total)


def output_kernel(mine, other, traj_hbm, out_ref, sem):
    _, rows, _, lon = out_ref.shape
    half = rows // 2
    t, _, _, h = place()

    def emit(upper):
        for r in range(rows):
            cols = slice((r % half) * lon, (r % half + 1) * lon)
            out_ref[:, r, 0, :] = (mine if (r < half) == upper else other)[:, cols]

    @pl.when((h == 0) & (t > 0))
    def _():
        emit(True)

    @pl.when((h == 1) & (t > 0))
    def _():
        emit(False)

    @pl.when(t == 0)
    def _():
        copy = pltpu.make_async_copy(traj_hbm, out_ref, sem)
        copy.start()
        copy.wait()


def call(body, outs, ins, specs=None, scratch=(), estimate=None):
    return pl.pallas_call(
        body,
        out_shape=tuple(jax.ShapeDtypeStruct(s, d) for s, d in outs),
        in_specs=specs or [VMEM] * len(ins),
        out_specs=tuple([VMEM] * len(outs)),
        scratch_shapes=list(scratch),
        compiler_params=LIMIT,
        cost_estimate=estimate,
    )(*ins)


def exchange(sent, total=None, *, groups, memory):
    gots, kept = [], []
    base, moved, unit = sent, None, 1
    while unit < groups:
        if unit > 1:
            rest = memory[len(kept)] if memory else 0.0
            sent = (total + moved + rest).astype(BF16)
            kept.append(base.astype(F32) + moved + rest - sent.astype(F32))
        for step in range(1, RADIX):
            shift = 2 * step * unit
            if shift < 2 * groups:
                gots.append(lax.ppermute(sent, "tm", [(i, i + shift) for i in range(2 * groups - shift)]))
        unit *= RADIX
        if groups > RADIX:
            moved = functools.reduce(jnp.add, [g.astype(F32) for g in gots])
    return gots, kept


def shards(
    traj, noise, step_index, embed_weight, time_weight, dw_weight, ln_gain, up_weight, down_weight, out_weight,
):
    times, bands = lax.axis_size("tm"), lax.axis_size("lat")
    groups = times // 2
    channels, rows, lon = traj.shape[1:]
    half = rows // 2
    width = embed_weight.shape[1]
    points, span, near = half * lon, (half + 2) * lon, 2 * lon
    axes = ("tm", "lat")

    def at(a, b):
        return a * bands + b

    cells = [(a, b, (a + b) % 2) for a in range(times) for b in range(bands)]
    swap = [(at(a, b), at(a ^ 1, b)) for a, b, _ in cells]
    side = [(at(a, b), at(a, b + (1 if c else -1))) for a, b, c in cells if 0 <= b + (1 if c else -1) < bands]
    cross = [(at(a, b), at(a ^ 1, b + (-1 if c else 1))) for a, b, c in cells if 0 <= b + (-1 if c else 1) < bands]

    root = traj.reshape(channels, rows, 1, lon)
    draws = noise.reshape(channels, rows, 1, lon)
    band = (channels, rows, 1, lon)
    chunks = width // LANES
    own3, inner_own, to_swap, to_side, to_cross = call(
        prep_kernel,
        [((PAD, points), BF16), ((PAD, near), BF16), ((PAD, span), BF16), ((PAD, near), BF16), ((PAD, near), BF16)],
        (step_index, root),
        [SMEM, HBM],
        [pltpu.VMEM(band, F32), pltpu.VMEM((PAD, rows * lon), BF16), pltpu.SemaphoreType.DMA],
        cost(1e9),
    )
    part5 = lax.ppermute(to_swap, axes, swap)
    outer_part = lax.ppermute(to_cross, axes, cross)
    outer_own = lax.ppermute(to_side, axes, side)
    dw = dw_weight.T
    work = 2 * points * width * (2 * channels + 25)

    def kept(slots):
        return [((slots, points, width), BF16), ((slots, chunks, half, lon, LANES), F32)]

    emb_own, coef_own, keep, partial, g_own, g_send = call(
        functools.partial(near_first_kernel, half),
        [((PAD, width), BF16), ((8, LANES), F32)] + kept(1) + [((channels, points), F32)] * 2,
        (step_index, own3, embed_weight, dw, time_weight, draws, root),
        [SMEM, VMEM, VMEM, VMEM, HBM, HBM, HBM],
        [
            act_scratch(chunks, half, lon),
            pltpu.VMEM(time_weight.shape, F32),
            pltpu.VMEM(band, F32),
            pltpu.VMEM(band, F32),
            pltpu.SemaphoreType.DMA((3,)),
        ],
        cost(20 * work),
    )
    g_part = lax.ppermute(g_send, axes, swap)
    weights = (dw, ln_gain.reshape(1, width), up_weight, down_weight, out_weight.T, g_own)
    staged = groups > RADIX
    inc_own, drift_part, emb_part, coef_part = far(
        True,
        staged,
        (inner_own, outer_own, part5, outer_part, emb_own, coef_own, keep, partial, embed_weight, time_weight),
        weights,
        half,
        lon,
    )
    sums = [((channels, points), BF16)] + [((channels, points), F32)] * (1 + staged)
    sent, even, *total = call(finish_kernel, sums, (inc_own, drift_part, g_part))
    gots, memory = exchange(sent, *total, groups=groups, memory=None)
    before = None
    for _ in range(1, ITERS):
        before, s_own, s_part, inner, outer = call(
            functools.partial(middle_kernel, len(gots), lon),
            [((channels, points), F32)] + [((PAD, points), BF16)] * 2 + [((PAD, 2 * near), BF16)] * 2,
            (*gots, even, own3, part5),
        )
        inner = lax.ppermute(inner, axes, swap)
        outer = lax.ppermute(outer, axes, side)
        keep, partial = call(
            functools.partial(near_later_kernel, half, lon),
            kept(2),
            (s_own, s_part, emb_own, emb_part, dw),
            scratch=[act_scratch(chunks, half, lon)] * 2,
            estimate=cost(20 * work),
        )
        sent, even, *total = far(
            False,
            staged,
            (inner, outer, emb_own, emb_part, coef_own, coef_part, keep, partial, sent),
            weights + (g_part,),
            half,
            lon,
        )
        gots, memory = exchange(sent, *total, groups=groups, memory=memory)
    mine, send = call(
        functools.partial(ending_kernel, len(gots)), [((channels, points), F32)] * 2, (*gots, before, even)
    )
    other = lax.ppermute(send, axes, swap)
    (result,) = call(output_kernel, [(band, F32)], (mine, other, root), [VMEM, VMEM, HBM], [pltpu.SemaphoreType.DMA])
    return result.reshape(1, channels, rows, lon)


def solution(mesh):
    in_specs = (P("tm", None, "lat", None), P("tm", None, "lat", None), P("tm")) + (P(),) * 7
    out_specs = P("tm", None, "lat", None)

    return jax.shard_map(shards, mesh=mesh, in_specs=in_specs, out_specs=out_specs, check_vma=False)
```

time: 87.7 us -> 76.2 us (0.87)
  waiting for transfers between devices: 35.7 us -> 27.9 us
  local copies, waits for them, and re-layouts: 5.06 us -> 1.08 us
  starting transfers between devices: 20.3 us -> 21.4 us
    pallas_call x2 -> x0, Pallas kernels: 21.9 us -> none  [denoise(): pl.pallas_call(functools.partial(denoise_kernel, first, (half, lon, chunk...]
    pallas_call x5 -> x9, Pallas kernels: 3.21 us -> 24.4 us  [call(): pl.pallas_call(body, out_shape=tuple((jax.ShapeDtypeStruct(s, d) for s, d...]
    ppermute x1, waiting for transfers between devices: 4.12 us -> 0.01 us  [shards(): outer_part = lax.ppermute(to_cross, axes, cross)]
    unnamed x24 -> x20, local copies, waits for them, and re-layouts: 5.06 us -> 1.08 us
    ppermute x1, waiting for transfers between devices: 3.16 us -> 0.01 us  [shards(): inner = lax.ppermute(inner, axes, swap)]
    ppermute x1, waiting for transfers between devices: 0.01 us -> 1.99 us  [shards(): part5 = lax.ppermute(to_swap, axes, swap)]
    ppermute x6, waiting for transfers between devices: 20.9 us -> 19.6 us  [exchange(): lax.ppermute(sent, 'tm', [(i, i + shift) for i in range(2 * groups - shif...]
    ppermute x1, starting transfers between devices: 0.1 us -> 1.29 us  [shards(): other = lax.ppermute(send, axes, swap)]
  transfers between devices with their start and end apart: 13 -> 13, of which waited for: 7 -> 6; matrix products, arithmetic and copies ran while one was open for 0% -> 0% of each run, Pallas kernels for 0% -> 20%
where the time goes in v4:
time: 76.2 us; the launch traced here: 75.8 us
  waiting for transfers between devices  27.9 us (37%)
  Pallas kernels  24.4 us (32%)
  starting transfers between devices  21.4 us (28%)
  between operations  1.11 us (1%)
  local copies, waits for them, and re-layouts  1.08 us (1%)
    pallas_call x9, Pallas kernels, call(): pl.pallas_call(body, out_shape=tuple((jax.ShapeDtypeStruct(s, d) for s, d...  24.4 us
    ppermute x6, waiting for transfers between devices, exchange(): lax.ppermute(sent, 'tm', [(i, i + shift) for i in range(2 * groups - shif...  19.6 us
    ppermute x6, starting transfers between devices, exchange(): lax.ppermute(sent, 'tm', [(i, i + shift) for i in range(2 * groups - shif...  9.95 us
    ppermute x1, waiting for transfers between devices, shards(): other = lax.ppermute(send, axes, swap)  6.31 us
    ppermute x1, starting transfers between devices, shards(): outer_part = lax.ppermute(to_cross, axes, cross)  4.77 us
    ppermute x1, starting transfers between devices, shards(): g_part = lax.ppermute(g_send, axes, swap)  2.05 us
    ppermute x1, waiting for transfers between devices, shards(): part5 = lax.ppermute(to_swap, axes, swap)  1.99 us
    ppermute x1, starting transfers between devices, shards(): inner = lax.ppermute(inner, axes, swap)  1.75 us
  transfers between devices with their start and end apart: 13, of which 6 were waited for; matrix products, arithmetic and copies ran while one was open for 0% of the time, Pallas kernels for 20%

profile of v4, /device:TPU:16, one launch (start us, length us, event | category | flops | bytes accessed | tf_op | source)
XLA Modules:
  0.0 75.8 jit_solution(6350434729698454434)
XLA Ops:
  0.7 0.0 copy-start
  0.7 1.0 %copy-done = f32[1,83,6,192]{3,0,2,1:T(1,128)S(1)} copy-done((f32[1,83,6,192]{3,0,2,1:T(1,128)S(1)}, f32[1,83,6,192]{3,0,2,1:T(1,128)}, u32[]{:S(2)}) %copy-start) | copy-done | bytes 382488
  1.7 1.1 %shard_map.100 = (bf16[88,576]{1,0:T(8,128)(2,1)S(1)}, bf16[88,384]{1,0:T(8,128)(2,1)S(1)}, bf16[88,960]{1,0:T(8,128)(2,1)S(1)}, bf16[88,384]{1,0:T(8,128)(2,1)S(1)}, bf16[88,384]{1,0:T(8,128)(2,1)S(1)}) custom-call(s32[1]{0:T(128)S(6)} %copy.11.idx_ref, f32[83,6,1,192]{3,2,1,0:T(1,128)S(1)} %bitcast.6), custom_call_target="tpu_custom_call" | custom-call | flops 1000000000 | bytes 1048576 | tf_op jit(solution)/shard_map/pallas_call | solution.py:488
  2.8 0.7 collective-permute-start
  3.5 4.8 %collective-permute-start.2 = (bf16[88,384]{1,0:T(8,128)(2,1)S(1)}, bf16[88,384]{1,0:T(8,128)(2,1)S(1)}, u32[]{:S(2)}, u32[]{:S(2)}) collective-permute-start(bf16[88,384]{1,0:T(8,128)(2,1)S(1)} %get-tuple-element.36), channel_id=1, source_target_pairs={{0,5},{1,4},{2,7},{3,6},{5,2},{6,1},{8,13},{9,12},{10,15},{11,14},... | collective-permute-start | bytes 202760 | tf_op jit(solution)/shard_map/ppermute | solution.py:549
  8.3 0.1 collective-permute-start.1
  8.4 0.0 copy-start.7
  8.4 0.0 copy-start.9
  8.4 3.2 %shard_map.101 = (bf16[88,512]{1,0:T(8,128)(2,1)S(1)}, f32[8,128]{1,0:T(8,128)S(1)}, bf16[1,576,512]{2,1,0:T(8,128)(2,1)S(1)}, f32[1,4,3,192,128]{4,3,2,1,0:T(8,...) custom-call(s32[1]{0:T(128)S(6)} %copy.11.idx_ref, bf16[88,576]{1,0:T(8,128)(2,1)S(1)} %get-tuple-element.37.own_ref.refs_4_, ...), custom_call_target="tpu_custom_call" | custom-call | flops 2253127680 | bytes 1048576 | tf_op jit(solution)/shard_map/pallas_call | solution.py:488
  11.6 2.0 %collective-permute-start.3 = (f32[83,576]{1,0:T(8,128)S(1)}, f32[83,576]{1,0:T(8,128)S(1)}, u32[]{:S(2)}, u32[]{:S(2)}) collective-permute-start(f32[83,576]{1,0:T(8,128)S(1)} %get-tuple-element.45), channel_id=1, source_target_pairs={{0,4},{1,5},{2,6},{3,7},{4,0},{5,1},{6,2},{7,3},{8,12},{9,13},{10,... | collective-permute-start | bytes 573704 | tf_op jit(solution)/shard_map/ppermute | solution.py:571
  13.7 2.0 %collective-permute-done.1.refs_2_.refs_5_ = bf16[88,960]{1,0:T(8,128)(2,1)S(1)} collective-permute-done((bf16[88,960]{1,0:T(8,128)(2,1)S(1)}, bf16[88,960]{1,0:T(8,128)(2,1)S(1)}, u32[]{:S(2)}, u32[]{:S(2)}) %collective-permute-start.1) | collective-permute-done | bytes 168992 | tf_op jit(solution)/shard_map/ppermute | solution.py:548
  15.7 8.8 %shard_map.102 = (f32[83,576]{1,0:T(8,128)S(1)}, f32[83,576]{1,0:T(8,128)S(1)}, bf16[88,512]{1,0:T(8,128)(2,1)S(1)}, f32[8,128]{1,0:T(8,128)S(1)}) custom-call(bf16[88,384]{1,0:T(8,128)(2,1)S(1)} %get-tuple-element.33.refs_0_, bf16[88,384]{1,0:T(8,128)(2,1)S(1)} %collective-permute-done.refs_1_, bf16[88,960]{1,0:T(8,128)(2,1)S(1)} %collective-permute-done.1.refs_2_.refs_5_, ...), custom_call_target="tpu_custom_call" | custom-call | flops 2641231872 | bytes 1048576 | tf_op jit(solution)/shard_map/pallas_call | solution.py:488
  24.5 0.1 shard_map.103
  24.6 0.7 collective-permute-start.6
  25.3 1.3 %collective-permute-start.5 = (bf16[83,576]{1,0:T(8,128)(2,1)S(1)}, bf16[83,576]{1,0:T(8,128)(2,1)S(1)}, u32[]{:S(2)}, u32[]{:S(2)}) collective-permute-start(bf16[83,576]{1,0:T(8,128)(2,1)S(1)} %get-tuple-element.46.refs_8_), channel_id=1, source_target_pairs={{0,16},{4,20},{8,24},{12,28},{1,17},{5,21},{9,25},{13,29},{2,18},{... | collective-permute-start | bytes 286856 | tf_op jit(solution)/shard_map/ppermute | solution.py:510
  26.6 4.1 %collective-permute-start.4 = (bf16[83,576]{1,0:T(8,128)(2,1)S(1)}, bf16[83,576]{1,0:T(8,128)(2,1)S(1)}, u32[]{:S(2)}, u32[]{:S(2)}) collective-permute-start(bf16[83,576]{1,0:T(8,128)(2,1)S(1)} %get-tuple-element.46.refs_8_), channel_id=1, source_target_pairs={{0,8},{4,12},{8,16},{12,20},{16,24},{20,28},{1,9},{5,13},{9,17},{1... | collective-permute-start | bytes 286856 | tf_op jit(solution)/shard_map/ppermute | solution.py:510
  30.7 5.5 %collective-permute-done.5.refs_1_ = bf16[83,576]{1,0:T(8,128)(2,1)S(1)} collective-permute-done((bf16[83,576]{1,0:T(8,128)(2,1)S(1)}, bf16[83,576]{1,0:T(8,128)(2,1)S(1)}, u32[]{:S(2)}, u32[]{:S(2)}) %collective-permute-start.5) | collective-permute-done | bytes 95648 | tf_op jit(solution)/shard_map/ppermute | solution.py:510
  36.1 3.5 %collective-permute-done.4.refs_0_ = bf16[83,576]{1,0:T(8,128)(2,1)S(1)} collective-permute-done((bf16[83,576]{1,0:T(8,128)(2,1)S(1)}, bf16[83,576]{1,0:T(8,128)(2,1)S(1)}, u32[]{:S(2)}, u32[]{:S(2)}) %collective-permute-start.4) | collective-permute-done | bytes 95648 | tf_op jit(solution)/shard_map/ppermute | solution.py:510
  39.7 0.2 shard_map.104
  39.9 1.7 %collective-permute-start.7 = (bf16[88,768]{1,0:T(8,128)(2,1)S(1)}, bf16[88,768]{1,0:T(8,128)(2,1)S(1)}, u32[]{:S(2)}, u32[]{:S(2)}) collective-permute-start(bf16[88,768]{1,0:T(8,128)(2,1)S(1)} %get-tuple-element.48), channel_id=1, source_target_pairs={{0,4},{1,5},{2,6},{3,7},{4,0},{5,1},{6,2},{7,3},{8,12},{9,13},{10,... | collective-permute-start | bytes 405512 | tf_op jit(solution)/shard_map/ppermute | solution.py:592
  41.6 0.9 %collective-permute-start.8 = (bf16[88,768]{1,0:T(8,128)(2,1)S(1)}, bf16[88,768]{1,0:T(8,128)(2,1)S(1)}, u32[]{:S(2)}, u32[]{:S(2)}) collective-permute-start(bf16[88,768]{1,0:T(8,128)(2,1)S(1)} %get-tuple-element.49), channel_id=1, source_target_pairs={{1,2},{2,1},{4,5},{5,4},{6,7},{7,6},{9,10},{10,9},{12,13},{13,12},... | collective-permute-start | bytes 405512 | tf_op jit(solution)/shard_map/ppermute | solution.py:593
  42.5 3.3 %shard_map.105 = (bf16[2,576,512]{2,1,0:T(8,128)(2,1)S(1)}, f32[2,4,3,192,128]{4,3,2,1,0:T(8,128)S(1)}) custom-call(bf16[88,576]{1,0:T(8,128)(2,1)S(1)} %get-tuple-element.52.own_ref, bf16[88,576]{1,0:T(8,128)(2,1)S(1)} %get-tuple-element.53.part_ref, bf16[88,512]{1,0:T(8,128)(2,1)S(1)} %get-tuple-element.38.refs_4_.emb_own.refs_2_, ...), custom_call_target="tpu_custom_call" | custom-call | flops 2253127680 | bytes 1048576 | tf_op jit(solution)/shard_map/pallas_call | solution.py:488
  45.8 6.5 %shard_map.106 = (bf16[83,576]{1,0:T(8,128)(2,1)S(1)}, f32[83,576]{1,0:T(8,128)S(1)}) custom-call(bf16[88,768]{1,0:T(8,128)(2,1)S(1)} %collective-permute-done.7.refs_0_, bf16[88,768]{1,0:T(8,128)(2,1)S(1)} %collective-permute-done.8.refs_1_, bf16[88,512]{1,0:T(8,128)(2,1)S(1)} %get-tuple-element.38.refs_4_.emb_own.refs_2_, ...), custom_call_target="tpu_custom_call" | custom-call | flops 2641231872 | bytes 1048576 | tf_op jit(solution)/shard_map/pallas_call | solution.py:488
  52.4 0.7 collective-permute-start.11
  53.1 1.3 %collective-permute-start.10 = (bf16[83,576]{1,0:T(8,128)(2,1)S(1)}, bf16[83,576]{1,0:T(8,128)(2,1)S(1)}, u32[]{:S(2)}, u32[]{:S(2)}) collective-permute-start(bf16[83,576]{1,0:T(8,128)(2,1)S(1)} %get-tuple-element.56), channel_id=1, source_target_pairs={{0,16},{4,20},{8,24},{12,28},{1,17},{5,21},{9,25},{13,29},{2,18},{... | collective-permute-start | bytes 286856 | tf_op jit(solution)/shard_map/ppermute | solution.py:510
  54.4 1.9 %collective-permute-start.9 = (bf16[83,576]{1,0:T(8,128)(2,1)S(1)}, bf16[83,576]{1,0:T(8,128)(2,1)S(1)}, u32[]{:S(2)}, u32[]{:S(2)}) collective-permute-start(bf16[83,576]{1,0:T(8,128)(2,1)S(1)} %get-tuple-element.56), channel_id=1, source_target_pairs={{0,8},{4,12},{8,16},{12,20},{16,24},{20,28},{1,9},{5,13},{9,17},{1... | collective-permute-start | bytes 286856 | tf_op jit(solution)/shard_map/ppermute | solution.py:510
  56.3 5.2 %collective-permute-done.10.refs_1_ = bf16[83,576]{1,0:T(8,128)(2,1)S(1)} collective-permute-done((bf16[83,576]{1,0:T(8,128)(2,1)S(1)}, bf16[83,576]{1,0:T(8,128)(2,1)S(1)}, u32[]{:S(2)}, u32[]{:S(2)}) %collective-permute-start.10) | collective-permute-done | bytes 95648 | tf_op jit(solution)/shard_map/ppermute | solution.py:510
  61.5 5.4 %collective-permute-done.9.refs_0_ = bf16[83,576]{1,0:T(8,128)(2,1)S(1)} collective-permute-done((bf16[83,576]{1,0:T(8,128)(2,1)S(1)}, bf16[83,576]{1,0:T(8,128)(2,1)S(1)}, u32[]{:S(2)}, u32[]{:S(2)}) %collective-permute-start.9) | collective-permute-done | bytes 95648 | tf_op jit(solution)/shard_map/ppermute | solution.py:510
  66.9 0.1 shard_map.107
  67.0 1.3 %collective-permute-start.12 = (f32[83,576]{1,0:T(8,128)S(1)}, f32[83,576]{1,0:T(8,128)S(1)}, u32[]{:S(2)}, u32[]{:S(2)}) collective-permute-start(f32[83,576]{1,0:T(8,128)S(1)} %get-tuple-element.60), channel_id=1, source_target_pairs={{0,4},{1,5},{2,6},{3,7},{4,0},{5,1},{6,2},{7,3},{8,12},{9,13},{10,... | collective-permute-start | bytes 573704 | tf_op jit(solution)/shard_map/ppermute | solution.py:613
  68.3 6.3 %collective-permute-done.12.other = f32[83,576]{1,0:T(8,128)S(1)} collective-permute-done((f32[83,576]{1,0:T(8,128)S(1)}, f32[83,576]{1,0:T(8,128)S(1)}, u32[]{:S(2)}, u32[]{:S(2)}) %collective-permute-start.12) | collective-permute-done | bytes 191264 | tf_op jit(solution)/shard_map/ppermute | solution.py:613
  74.6 1.1 %shard_map.108 = f32[83,6,1,192]{3,2,1,0:T(1,128)} custom-call(f32[83,576]{1,0:T(8,128)S(1)} %get-tuple-element.59.mine, f32[83,576]{1,0:T(8,128)S(1)} %collective-permute-done.12.other, f32[83,6,1,192]{3,2,1,0:T(1,128)S(1)} %bitcast.8), custom_call_target="tpu_custom_call" | custom-call | tf_op jit(solution)/shard_map/pallas_call | solution.py:488
  (23 shorter events, 0.1 us)
Async XLA Ops:
  0.7 1.0 %copy-start = (f32[1,83,6,192]{3,0,2,1:T(1,128)S(1)}, f32[1,83,6,192]{3,0,2,1:T(1,128)}, u32[]{:S(2)}) copy-start(f32[1,83,6,192]{3,0,2,1:T(1,128)} %param.10) | copy-start | bytes 1147396
  1.7 6.6 %copy-start.2 = (f32[512,512]{1,0:T(8,128)S(1)}, f32[512,512]{1,0:T(8,128)}, u32[]{:S(2)}) copy-start(f32[512,512]{1,0:T(8,128)} %refs_9_.1) | copy-start | bytes 3145732
  1.7 6.7 %copy-start.5 = (f32[1,83,6,192]{3,0,2,1:T(1,128)S(1)}, f32[1,83,6,192]{3,0,2,1:T(1,128)}, u32[]{:S(2)}) copy-start(f32[1,83,6,192]{3,0,2,1:T(1,128)} %param.11) | copy-start | bytes 1147396
  1.7 6.7 %copy-start.6 = (bf16[83,512]{1,0:T(8,128)(2,1)S(1)}, bf16[83,512]{1,0:T(8,128)(2,1)}, u32[]{:S(2)}) copy-start(bf16[83,512]{1,0:T(8,128)(2,1)} %refs_8_.1) | copy-start | bytes 254980
  1.7 6.7 %copy-start.8 = (f32[512,25]{0,1:T(8,128)S(1)}, f32[512,25]{0,1:T(8,128)}, u32[]{:S(2)}) copy-start(f32[512,25]{0,1:T(8,128)} %param.15) | copy-start | bytes 153604
  2.8 10.8 %collective-permute-start = (bf16[88,384]{1,0:T(8,128)(2,1)S(1)}, bf16[88,384]{1,0:T(8,128)(2,1)S(1)}, u32[]{:S(2)}, u32[]{:S(2)}) collective-permute-start(bf16[88,384]{1,0:T(8,128)(2,1)S(1)} %get-tuple-element.34), channel_id=1, source_target_pairs={{1,2},{2,1},{4,5},{5,4},{6,7},{7,6},{9,10},{10,9},{12,13},{13,12},... | collective-permute-start | bytes 202760 | tf_op jit(solution)/shard_map/ppermute | solution.py:550
  3.5 10.2 %collective-permute-start.2 = (bf16[88,384]{1,0:T(8,128)(2,1)S(1)}, bf16[88,384]{1,0:T(8,128)(2,1)S(1)}, u32[]{:S(2)}, u32[]{:S(2)}) collective-permute-start(bf16[88,384]{1,0:T(8,128)(2,1)S(1)} %get-tuple-element.36), channel_id=1, source_target_pairs={{0,5},{1,4},{2,7},{3,6},{5,2},{6,1},{8,13},{9,12},{10,15},{11,14},... | collective-permute-start | bytes 202760 | tf_op jit(solution)/shard_map/ppermute | solution.py:549
  8.3 7.4 %collective-permute-start.1 = (bf16[88,960]{1,0:T(8,128)(2,1)S(1)}, bf16[88,960]{1,0:T(8,128)(2,1)S(1)}, u32[]{:S(2)}, u32[]{:S(2)}) collective-permute-start(bf16[88,960]{1,0:T(8,128)(2,1)S(1)} %get-tuple-element.35), channel_id=1, source_target_pairs={{0,4},{1,5},{2,6},{3,7},{4,0},{5,1},{6,2},{7,3},{8,12},{9,13},{10,... | collective-permute-start | bytes 506888 | tf_op jit(solution)/shard_map/ppermute | solution.py:548
  8.4 7.3 %copy-start.3 = (bf16[512,1024]{1,0:T(8,128)(2,1)S(1)}, bf16[512,1024]{1,0:T(8,128)(2,1)}, u32[]{:S(2)}) copy-start(bf16[512,1024]{1,0:T(8,128)(2,1)} %refs_11_.1) | copy-start | bytes 3145732
  8.4 7.3 %copy-start.4 = (bf16[1024,512]{1,0:T(8,128)(2,1)S(1)}, bf16[1024,512]{1,0:T(8,128)(2,1)}, u32[]{:S(2)}) copy-start(bf16[1024,512]{1,0:T(8,128)(2,1)} %refs_12_.3) | copy-start | bytes 3145732
  8.4 7.2 %copy-start.7 = (bf16[512,83]{0,1:T(8,128)(2,1)S(1)}, bf16[512,83]{0,1:T(8,128)(2,1)}, u32[]{:S(2)}) copy-start(bf16[512,83]{0,1:T(8,128)(2,1)} %param.19) | copy-start | bytes 254980
  8.4 7.2 %copy-start.9 = (f32[512]{0:T(512)S(1)}, f32[512]{0:T(512)}, u32[]{:S(2)}) copy-start(f32[512]{0:T(512)} %param.16) | copy-start | bytes 6148
  11.6 12.9 %collective-permute-start.3 = (f32[83,576]{1,0:T(8,128)S(1)}, f32[83,576]{1,0:T(8,128)S(1)}, u32[]{:S(2)}, u32[]{:S(2)}) collective-permute-start(f32[83,576]{1,0:T(8,128)S(1)} %get-tuple-element.45), channel_id=1, source_target_pairs={{0,4},{1,5},{2,6},{3,7},{4,0},{5,1},{6,2},{7,3},{8,12},{9,13},{10,... | collective-permute-start | bytes 573704 | tf_op jit(solution)/shard_map/ppermute | solution.py:571
  24.6 6.1 %collective-permute-start.6 = (bf16[83,576]{1,0:T(8,128)(2,1)S(1)}, bf16[83,576]{1,0:T(8,128)(2,1)S(1)}, u32[]{:S(2)}, u32[]{:S(2)}) collective-permute-start(bf16[83,576]{1,0:T(8,128)(2,1)S(1)} %get-tuple-element.46.refs_8_), channel_id=1, source_target_pairs={{0,24},{4,28},{1,25},{5,29},{2,26},{6,30},{3,27},{7,31}} | collective-permute-start | bytes 286856 | tf_op jit(solution)/shard_map/ppermute | solution.py:510
  25.3 10.9 %collective-permute-start.5 = (bf16[83,576]{1,0:T(8,128)(2,1)S(1)}, bf16[83,576]{1,0:T(8,128)(2,1)S(1)}, u32[]{:S(2)}, u32[]{:S(2)}) collective-permute-start(bf16[83,576]{1,0:T(8,128)(2,1)S(1)} %get-tuple-element.46.refs_8_), channel_id=1, source_target_pairs={{0,16},{4,20},{8,24},{12,28},{1,17},{5,21},{9,25},{13,29},{2,18},{... | collective-permute-start | bytes 286856 | tf_op jit(solution)/shard_map/ppermute | solution.py:510
  26.6 13.1 %collective-permute-start.4 = (bf16[83,576]{1,0:T(8,128)(2,1)S(1)}, bf16[83,576]{1,0:T(8,128)(2,1)S(1)}, u32[]{:S(2)}, u32[]{:S(2)}) collective-permute-start(bf16[83,576]{1,0:T(8,128)(2,1)S(1)} %get-tuple-element.46.refs_8_), channel_id=1, source_target_pairs={{0,8},{4,12},{8,16},{12,20},{16,24},{20,28},{1,9},{5,13},{9,17},{1... | collective-permute-start | bytes 286856 | tf_op jit(solution)/shard_map/ppermute | solution.py:510
  39.9 5.9 %collective-permute-start.7 = (bf16[88,768]{1,0:T(8,128)(2,1)S(1)}, bf16[88,768]{1,0:T(8,128)(2,1)S(1)}, u32[]{:S(2)}, u32[]{:S(2)}) collective-permute-start(bf16[88,768]{1,0:T(8,128)(2,1)S(1)} %get-tuple-element.48), channel_id=1, source_target_pairs={{0,4},{1,5},{2,6},{3,7},{4,0},{5,1},{6,2},{7,3},{8,12},{9,13},{10,... | collective-permute-start | bytes 405512 | tf_op jit(solution)/shard_map/ppermute | solution.py:592
  41.6 4.2 %collective-permute-start.8 = (bf16[88,768]{1,0:T(8,128)(2,1)S(1)}, bf16[88,768]{1,0:T(8,128)(2,1)S(1)}, u32[]{:S(2)}, u32[]{:S(2)}) collective-permute-start(bf16[88,768]{1,0:T(8,128)(2,1)S(1)} %get-tuple-element.49), channel_id=1, source_target_pairs={{1,2},{2,1},{4,5},{5,4},{6,7},{7,6},{9,10},{10,9},{12,13},{13,12},... | collective-permute-start | bytes 405512 | tf_op jit(solution)/shard_map/ppermute | solution.py:593
  45.8 28.8 %copy-start.1 = (f32[1,83,6,192]{3,0,2,1:T(1,128)S(1)}, f32[1,83,6,192]{3,0,2,1:T(1,128)}, u32[]{:S(2)}) copy-start(f32[1,83,6,192]{3,0,2,1:T(1,128)} %param.10) | copy-start | bytes 1147396
  52.4 3.9 %collective-permute-start.11 = (bf16[83,576]{1,0:T(8,128)(2,1)S(1)}, bf16[83,576]{1,0:T(8,128)(2,1)S(1)}, u32[]{:S(2)}, u32[]{:S(2)}) collective-permute-start(bf16[83,576]{1,0:T(8,128)(2,1)S(1)} %get-tuple-element.56), channel_id=1, source_target_pairs={{0,24},{4,28},{1,25},{5,29},{2,26},{6,30},{3,27},{7,31}} | collective-permute-start | bytes 286856 | tf_op jit(solution)/shard_map/ppermute | solution.py:510
  53.1 8.4 %collective-permute-start.10 = (bf16[83,576]{1,0:T(8,128)(2,1)S(1)}, bf16[83,576]{1,0:T(8,128)(2,1)S(1)}, u32[]{:S(2)}, u32[]{:S(2)}) collective-permute-start(bf16[83,576]{1,0:T(8,128)(2,1)S(1)} %get-tuple-element.56), channel_id=1, source_target_pairs={{0,16},{4,20},{8,24},{12,28},{1,17},{5,21},{9,25},{13,29},{2,18},{... | collective-permute-start | bytes 286856 | tf_op jit(solution)/shard_map/ppermute | solution.py:510
  54.4 12.5 %collective-permute-start.9 = (bf16[83,576]{1,0:T(8,128)(2,1)S(1)}, bf16[83,576]{1,0:T(8,128)(2,1)S(1)}, u32[]{:S(2)}, u32[]{:S(2)}) collective-permute-start(bf16[83,576]{1,0:T(8,128)(2,1)S(1)} %get-tuple-element.56), channel_id=1, source_target_pairs={{0,8},{4,12},{8,16},{12,20},{16,24},{20,28},{1,9},{5,13},{9,17},{1... | collective-permute-start | bytes 286856 | tf_op jit(solution)/shard_map/ppermute | solution.py:510
  67.0 7.6 %collective-permute-start.12 = (f32[83,576]{1,0:T(8,128)S(1)}, f32[83,576]{1,0:T(8,128)S(1)}, u32[]{:S(2)}, u32[]{:S(2)}) collective-permute-start(f32[83,576]{1,0:T(8,128)S(1)} %get-tuple-element.60), channel_id=1, source_target_pairs={{0,4},{1,5},{2,6},{3,7},{4,0},{5,1},{6,2},{7,3},{8,12},{9,13},{10,... | collective-permute-start | bytes 573704 | tf_op jit(solution)/shard_map/ppermute | solution.py:613

commit v5 on v4

--- a/solution.py
+++ b/solution.py
@@ -34,7 +34,7 @@
     return 2.0 * jnp.exp(index * (math.log(0.1) / (LEVELS - 1)))
 
 
-def prep_kernel(idx_ref, traj_hbm, own_ref, inner_ref, swap_ref, side_ref, cross_ref, traj_ref, v_ref, sem):
+def prep_kernel(idx_ref, traj_hbm, own_ref, inner_ref, swap_ref, side_ref, traj_ref, v_ref, sem):
     channels, rows, _, lon = traj_ref.shape
     half = rows // 2
     _, _, _, h = place()
@@ -53,7 +53,6 @@
         inner_ref[...] = v_ref[:, half * lon : span] if upper else v_ref[:, lon : half * lon]
         swap_ref[...] = high if upper else low
         side_ref[...] = first if upper else last
-        cross_ref[...] = last if upper else first
 
     @pl.when(h == 0)
     def _():
@@ -193,15 +192,35 @@
         unit()
 
 
+def pack(ref, value):
+    channels, points = value.shape
+    for k in range(PAD // 8):
+        piece = value[8 * k : min(8 * k + 8, channels), :]
+        ref[: piece.shape[0], k * points : (k + 1) * points] = piece.astype(ref.dtype)
+
+
+def unpack(ref, channels, points, start=0, count=None):
+    count = points if count is None else count
+    pieces = []
+    for k in range(PAD // 8):
+        at = k * points + start
+        pieces.append(ref[: min(8, channels - 8 * k), at : at + count].astype(F32))
+    return jnp.concatenate(pieces, axis=0)
+
+
+def packed(points, dtype):
+    return ((8, PAD // 8 * points), dtype)
+
+
 def finish(first_sum, second_sum, known, sent_ref, even_ref, rest):
     _, _, y, _ = place()
     even_ref[...] = jnp.where(y == 0, first_sum, second_sum)
     total = first_sum + second_sum
     if known is not None:
-        total = total - known.astype(F32)
-    sent_ref[...] = total.astype(BF16)
+        total = total - unpack(known, *total.shape)
+    pack(sent_ref, total)
     for total_ref in rest:
-        total_ref[...] = total
+        pack(total_ref, total)
 
 
 def finish_kernel(inc_own, drift_part, g_part, sent_ref, even_ref, *rest):
@@ -219,7 +238,7 @@
         return got
 
     if first:
-        inner_own, outer_own, part5, outer_part = take(4)
+        inner_own, part5, outer = take(3)
         emb_own, coef_own, keep_in, partial, emb_ref, time_hbm = take(6)
     else:
         inner, outer = take(2)
@@ -261,9 +280,9 @@
                 (outer, slice(slot * near, (slot + 1) * near), outside),
             )
         elif slot == 0:
-            pieces = ((inner_own, slice(0, near), inside), (outer_own, slice(0, near), outside))
+            pieces = ((inner_own, slice(0, near), inside), (outer, slice(0, near), outside))
         else:
-            pieces = ((part5, slice(0, (half + 2) * lon), 2 * (1 - h)), (outer_part, slice(0, near), outside))
+            pieces = ((part5, slice(0, (half + 2) * lon), 2 * (1 - h)), (outer, slice(near, 2 * near), outside))
         units = []
         for ref, cols, base in pieces:
             held = []
@@ -371,7 +390,7 @@
         unit()
     out_unit(1)
     if not first:
-        finish(incs[0], incs[1], sent_in[...], sent_ref, even_ref, rest)
+        finish(incs[0], incs[1], sent_in, sent_ref, even_ref, rest)
 
 
 def cost(flops, nbytes=1 << 20):
@@ -389,7 +408,7 @@
     chunks = width // LANES
     block = points // 2
     grid = ((channels, points), F32)
-    outs = [grid, grid] if first else [((channels, points), BF16), grid] + [grid] * staged
+    outs = [grid, grid] if first else [packed(points, BF16), grid] + [packed(points, F32)] * staged
     specs = [VMEM] * (len(head) + len(weights))
     scratch = [act_scratch(chunks, half + 4, lon)] * 2 + [
         pltpu.VMEM((2, chunks, half, lon // 2, LANES), F32),
@@ -412,15 +431,28 @@
     )
 
 
+def edges_kernel(near, own_ref, part_ref, out_ref):
+    _, _, _, h = place()
+    out_ref[:, :near] = own_ref[...]
+
+    @pl.when(h == 0)
+    def _():
+        out_ref[:, near:] = part_ref[:, :near]
+
+    @pl.when(h == 1)
+    def _():
+        out_ref[:, near:] = part_ref[:, part_ref.shape[1] - near :]
+
+
 def middle_kernel(count, lon, *refs):
     gots, refs = refs[:count], refs[count:]
     even, own3, part5, sum_ref, own_ref, part_ref, inner_ref, outer_ref = refs
     channels, points = even.shape
     t, _, y, h = place()
     near = 2 * lon
-    total = gots[0][...].astype(F32)
+    total = unpack(gots[0], channels, points)
     for g in gots[1:]:
-        total = total + g[...].astype(F32)
+        total = total + unpack(g, channels, points)
     sum_ref[...] = total
     odd = (total + even[...]).astype(BF16)
     flat = total.astype(BF16)
@@ -453,21 +485,24 @@
     _, _, y, _ = place()
     total = before[...]
     for g in gots:
-        total = total + g[...].astype(F32)
+        total = total + unpack(g, *total.shape)
     odd = total + even[...]
     mine_ref[...] = jnp.where(y == 0, total, odd)
-    send_ref[...] = jnp.where(y == 0, odd, total)
+    pack(send_ref, jnp.where(y == 0, odd, total))
 
 
 def output_kernel(mine, other, traj_hbm, out_ref, sem):
-    _, rows, _, lon = out_ref.shape
+    channels, rows, _, lon = out_ref.shape
     half = rows // 2
     t, _, _, h = place()
 
     def emit(upper):
         for r in range(rows):
-            cols = slice((r % half) * lon, (r % half + 1) * lon)
-            out_ref[:, r, 0, :] = (mine if (r < half) == upper else other)[:, cols]
+            start = (r % half) * lon
+            if (r < half) == upper:
+                out_ref[:, r, 0, :] = mine[:, start : start + lon]
+            else:
+                out_ref[:, r, 0, :] = unpack(other, channels, half * lon, start, lon)
 
     @pl.when((h == 0) & (t > 0))
     def _():
@@ -531,23 +566,20 @@
     cells = [(a, b, (a + b) % 2) for a in range(times) for b in range(bands)]
     swap = [(at(a, b), at(a ^ 1, b)) for a, b, _ in cells]
     side = [(at(a, b), at(a, b + (1 if c else -1))) for a, b, c in cells if 0 <= b + (1 if c else -1) < bands]
-    cross = [(at(a, b), at(a ^ 1, b + (-1 if c else 1))) for a, b, c in cells if 0 <= b + (-1 if c else 1) < bands]
 
     root = traj.reshape(channels, rows, 1, lon)
     draws = noise.reshape(channels, rows, 1, lon)
     band = (channels, rows, 1, lon)
     chunks = width // LANES
-    own3, inner_own, to_swap, to_side, to_cross = call(
+    own3, inner_own, to_swap, to_side = call(
         prep_kernel,
-        [((PAD, points), BF16), ((PAD, near), BF16), ((PAD, span), BF16), ((PAD, near), BF16), ((PAD, near), BF16)],
+        [((PAD, points), BF16), ((PAD, near), BF16), ((PAD, span), BF16), ((PAD, near), BF16)],
         (step_index, root),
         [SMEM, HBM],
         [pltpu.VMEM(band, F32), pltpu.VMEM((PAD, rows * lon), BF16), pltpu.SemaphoreType.DMA],
         cost(1e9),
     )
     part5 = lax.ppermute(to_swap, axes, swap)
-    outer_part = lax.ppermute(to_cross, axes, cross)
-    outer_own = lax.ppermute(to_side, axes, side)
     dw = dw_weight.T
     work = 2 * points * width * (2 * channels + 25)
 
@@ -568,18 +600,20 @@
         ],
         cost(20 * work),
     )
+    (to_side,) = call(functools.partial(edges_kernel, near), [((PAD, 2 * near), BF16)], (to_side, part5))
+    outer = lax.ppermute(to_side, axes, side)
     g_part = lax.ppermute(g_send, axes, swap)
     weights = (dw, ln_gain.reshape(1, width), up_weight, down_weight, out_weight.T, g_own)
     staged = groups > RADIX
     inc_own, drift_part, emb_part, coef_part = far(
         True,
         staged,
-        (inner_own, outer_own, part5, outer_part, emb_own, coef_own, keep, partial, embed_weight, time_weight),
+        (inner_own, part5, outer, emb_own, coef_own, keep, partial, embed_weight, time_weight),
         weights,
         half,
         lon,
     )
-    sums = [((channels, points), BF16)] + [((channels, points), F32)] * (1 + staged)
+    sums = [packed(points, BF16), ((channels, points), F32)] + [packed(points, F32)] * staged
     sent, even, *total = call(finish_kernel, sums, (inc_own, drift_part, g_part))
     gots, memory = exchange(sent, *total, groups=groups, memory=None)
     before = None
@@ -608,7 +642,9 @@
         )
         gots, memory = exchange(sent, *total, groups=groups, memory=memory)
     mine, send = call(
-        functools.partial(ending_kernel, len(gots)), [((channels, points), F32)] * 2, (*gots, before, even)
+        functools.partial(ending_kernel, len(gots)),
+        [((channels, points), F32), packed(points, F32)],
+        (*gots, before, even),
     )
     other = lax.ppermute(send, axes, swap)
     (result,) = call(output_kernel, [(band, F32)], (mine, other, root), [VMEM, VMEM, HBM], [pltpu.SemaphoreType.DMA])

time: 76.2 us -> 75.8 us (level)
  the two profiles are of different devices: /device:TPU:16 before, /device:TPU:20 now
where the time goes in v5:
time: 75.8 us; the launch traced here: 75.5 us
  waiting for transfers between devices  32 us (42%)
  Pallas kernels  24.8 us (33%)
  starting transfers between devices  16.5 us (22%)
  between operations  1.13 us (1%)
  local copies, waits for them, and re-layouts  1.07 us (1%)
    pallas_call x10, Pallas kernels, call(): pl.pallas_call(body, out_shape=tuple((jax.ShapeDtypeStruct(s, d) for s, d...  24.8 us
    ppermute x6, waiting for transfers between devices, exchange(): lax.ppermute(sent, 'tm', [(i, i + shift) for i in range(2 * groups - shif...  19.5 us
    ppermute x6, starting transfers between devices, exchange(): lax.ppermute(sent, 'tm', [(i, i + shift) for i in range(2 * groups - shif...  9.95 us
    ppermute x1, waiting for transfers between devices, shards(): other = lax.ppermute(send, axes, swap)  6.68 us
    ppermute x1, waiting for transfers between devices, shards(): part5 = lax.ppermute(to_swap, axes, swap)  5.78 us
    ppermute x1, starting transfers between devices, shards(): outer = lax.ppermute(outer, axes, side)  2.13 us
    ppermute x1, starting transfers between devices, shards(): outer = lax.ppermute(to_side, axes, side)  1.92 us
  transfers between devices with their start and end apart: 12, of which 6 were waited for; matrix products, arithmetic and copies ran while one was open for 0% of the time, Pallas kernels for 20%

profile of v5, /device:TPU:20, one launch (start us, length us, event | category | flops | bytes accessed | tf_op | source)
XLA Modules:
  0.0 75.5 jit_solution(17840550404448330132)
XLA Ops:
  0.7 1.0 %copy-done = f32[1,83,6,192]{3,0,2,1:T(1,128)S(1)} copy-done((f32[1,83,6,192]{3,0,2,1:T(1,128)S(1)}, f32[1,83,6,192]{3,0,2,1:T(1,128)}, u32[]{:S(2)}) %copy-start) | copy-done | bytes 382488
  1.7 1.1 %shard_map.100 = (bf16[88,576]{1,0:T(8,128)(2,1)S(1)}, bf16[88,384]{1,0:T(8,128)(2,1)S(1)}, bf16[88,960]{1,0:T(8,128)(2,1)S(1)}, bf16[88,384]{1,0:T(8,128)(2,1)S(1)}) custom-call(s32[1]{0:T(128)S(6)} %copy.11.idx_ref, f32[83,6,1,192]{3,2,1,0:T(1,128)S(1)} %bitcast.6), custom_call_target="tpu_custom_call" | custom-call | flops 1000000000 | bytes 1048576 | tf_op jit(solution)/shard_map/pallas_call | solution.py:523
  2.8 0.6 collective-permute-start
  3.4 5.8 %collective-permute-done.part_ref.refs_1_.refs_5_ = bf16[88,960]{1,0:T(8,128)(2,1)S(1)} collective-permute-done((bf16[88,960]{1,0:T(8,128)(2,1)S(1)}, bf16[88,960]{1,0:T(8,128)(2,1)S(1)}, u32[]{:S(2)}, u32[]{:S(2)}) %collective-permute-start) | collective-permute-done | bytes 168992 | tf_op jit(solution)/shard_map/ppermute | solution.py:582
  9.2 0.1 shard_map.101
  9.3 1.9 %collective-permute-start.1 = (bf16[88,768]{1,0:T(8,128)(2,1)S(1)}, bf16[88,768]{1,0:T(8,128)(2,1)S(1)}, u32[]{:S(2)}, u32[]{:S(2)}) collective-permute-start(bf16[88,768]{1,0:T(8,128)(2,1)S(1)} %shard_map.101), channel_id=1, source_target_pairs={{1,2},{2,1},{4,5},{5,4},{6,7},{7,6},{9,10},{10,9},{12,13},{13,12},... | collective-permute-start | bytes 405512 | tf_op jit(solution)/shard_map/ppermute | solution.py:604
  11.3 0.0 copy-start.3
  11.3 0.0 copy-start.4
  11.3 0.0 copy-start.7
  11.3 3.2 %shard_map.102 = (bf16[88,512]{1,0:T(8,128)(2,1)S(1)}, f32[8,128]{1,0:T(8,128)S(1)}, bf16[1,576,512]{2,1,0:T(8,128)(2,1)S(1)}, f32[1,4,3,192,128]{4,3,2,1,0:T(8,...) custom-call(s32[1]{0:T(128)S(6)} %copy.11.idx_ref, bf16[88,576]{1,0:T(8,128)(2,1)S(1)} %get-tuple-element.35.own_ref.refs_4_, ...), custom_call_target="tpu_custom_call" | custom-call | flops 2253127680 | bytes 1048576 | tf_op jit(solution)/shard_map/pallas_call | solution.py:523
  14.5 0.1 collective-permute-start.2
  14.6 9.0 %shard_map.103 = (f32[83,576]{1,0:T(8,128)S(1)}, f32[83,576]{1,0:T(8,128)S(1)}, bf16[88,512]{1,0:T(8,128)(2,1)S(1)}, f32[8,128]{1,0:T(8,128)S(1)}) custom-call(bf16[88,384]{1,0:T(8,128)(2,1)S(1)} %get-tuple-element.32.refs_0_, bf16[88,960]{1,0:T(8,128)(2,1)S(1)} %collective-permute-done.part_ref.refs_1_.refs_5_, ...), custom_call_target="tpu_custom_call" | custom-call | flops 2641231872 | bytes 1048576 | tf_op jit(solution)/shard_map/pallas_call | solution.py:523
  23.6 0.1 shard_map.104
  23.7 0.7 collective-permute-start.5
  24.4 1.3 %collective-permute-start.4 = (bf16[8,6336]{1,0:T(8,128)(2,1)S(1)}, bf16[8,6336]{1,0:T(8,128)(2,1)S(1)}, u32[]{:S(2)}, u32[]{:S(2)}) collective-permute-start(bf16[8,6336]{1,0:T(8,128)(2,1)S(1)} %get-tuple-element.44.refs_8_), channel_id=1, source_target_pairs={{0,16},{4,20},{8,24},{12,28},{1,17},{5,21},{9,25},{13,29},{2,18},{... | collective-permute-start | bytes 304136 | tf_op jit(solution)/shard_map/ppermute | solution.py:545
  25.7 4.1 %collective-permute-start.3 = (bf16[8,6336]{1,0:T(8,128)(2,1)S(1)}, bf16[8,6336]{1,0:T(8,128)(2,1)S(1)}, u32[]{:S(2)}, u32[]{:S(2)}) collective-permute-start(bf16[8,6336]{1,0:T(8,128)(2,1)S(1)} %get-tuple-element.44.refs_8_), channel_id=1, source_target_pairs={{0,8},{4,12},{8,16},{12,20},{16,24},{20,28},{1,9},{5,13},{9,17},{1... | collective-permute-start | bytes 304136 | tf_op jit(solution)/shard_map/ppermute | solution.py:545
  29.8 5.0 %collective-permute-done.4.refs_1_ = bf16[8,6336]{1,0:T(8,128)(2,1)S(1)} collective-permute-done((bf16[8,6336]{1,0:T(8,128)(2,1)S(1)}, bf16[8,6336]{1,0:T(8,128)(2,1)S(1)}, u32[]{:S(2)}, u32[]{:S(2)}) %collective-permute-start.4) | collective-permute-done | bytes 101408 | tf_op jit(solution)/shard_map/ppermute | solution.py:545
  34.8 5.0 %collective-permute-done.3.refs_0_ = bf16[8,6336]{1,0:T(8,128)(2,1)S(1)} collective-permute-done((bf16[8,6336]{1,0:T(8,128)(2,1)S(1)}, bf16[8,6336]{1,0:T(8,128)(2,1)S(1)}, u32[]{:S(2)}, u32[]{:S(2)}) %collective-permute-start.3) | collective-permute-done | bytes 101408 | tf_op jit(solution)/shard_map/ppermute | solution.py:545
  39.8 0.3 shard_map.105
  40.0 1.4 %collective-permute-start.6 = (bf16[88,768]{1,0:T(8,128)(2,1)S(1)}, bf16[88,768]{1,0:T(8,128)(2,1)S(1)}, u32[]{:S(2)}, u32[]{:S(2)}) collective-permute-start(bf16[88,768]{1,0:T(8,128)(2,1)S(1)} %get-tuple-element.46), channel_id=1, source_target_pairs={{0,4},{1,5},{2,6},{3,7},{4,0},{5,1},{6,2},{7,3},{8,12},{9,13},{10,... | collective-permute-start | bytes 405512 | tf_op jit(solution)/shard_map/ppermute | solution.py:626
  41.4 2.1 %collective-permute-start.7 = (bf16[88,768]{1,0:T(8,128)(2,1)S(1)}, bf16[88,768]{1,0:T(8,128)(2,1)S(1)}, u32[]{:S(2)}, u32[]{:S(2)}) collective-permute-start(bf16[88,768]{1,0:T(8,128)(2,1)S(1)} %get-tuple-element.47), channel_id=1, source_target_pairs={{1,2},{2,1},{4,5},{5,4},{6,7},{7,6},{9,10},{10,9},{12,13},{13,12},... | collective-permute-start | bytes 405512 | tf_op jit(solution)/shard_map/ppermute | solution.py:627
  43.6 3.3 %shard_map.106 = (bf16[2,576,512]{2,1,0:T(8,128)(2,1)S(1)}, f32[2,4,3,192,128]{4,3,2,1,0:T(8,128)S(1)}) custom-call(bf16[88,576]{1,0:T(8,128)(2,1)S(1)} %get-tuple-element.50.own_ref, bf16[88,576]{1,0:T(8,128)(2,1)S(1)} %get-tuple-element.51.part_ref, bf16[88,512]{1,0:T(8,128)(2,1)S(1)} %get-tuple-element.36.refs_3_.emb_own.refs_2_, ...), custom_call_target="tpu_custom_call" | custom-call | flops 2253127680 | bytes 1048576 | tf_op jit(solution)/shard_map/pallas_call | solution.py:523
  46.9 6.5 %shard_map.107 = (bf16[8,6336]{1,0:T(8,128)(2,1)S(1)}, f32[83,576]{1,0:T(8,128)S(1)}) custom-call(bf16[88,768]{1,0:T(8,128)(2,1)S(1)} %collective-permute-done.6.refs_0_, bf16[88,768]{1,0:T(8,128)(2,1)S(1)} %collective-permute-done.7.refs_1_, bf16[88,512]{1,0:T(8,128)(2,1)S(1)} %get-tuple-element.36.refs_3_.emb_own.refs_2_, ...), custom_call_target="tpu_custom_call" | custom-call | flops 2641231872 | bytes 1048576 | tf_op jit(solution)/shard_map/pallas_call | solution.py:523
  53.4 0.7 collective-permute-start.10
  54.1 1.3 %collective-permute-start.9 = (bf16[8,6336]{1,0:T(8,128)(2,1)S(1)}, bf16[8,6336]{1,0:T(8,128)(2,1)S(1)}, u32[]{:S(2)}, u32[]{:S(2)}) collective-permute-start(bf16[8,6336]{1,0:T(8,128)(2,1)S(1)} %get-tuple-element.54), channel_id=1, source_target_pairs={{0,16},{4,20},{8,24},{12,28},{1,17},{5,21},{9,25},{13,29},{2,18},{... | collective-permute-start | bytes 304136 | tf_op jit(solution)/shard_map/ppermute | solution.py:545
  55.4 1.9 %collective-permute-start.8 = (bf16[8,6336]{1,0:T(8,128)(2,1)S(1)}, bf16[8,6336]{1,0:T(8,128)(2,1)S(1)}, u32[]{:S(2)}, u32[]{:S(2)}) collective-permute-start(bf16[8,6336]{1,0:T(8,128)(2,1)S(1)} %get-tuple-element.54), channel_id=1, source_target_pairs={{0,8},{4,12},{8,16},{12,20},{16,24},{20,28},{1,9},{5,13},{9,17},{1... | collective-permute-start | bytes 304136 | tf_op jit(solution)/shard_map/ppermute | solution.py:545
  57.4 5.5 %collective-permute-done.9.refs_1_ = bf16[8,6336]{1,0:T(8,128)(2,1)S(1)} collective-permute-done((bf16[8,6336]{1,0:T(8,128)(2,1)S(1)}, bf16[8,6336]{1,0:T(8,128)(2,1)S(1)}, u32[]{:S(2)}, u32[]{:S(2)}) %collective-permute-start.9) | collective-permute-done | bytes 101408 | tf_op jit(solution)/shard_map/ppermute | solution.py:545
  62.8 4.0 %collective-permute-done.8.refs_0_ = bf16[8,6336]{1,0:T(8,128)(2,1)S(1)} collective-permute-done((bf16[8,6336]{1,0:T(8,128)(2,1)S(1)}, bf16[8,6336]{1,0:T(8,128)(2,1)S(1)}, u32[]{:S(2)}, u32[]{:S(2)}) %collective-permute-start.8) | collective-permute-done | bytes 101408 | tf_op jit(solution)/shard_map/ppermute | solution.py:545
  66.9 0.2 shard_map.108
  67.1 0.4 collective-permute-start.11
  67.5 6.7 %collective-permute-done.11.other = f32[8,6336]{1,0:T(8,128)S(1)} collective-permute-done((f32[8,6336]{1,0:T(8,128)S(1)}, f32[8,6336]{1,0:T(8,128)S(1)}, u32[]{:S(2)}, u32[]{:S(2)}) %collective-permute-start.11) | collective-permute-done | bytes 202784 | tf_op jit(solution)/shard_map/ppermute | solution.py:649
  74.2 1.1 %shard_map.109 = f32[83,6,1,192]{3,2,1,0:T(1,128)} custom-call(f32[83,576]{1,0:T(8,128)S(1)} %get-tuple-element.57.mine, f32[8,6336]{1,0:T(8,128)S(1)} %collective-permute-done.11.other, f32[83,6,1,192]{3,2,1,0:T(1,128)S(1)} %bitcast.8), custom_call_target="tpu_custom_call" | custom-call | tf_op jit(solution)/shard_map/pallas_call | solution.py:523
  (22 shorter events, 0.0 us)
Async XLA Ops:
  0.7 1.0 %copy-start = (f32[1,83,6,192]{3,0,2,1:T(1,128)S(1)}, f32[1,83,6,192]{3,0,2,1:T(1,128)}, u32[]{:S(2)}) copy-start(f32[1,83,6,192]{3,0,2,1:T(1,128)} %param.10) | copy-start | bytes 1147396
  1.7 9.5 %copy-start.1 = (f32[1,83,6,192]{3,0,2,1:T(1,128)S(1)}, f32[1,83,6,192]{3,0,2,1:T(1,128)}, u32[]{:S(2)}) copy-start(f32[1,83,6,192]{3,0,2,1:T(1,128)} %param.10) | copy-start | bytes 1147396
  1.7 9.5 %copy-start.2 = (f32[512,512]{1,0:T(8,128)S(1)}, f32[512,512]{1,0:T(8,128)}, u32[]{:S(2)}) copy-start(f32[512,512]{1,0:T(8,128)} %refs_8_.1) | copy-start | bytes 3145732
  1.7 9.5 %copy-start.5 = (f32[1,83,6,192]{3,0,2,1:T(1,128)S(1)}, f32[1,83,6,192]{3,0,2,1:T(1,128)}, u32[]{:S(2)}) copy-start(f32[1,83,6,192]{3,0,2,1:T(1,128)} %param.11) | copy-start | bytes 1147396
  1.7 9.5 %copy-start.6 = (bf16[83,512]{1,0:T(8,128)(2,1)S(1)}, bf16[83,512]{1,0:T(8,128)(2,1)}, u32[]{:S(2)}) copy-start(bf16[83,512]{1,0:T(8,128)(2,1)} %refs_7_.1) | copy-start | bytes 254980
  1.7 9.5 %copy-start.8 = (f32[512,25]{0,1:T(8,128)S(1)}, f32[512,25]{0,1:T(8,128)}, u32[]{:S(2)}) copy-start(f32[512,25]{0,1:T(8,128)} %param.15) | copy-start | bytes 153604
  2.8 6.4 %collective-permute-start = (bf16[88,960]{1,0:T(8,128)(2,1)S(1)}, bf16[88,960]{1,0:T(8,128)(2,1)S(1)}, u32[]{:S(2)}, u32[]{:S(2)}) collective-permute-start(bf16[88,960]{1,0:T(8,128)(2,1)S(1)} %get-tuple-element.33), channel_id=1, source_target_pairs={{0,4},{1,5},{2,6},{3,7},{4,0},{5,1},{6,2},{7,3},{8,12},{9,13},{10,... | collective-permute-start | bytes 506888 | tf_op jit(solution)/shard_map/ppermute | solution.py:582
  9.3 5.3 %collective-permute-start.1 = (bf16[88,768]{1,0:T(8,128)(2,1)S(1)}, bf16[88,768]{1,0:T(8,128)(2,1)S(1)}, u32[]{:S(2)}, u32[]{:S(2)}) collective-permute-start(bf16[88,768]{1,0:T(8,128)(2,1)S(1)} %shard_map.101), channel_id=1, source_target_pairs={{1,2},{2,1},{4,5},{5,4},{6,7},{7,6},{9,10},{10,9},{12,13},{13,12},... | collective-permute-start | bytes 405512 | tf_op jit(solution)/shard_map/ppermute | solution.py:604
  11.3 3.3 %copy-start.3 = (bf16[512,1024]{1,0:T(8,128)(2,1)S(1)}, bf16[512,1024]{1,0:T(8,128)(2,1)}, u32[]{:S(2)}) copy-start(bf16[512,1024]{1,0:T(8,128)(2,1)} %refs_11_.3) | copy-start | bytes 3145732
  11.3 3.3 %copy-start.4 = (bf16[1024,512]{1,0:T(8,128)(2,1)S(1)}, bf16[1024,512]{1,0:T(8,128)(2,1)}, u32[]{:S(2)}) copy-start(bf16[1024,512]{1,0:T(8,128)(2,1)} %refs_12_.3) | copy-start | bytes 3145732
  11.3 3.3 %copy-start.7 = (bf16[512,83]{0,1:T(8,128)(2,1)S(1)}, bf16[512,83]{0,1:T(8,128)(2,1)}, u32[]{:S(2)}) copy-start(bf16[512,83]{0,1:T(8,128)(2,1)} %param.19) | copy-start | bytes 254980
  11.3 3.3 %copy-start.9 = (f32[512]{0:T(512)S(1)}, f32[512]{0:T(512)}, u32[]{:S(2)}) copy-start(f32[512]{0:T(512)} %param.16) | copy-start | bytes 6148
  14.5 9.1 %collective-permute-start.2 = (f32[83,576]{1,0:T(8,128)S(1)}, f32[83,576]{1,0:T(8,128)S(1)}, u32[]{:S(2)}, u32[]{:S(2)}) collective-permute-start(f32[83,576]{1,0:T(8,128)S(1)} %get-tuple-element.43), channel_id=1, source_target_pairs={{0,4},{1,5},{2,6},{3,7},{4,0},{5,1},{6,2},{7,3},{8,12},{9,13},{10,... | collective-permute-start | bytes 573704 | tf_op jit(solution)/shard_map/ppermute | solution.py:605
  23.7 6.1 %collective-permute-start.5 = (bf16[8,6336]{1,0:T(8,128)(2,1)S(1)}, bf16[8,6336]{1,0:T(8,128)(2,1)S(1)}, u32[]{:S(2)}, u32[]{:S(2)}) collective-permute-start(bf16[8,6336]{1,0:T(8,128)(2,1)S(1)} %get-tuple-element.44.refs_8_), channel_id=1, source_target_pairs={{0,24},{4,28},{1,25},{5,29},{2,26},{6,30},{3,27},{7,31}} | collective-permute-start | bytes 304136 | tf_op jit(solution)/shard_map/ppermute | solution.py:545
  24.4 10.4 %collective-permute-start.4 = (bf16[8,6336]{1,0:T(8,128)(2,1)S(1)}, bf16[8,6336]{1,0:T(8,128)(2,1)S(1)}, u32[]{:S(2)}, u32[]{:S(2)}) collective-permute-start(bf16[8,6336]{1,0:T(8,128)(2,1)S(1)} %get-tuple-element.44.refs_8_), channel_id=1, source_target_pairs={{0,16},{4,20},{8,24},{12,28},{1,17},{5,21},{9,25},{13,29},{2,18},{... | collective-permute-start | bytes 304136 | tf_op jit(solution)/shard_map/ppermute | solution.py:545
  25.7 14.1 %collective-permute-start.3 = (bf16[8,6336]{1,0:T(8,128)(2,1)S(1)}, bf16[8,6336]{1,0:T(8,128)(2,1)S(1)}, u32[]{:S(2)}, u32[]{:S(2)}) collective-permute-start(bf16[8,6336]{1,0:T(8,128)(2,1)S(1)} %get-tuple-element.44.refs_8_), channel_id=1, source_target_pairs={{0,8},{4,12},{8,16},{12,20},{16,24},{20,28},{1,9},{5,13},{9,17},{1... | collective-permute-start | bytes 304136 | tf_op jit(solution)/shard_map/ppermute | solution.py:545
  40.0 6.8 %collective-permute-start.6 = (bf16[88,768]{1,0:T(8,128)(2,1)S(1)}, bf16[88,768]{1,0:T(8,128)(2,1)S(1)}, u32[]{:S(2)}, u32[]{:S(2)}) collective-permute-start(bf16[88,768]{1,0:T(8,128)(2,1)S(1)} %get-tuple-element.46), channel_id=1, source_target_pairs={{0,4},{1,5},{2,6},{3,7},{4,0},{5,1},{6,2},{7,3},{8,12},{9,13},{10,... | collective-permute-start | bytes 405512 | tf_op jit(solution)/shard_map/ppermute | solution.py:626
  41.4 5.5 %collective-permute-start.7 = (bf16[88,768]{1,0:T(8,128)(2,1)S(1)}, bf16[88,768]{1,0:T(8,128)(2,1)S(1)}, u32[]{:S(2)}, u32[]{:S(2)}) collective-permute-start(bf16[88,768]{1,0:T(8,128)(2,1)S(1)} %get-tuple-element.47), channel_id=1, source_target_pairs={{1,2},{2,1},{4,5},{5,4},{6,7},{7,6},{9,10},{10,9},{12,13},{13,12},... | collective-permute-start | bytes 405512 | tf_op jit(solution)/shard_map/ppermute | solution.py:627
  53.4 3.9 %collective-permute-start.10 = (bf16[8,6336]{1,0:T(8,128)(2,1)S(1)}, bf16[8,6336]{1,0:T(8,128)(2,1)S(1)}, u32[]{:S(2)}, u32[]{:S(2)}) collective-permute-start(bf16[8,6336]{1,0:T(8,128)(2,1)S(1)} %get-tuple-element.54), channel_id=1, source_target_pairs={{0,24},{4,28},{1,25},{5,29},{2,26},{6,30},{3,27},{7,31}} | collective-permute-start | bytes 304136 | tf_op jit(solution)/shard_map/ppermute | solution.py:545
  54.1 8.7 %collective-permute-start.9 = (bf16[8,6336]{1,0:T(8,128)(2,1)S(1)}, bf16[8,6336]{1,0:T(8,128)(2,1)S(1)}, u32[]{:S(2)}, u32[]{:S(2)}) collective-permute-start(bf16[8,6336]{1,0:T(8,128)(2,1)S(1)} %get-tuple-element.54), channel_id=1, source_target_pairs={{0,16},{4,20},{8,24},{12,28},{1,17},{5,21},{9,25},{13,29},{2,18},{... | collective-permute-start | bytes 304136 | tf_op jit(solution)/shard_map/ppermute | solution.py:545
  55.4 11.5 %collective-permute-start.8 = (bf16[8,6336]{1,0:T(8,128)(2,1)S(1)}, bf16[8,6336]{1,0:T(8,128)(2,1)S(1)}, u32[]{:S(2)}, u32[]{:S(2)}) collective-permute-start(bf16[8,6336]{1,0:T(8,128)(2,1)S(1)} %get-tuple-element.54), channel_id=1, source_target_pairs={{0,8},{4,12},{8,16},{12,20},{16,24},{20,28},{1,9},{5,13},{9,17},{1... | collective-permute-start | bytes 304136 | tf_op jit(solution)/shard_map/ppermute | solution.py:545
  67.1 7.1 %collective-permute-start.11 = (f32[8,6336]{1,0:T(8,128)S(1)}, f32[8,6336]{1,0:T(8,128)S(1)}, u32[]{:S(2)}, u32[]{:S(2)}) collective-permute-start(f32[8,6336]{1,0:T(8,128)S(1)} %get-tuple-element.58), channel_id=1, source_target_pairs={{0,4},{1,5},{2,6},{3,7},{4,0},{5,1},{6,2},{7,3},{8,12},{9,13},{10,... | collective-permute-start | bytes 608264 | tf_op jit(solution)/shard_map/ppermute | solution.py:649

commit v6 on v5

--- a/solution.py
+++ b/solution.py
@@ -212,22 +212,21 @@
     return ((8, PAD // 8 * points), dtype)
 
 
-def finish(first_sum, second_sum, known, sent_ref, even_ref, rest):
+def finish(first_sum, second_sum, known, sent_ref, even_ref, total_ref):
     _, _, y, _ = place()
     even_ref[...] = jnp.where(y == 0, first_sum, second_sum)
     total = first_sum + second_sum
     if known is not None:
         total = total - unpack(known, *total.shape)
     pack(sent_ref, total)
-    for total_ref in rest:
-        pack(total_ref, total)
-
-
-def finish_kernel(inc_own, drift_part, g_part, sent_ref, even_ref, *rest):
-    finish(inc_own[...], drift_part[...] + g_part[...], None, sent_ref, even_ref, rest)
-
-
-def far_kernel(first, staged, sizes, *refs):
+    pack(total_ref, total)
+
+
+def finish_kernel(inc_own, drift_part, g_part, sent_ref, even_ref, total_ref):
+    finish(inc_own[...], drift_part[...] + g_part[...], None, sent_ref, even_ref, total_ref)
+
+
+def far_kernel(first, sizes, *refs):
     half, lon, chunks, ff, _ = sizes
     width = chunks * LANES
     refs = list(refs)
@@ -248,8 +247,7 @@
         inc_own, drift_part, emb_part, coef_part = take(4)
     else:
         (g_part,) = take(1)
-        sent_ref, even_ref = take(2)
-        rest = take(1) if staged else []
+        sent_ref, even_ref, total_ref = take(3)
     act0, act1, conv_ref, norm_ref, up_out, hid_ref, bo_ref = take(7)
     if first:
         time_ref, time_sem = take(2)
@@ -390,7 +388,7 @@
         unit()
     out_unit(1)
     if not first:
-        finish(incs[0], incs[1], sent_in, sent_ref, even_ref, rest)
+        finish(incs[0], incs[1], sent_in, sent_ref, even_ref, total_ref)
 
 
 def cost(flops, nbytes=1 << 20):
@@ -401,14 +399,14 @@
     return pltpu.VMEM((chunks, rows, lon + 2 * LEAD, LANES), F32)
 
 
-def far(first, staged, head, weights, half, lon):
+def far(first, head, weights, half, lon):
     _, _, up, _, _, g_own = weights[:6]
     channels, points = g_own.shape
     width, ff = up.shape
     chunks = width // LANES
     block = points // 2
     grid = ((channels, points), F32)
-    outs = [grid, grid] if first else [packed(points, BF16), grid] + [packed(points, F32)] * staged
+    outs = [grid, grid] if first else [packed(points, BF16), grid, packed(points, F32)]
     specs = [VMEM] * (len(head) + len(weights))
     scratch = [act_scratch(chunks, half + 4, lon)] * 2 + [
         pltpu.VMEM((2, chunks, half, lon // 2, LANES), F32),
@@ -422,7 +420,7 @@
         specs[len(head) - 1] = HBM
         scratch += [pltpu.VMEM(head[-1].shape, F32), pltpu.SemaphoreType.DMA]
     return call(
-        functools.partial(far_kernel, first, staged, (half, lon, chunks, ff, channels)),
+        functools.partial(far_kernel, first, (half, lon, chunks, ff, channels)),
         outs,
         (*head, *weights),
         specs,
@@ -444,8 +442,18 @@
         out_ref[:, near:] = part_ref[:, part_ref.shape[1] - near :]
 
 
-def middle_kernel(count, lon, *refs):
-    gots, refs = refs[:count], refs[count:]
+def relay_kernel(total_ref, got_ref, out_ref):
+    out_ref[...] = (total_ref[...] + got_ref[...].astype(F32)).astype(BF16)
+
+
+def middle_kernel(count, chained, lon, *refs):
+    gots, refs = refs[:count], list(refs[count:])
+    if chained:
+        total_ref, offset_ref = refs.pop(0), refs.pop()
+        arrived = gots[0][...].astype(F32)
+        for g in gots[1:]:
+            arrived = arrived + g[...].astype(F32)
+        offset_ref[...] = (total_ref[...] + arrived).astype(BF16).astype(F32) - arrived
     even, own3, part5, sum_ref, own_ref, part_ref, inner_ref, outer_ref = refs
     channels, points = even.shape
     t, _, y, h = place()
@@ -531,7 +539,16 @@
     )(*ins)
 
 
-def exchange(sent, total=None, *, groups, memory):
+def chain(sent, total, groups):
+    gots = []
+    for last in range(groups - 1):
+        if last:
+            (sent,) = call(relay_kernel, [(total.shape, BF16)], (total, gots[-1]))
+        gots.append(lax.ppermute(sent, "tm", [(2 * last + y, 2 * last + 2 + y) for y in range(2)]))
+    return gots
+
+
+def exchange(sent, total, groups, memory):
     gots, kept = [], []
     base, moved, unit = sent, None, 1
     while unit < groups:
@@ -607,22 +624,31 @@
     staged = groups > RADIX
     inc_own, drift_part, emb_part, coef_part = far(
         True,
-        staged,
         (inner_own, part5, outer, emb_own, coef_own, keep, partial, embed_weight, time_weight),
         weights,
         half,
         lon,
     )
-    sums = [packed(points, BF16), ((channels, points), F32)] + [packed(points, F32)] * staged
-    sent, even, *total = call(finish_kernel, sums, (inc_own, drift_part, g_part))
-    gots, memory = exchange(sent, *total, groups=groups, memory=None)
+    sums = [packed(points, BF16), ((channels, points), F32), packed(points, F32)]
+    sent, even, total = call(finish_kernel, sums, (inc_own, drift_part, g_part))
+
+    def collect(sent, total, memory):
+        if staged:
+            return exchange(sent, total, groups, memory)
+        return chain(sent, total, groups), memory
+
+    gots, memory = collect(sent, total, None)
     before = None
     for _ in range(1, ITERS):
-        before, s_own, s_part, inner, outer = call(
-            functools.partial(middle_kernel, len(gots), lon),
-            [((channels, points), F32)] + [((PAD, points), BF16)] * 2 + [((PAD, 2 * near), BF16)] * 2,
-            (*gots, even, own3, part5),
+        before, s_own, s_part, inner, outer, *offset = call(
+            functools.partial(middle_kernel, len(gots), not staged, lon),
+            [((channels, points), F32)]
+            + [((PAD, points), BF16)] * 2
+            + [((PAD, 2 * near), BF16)] * 2
+            + [packed(points, F32)] * (not staged),
+            (*gots, *([] if staged else [total]), even, own3, part5),
         )
+        known = sent.astype(F32) if staged else offset[0]
         inner = lax.ppermute(inner, axes, swap)
         outer = lax.ppermute(outer, axes, side)
         keep, partial = call(
@@ -632,15 +658,14 @@
             scratch=[act_scratch(chunks, half, lon)] * 2,
             estimate=cost(20 * work),
         )
-        sent, even, *total = far(
+        sent, even, total = far(
             False,
-            staged,
-            (inner, outer, emb_own, emb_part, coef_own, coef_part, keep, partial, sent),
+            (inner, outer, emb_own, emb_part, coef_own, coef_part, keep, partial, known),
             weights + (g_part,),
             half,
             lon,
         )
-        gots, memory = exchange(sent, *total, groups=groups, memory=memory)
+        gots, memory = collect(sent, total, memory)
     mine, send = call(
         functools.partial(ending_kernel, len(gots)),
         [((channels, points), F32), packed(points, F32)],

time: 75.8 us -> 73.9 us (0.975)
  the two profiles are of different devices: /device:TPU:20 before, /device:TPU:24 now
where the time goes in v6:
time: 73.9 us; the launch traced here: 73.6 us
  waiting for transfers between devices  32.6 us (44%)
  Pallas kernels  24.5 us (33%)
  starting transfers between devices  14.3 us (19%)
  between operations  1.16 us (2%)
  local copies, waits for them, and re-layouts  1.07 us (1%)
    pallas_call x14, Pallas kernels, call(): pl.pallas_call(body, out_shape=tuple((jax.ShapeDtypeStruct(s, d) for s, d...  24.5 us
    ppermute x6, waiting for transfers between devices, chain(): lax.ppermute(sent, 'tm', [(2 * last + y, 2 * last + 2 + y) for y in range...  22.2 us
    ppermute x1, waiting for transfers between devices, shards(): other = lax.ppermute(send, axes, swap)  5.64 us
    ppermute x6, starting transfers between devices, chain(): lax.ppermute(sent, 'tm', [(2 * last + y, 2 * last + 2 + y) for y in range...  5.25 us
    ppermute x1, waiting for transfers between devices, shards(): part5 = lax.ppermute(to_swap, axes, swap)  4.77 us
    ppermute x1, starting transfers between devices, shards(): g_part = lax.ppermute(g_send, axes, swap)  2.93 us
    ppermute x1, starting transfers between devices, shards(): part5 = lax.ppermute(to_swap, axes, swap)  1.57 us
    ppermute x1, starting transfers between devices, shards(): other = lax.ppermute(send, axes, swap)  1.53 us
  transfers between devices with their start and end apart: 12, of which 4 were waited for; matrix products, arithmetic and copies ran while one was open for 0% of the time, Pallas kernels for 20%

profile of v6, /device:TPU:24, one launch (start us, length us, event | category | flops | bytes accessed | tf_op | source)
XLA Modules:
  0.0 73.6 jit_solution(3273209919704968957)
XLA Ops:
  0.7 1.0 %copy-done = f32[1,83,6,192]{3,0,2,1:T(1,128)S(1)} copy-done((f32[1,83,6,192]{3,0,2,1:T(1,128)S(1)}, f32[1,83,6,192]{3,0,2,1:T(1,128)}, u32[]{:S(2)}) %copy-start) | copy-done | bytes 382488
  1.7 1.1 %shard_map.100 = (bf16[88,576]{1,0:T(8,128)(2,1)S(1)}, bf16[88,384]{1,0:T(8,128)(2,1)S(1)}, bf16[88,960]{1,0:T(8,128)(2,1)S(1)}, bf16[88,384]{1,0:T(8,128)(2,1)S(1)}) custom-call(s32[1]{0:T(128)S(6)} %copy.11.idx_ref, f32[83,6,1,192]{3,2,1,0:T(1,128)S(1)} %bitcast.6), custom_call_target="tpu_custom_call" | custom-call | flops 1000000000 | bytes 1048576 | tf_op jit(solution)/shard_map/pallas_call | solution.py:531
  2.8 1.6 %collective-permute-start = (bf16[88,960]{1,0:T(8,128)(2,1)S(1)}, bf16[88,960]{1,0:T(8,128)(2,1)S(1)}, u32[]{:S(2)}, u32[]{:S(2)}) collective-permute-start(bf16[88,960]{1,0:T(8,128)(2,1)S(1)} %get-tuple-element.36), channel_id=1, source_target_pairs={{0,4},{1,5},{2,6},{3,7},{4,0},{5,1},{6,2},{7,3},{8,12},{9,13},{10,... | collective-permute-start | bytes 506888 | tf_op jit(solution)/shard_map/ppermute | solution.py:599
  4.4 4.8 %collective-permute-done.part_ref.refs_1_.refs_6_ = bf16[88,960]{1,0:T(8,128)(2,1)S(1)} collective-permute-done((bf16[88,960]{1,0:T(8,128)(2,1)S(1)}, bf16[88,960]{1,0:T(8,128)(2,1)S(1)}, u32[]{:S(2)}, u32[]{:S(2)}) %collective-permute-start) | collective-permute-done | bytes 168992 | tf_op jit(solution)/shard_map/ppermute | solution.py:599
  9.2 0.7 collective-permute-start.1
  9.9 0.0 copy-start.3
  9.9 0.0 copy-start.4
  9.9 0.0 copy-start.7
  9.9 0.0 copy-start.9
  10.0 3.2 %shard_map.102 = (bf16[88,512]{1,0:T(8,128)(2,1)S(1)}, f32[8,128]{1,0:T(8,128)S(1)}, bf16[1,576,512]{2,1,0:T(8,128)(2,1)S(1)}, f32[1,4,3,192,128]{4,3,2,1,0:T(8,...) custom-call(s32[1]{0:T(128)S(6)} %copy.11.idx_ref, bf16[88,576]{1,0:T(8,128)(2,1)S(1)} %get-tuple-element.38.own_ref.refs_5_, ...), custom_call_target="tpu_custom_call" | custom-call | flops 2253127680 | bytes 1048576 | tf_op jit(solution)/shard_map/pallas_call | solution.py:531
  13.1 2.9 %collective-permute-start.2 = (f32[83,576]{1,0:T(8,128)S(1)}, f32[83,576]{1,0:T(8,128)S(1)}, u32[]{:S(2)}, u32[]{:S(2)}) collective-permute-start(f32[83,576]{1,0:T(8,128)S(1)} %get-tuple-element.46), channel_id=1, source_target_pairs={{0,4},{1,5},{2,6},{3,7},{4,0},{5,1},{6,2},{7,3},{8,12},{9,13},{10,... | collective-permute-start | bytes 573704 | tf_op jit(solution)/shard_map/ppermute | solution.py:622
  16.1 8.6 %shard_map.103 = (f32[83,576]{1,0:T(8,128)S(1)}, f32[83,576]{1,0:T(8,128)S(1)}, bf16[88,512]{1,0:T(8,128)(2,1)S(1)}, f32[8,128]{1,0:T(8,128)S(1)}) custom-call(bf16[88,384]{1,0:T(8,128)(2,1)S(1)} %get-tuple-element.35.refs_0_, bf16[88,960]{1,0:T(8,128)(2,1)S(1)} %collective-permute-done.part_ref.refs_1_.refs_6_, ...), custom_call_target="tpu_custom_call" | custom-call | flops 2641231872 | bytes 1048576 | tf_op jit(solution)/shard_map/pallas_call | solution.py:531
  24.7 0.0 collective-permute-done.2.g_part.refs_15_
  24.7 0.1 shard_map.104
  24.9 0.7 collective-permute-start.3
  25.5 0.0 collective-permute-done.3.got_ref.refs_0_
  25.6 0.7 collective-permute-start.4
  26.3 1.3 %collective-permute-start.5 = (bf16[8,6336]{1,0:T(8,128)(2,1)S(1)}, bf16[8,6336]{1,0:T(8,128)(2,1)S(1)}, u32[]{:S(2)}, u32[]{:S(2)}) collective-permute-start(bf16[8,6336]{1,0:T(8,128)(2,1)S(1)} %shard_map.106), channel_id=1, source_target_pairs={{16,24},{20,28},{17,25},{21,29},{18,26},{22,30},{19,27},{23,31}} | collective-permute-start | bytes 304136 | tf_op jit(solution)/shard_map/ppermute | solution.py:547
  27.6 13.0 %collective-permute-done.5.refs_2_ = bf16[8,6336]{1,0:T(8,128)(2,1)S(1)} collective-permute-done((bf16[8,6336]{1,0:T(8,128)(2,1)S(1)}, bf16[8,6336]{1,0:T(8,128)(2,1)S(1)}, u32[]{:S(2)}, u32[]{:S(2)}) %collective-permute-start.5) | collective-permute-done | bytes 101408 | tf_op jit(solution)/shard_map/ppermute | solution.py:547
  40.5 0.3 shard_map.107
  40.9 1.5 %collective-permute-start.6 = (bf16[88,768]{1,0:T(8,128)(2,1)S(1)}, bf16[88,768]{1,0:T(8,128)(2,1)S(1)}, u32[]{:S(2)}, u32[]{:S(2)}) collective-permute-start(bf16[88,768]{1,0:T(8,128)(2,1)S(1)} %get-tuple-element.50), channel_id=1, source_target_pairs={{0,4},{1,5},{2,6},{3,7},{4,0},{5,1},{6,2},{7,3},{8,12},{9,13},{10,... | collective-permute-start | bytes 405512 | tf_op jit(solution)/shard_map/ppermute | solution.py:652
  42.3 0.9 %collective-permute-start.7 = (bf16[88,768]{1,0:T(8,128)(2,1)S(1)}, bf16[88,768]{1,0:T(8,128)(2,1)S(1)}, u32[]{:S(2)}, u32[]{:S(2)}) collective-permute-start(bf16[88,768]{1,0:T(8,128)(2,1)S(1)} %get-tuple-element.51), channel_id=1, source_target_pairs={{1,2},{2,1},{4,5},{5,4},{6,7},{7,6},{9,10},{10,9},{12,13},{13,12},... | collective-permute-start | bytes 405512 | tf_op jit(solution)/shard_map/ppermute | solution.py:653
  43.2 3.3 %shard_map.108 = (bf16[2,576,512]{2,1,0:T(8,128)(2,1)S(1)}, f32[2,4,3,192,128]{4,3,2,1,0:T(8,128)S(1)}) custom-call(bf16[88,576]{1,0:T(8,128)(2,1)S(1)} %get-tuple-element.54.own_ref, bf16[88,576]{1,0:T(8,128)(2,1)S(1)} %get-tuple-element.55.part_ref, bf16[88,512]{1,0:T(8,128)(2,1)S(1)} %get-tuple-element.39.refs_3_.emb_own.refs_2_, ...), custom_call_target="tpu_custom_call" | custom-call | flops 2253127680 | bytes 1048576 | tf_op jit(solution)/shard_map/pallas_call | solution.py:531
  46.5 6.4 %shard_map.109 = (bf16[8,6336]{1,0:T(8,128)(2,1)S(1)}, f32[83,576]{1,0:T(8,128)S(1)}, f32[8,6336]{1,0:T(8,128)S(1)}) custom-call(bf16[88,768]{1,0:T(8,128)(2,1)S(1)} %collective-permute-done.6.refs_0_, bf16[88,768]{1,0:T(8,128)(2,1)S(1)} %collective-permute-done.7.refs_1_, bf16[88,512]{1,0:T(8,128)(2,1)S(1)} %get-tuple-element.39.refs_3_.emb_own.refs_2_, ...), custom_call_target="tpu_custom_call" | custom-call | flops 2641231872 | bytes 1048576 | tf_op jit(solution)/shard_map/pallas_call | solution.py:531
  52.9 0.7 collective-permute-start.8
  53.6 0.7 collective-permute-start.9
  54.3 1.3 %collective-permute-start.10 = (bf16[8,6336]{1,0:T(8,128)(2,1)S(1)}, bf16[8,6336]{1,0:T(8,128)(2,1)S(1)}, u32[]{:S(2)}, u32[]{:S(2)}) collective-permute-start(bf16[8,6336]{1,0:T(8,128)(2,1)S(1)} %shard_map.111), channel_id=1, source_target_pairs={{16,24},{20,28},{17,25},{21,29},{18,26},{22,30},{19,27},{23,31}} | collective-permute-start | bytes 304136 | tf_op jit(solution)/shard_map/ppermute | solution.py:547
  55.6 9.2 %collective-permute-done.10.refs_2_ = bf16[8,6336]{1,0:T(8,128)(2,1)S(1)} collective-permute-done((bf16[8,6336]{1,0:T(8,128)(2,1)S(1)}, bf16[8,6336]{1,0:T(8,128)(2,1)S(1)}, u32[]{:S(2)}, u32[]{:S(2)}) %collective-permute-start.10) | collective-permute-done | bytes 101408 | tf_op jit(solution)/shard_map/ppermute | solution.py:547
  64.9 0.2 shard_map.112
  65.1 1.5 %collective-permute-start.11 = (f32[8,6336]{1,0:T(8,128)S(1)}, f32[8,6336]{1,0:T(8,128)S(1)}, u32[]{:S(2)}, u32[]{:S(2)}) collective-permute-start(f32[8,6336]{1,0:T(8,128)S(1)} %get-tuple-element.64), channel_id=1, source_target_pairs={{0,4},{1,5},{2,6},{3,7},{4,0},{5,1},{6,2},{7,3},{8,12},{9,13},{10,... | collective-permute-start | bytes 608264 | tf_op jit(solution)/shard_map/ppermute | solution.py:674
  66.6 5.6 %collective-permute-done.11.other = f32[8,6336]{1,0:T(8,128)S(1)} collective-permute-done((f32[8,6336]{1,0:T(8,128)S(1)}, f32[8,6336]{1,0:T(8,128)S(1)}, u32[]{:S(2)}, u32[]{:S(2)}) %collective-permute-start.11) | collective-permute-done | bytes 202784 | tf_op jit(solution)/shard_map/ppermute | solution.py:674
  72.3 1.2 %shard_map.113 = f32[83,6,1,192]{3,2,1,0:T(1,128)} custom-call(f32[83,576]{1,0:T(8,128)S(1)} %get-tuple-element.63.mine, f32[8,6336]{1,0:T(8,128)S(1)} %collective-permute-done.11.other, f32[83,6,1,192]{3,2,1,0:T(1,128)S(1)} %bitcast.8), custom_call_target="tpu_custom_call" | custom-call | tf_op jit(solution)/shard_map/pallas_call | solution.py:531
  (26 shorter events, 0.2 us)
Async XLA Ops:
  0.7 1.0 %copy-start = (f32[1,83,6,192]{3,0,2,1:T(1,128)S(1)}, f32[1,83,6,192]{3,0,2,1:T(1,128)}, u32[]{:S(2)}) copy-start(f32[1,83,6,192]{3,0,2,1:T(1,128)} %param.10) | copy-start | bytes 1147396
  1.7 8.2 %copy-start.1 = (f32[1,83,6,192]{3,0,2,1:T(1,128)S(1)}, f32[1,83,6,192]{3,0,2,1:T(1,128)}, u32[]{:S(2)}) copy-start(f32[1,83,6,192]{3,0,2,1:T(1,128)} %param.10) | copy-start | bytes 1147396
  1.7 8.2 %copy-start.2 = (f32[512,512]{1,0:T(8,128)S(1)}, f32[512,512]{1,0:T(8,128)}, u32[]{:S(2)}) copy-start(f32[512,512]{1,0:T(8,128)} %refs_8_.1) | copy-start | bytes 3145732
  1.7 8.2 %copy-start.5 = (f32[1,83,6,192]{3,0,2,1:T(1,128)S(1)}, f32[1,83,6,192]{3,0,2,1:T(1,128)}, u32[]{:S(2)}) copy-start(f32[1,83,6,192]{3,0,2,1:T(1,128)} %param.11) | copy-start | bytes 1147396
  1.7 8.2 %copy-start.6 = (bf16[83,512]{1,0:T(8,128)(2,1)S(1)}, bf16[83,512]{1,0:T(8,128)(2,1)}, u32[]{:S(2)}) copy-start(bf16[83,512]{1,0:T(8,128)(2,1)} %refs_7_.1) | copy-start | bytes 254980
  1.7 8.2 %copy-start.8 = (f32[512,25]{0,1:T(8,128)S(1)}, f32[512,25]{0,1:T(8,128)}, u32[]{:S(2)}) copy-start(f32[512,25]{0,1:T(8,128)} %param.15) | copy-start | bytes 153604
  2.8 6.3 %collective-permute-start = (bf16[88,960]{1,0:T(8,128)(2,1)S(1)}, bf16[88,960]{1,0:T(8,128)(2,1)S(1)}, u32[]{:S(2)}, u32[]{:S(2)}) collective-permute-start(bf16[88,960]{1,0:T(8,128)(2,1)S(1)} %get-tuple-element.36), channel_id=1, source_target_pairs={{0,4},{1,5},{2,6},{3,7},{4,0},{5,1},{6,2},{7,3},{8,12},{9,13},{10,... | collective-permute-start | bytes 506888 | tf_op jit(solution)/shard_map/ppermute | solution.py:599
  9.2 6.9 %collective-permute-start.1 = (bf16[88,768]{1,0:T(8,128)(2,1)S(1)}, bf16[88,768]{1,0:T(8,128)(2,1)S(1)}, u32[]{:S(2)}, u32[]{:S(2)}) collective-permute-start(bf16[88,768]{1,0:T(8,128)(2,1)S(1)} %shard_map.101), channel_id=1, source_target_pairs={{1,2},{2,1},{4,5},{5,4},{6,7},{7,6},{9,10},{10,9},{12,13},{13,12},... | collective-permute-start | bytes 405512 | tf_op jit(solution)/shard_map/ppermute | solution.py:621
  9.9 6.2 %copy-start.3 = (bf16[512,1024]{1,0:T(8,128)(2,1)S(1)}, bf16[512,1024]{1,0:T(8,128)(2,1)}, u32[]{:S(2)}) copy-start(bf16[512,1024]{1,0:T(8,128)(2,1)} %refs_11_.3) | copy-start | bytes 3145732
  9.9 6.1 %copy-start.4 = (bf16[1024,512]{1,0:T(8,128)(2,1)S(1)}, bf16[1024,512]{1,0:T(8,128)(2,1)}, u32[]{:S(2)}) copy-start(bf16[1024,512]{1,0:T(8,128)(2,1)} %refs_12_.3) | copy-start | bytes 3145732
  9.9 6.1 %copy-start.7 = (bf16[512,83]{0,1:T(8,128)(2,1)S(1)}, bf16[512,83]{0,1:T(8,128)(2,1)}, u32[]{:S(2)}) copy-start(bf16[512,83]{0,1:T(8,128)(2,1)} %param.19) | copy-start | bytes 254980
  9.9 6.1 %copy-start.9 = (f32[512]{0:T(512)S(1)}, f32[512]{0:T(512)}, u32[]{:S(2)}) copy-start(f32[512]{0:T(512)} %param.16) | copy-start | bytes 6148
  13.1 11.6 %collective-permute-start.2 = (f32[83,576]{1,0:T(8,128)S(1)}, f32[83,576]{1,0:T(8,128)S(1)}, u32[]{:S(2)}, u32[]{:S(2)}) collective-permute-start(f32[83,576]{1,0:T(8,128)S(1)} %get-tuple-element.46), channel_id=1, source_target_pairs={{0,4},{1,5},{2,6},{3,7},{4,0},{5,1},{6,2},{7,3},{8,12},{9,13},{10,... | collective-permute-start | bytes 573704 | tf_op jit(solution)/shard_map/ppermute | solution.py:622
  24.9 0.7 collective-permute-start.3
  25.6 0.7 collective-permute-start.4
  26.3 14.3 %collective-permute-start.5 = (bf16[8,6336]{1,0:T(8,128)(2,1)S(1)}, bf16[8,6336]{1,0:T(8,128)(2,1)S(1)}, u32[]{:S(2)}, u32[]{:S(2)}) collective-permute-start(bf16[8,6336]{1,0:T(8,128)(2,1)S(1)} %shard_map.106), channel_id=1, source_target_pairs={{16,24},{20,28},{17,25},{21,29},{18,26},{22,30},{19,27},{23,31}} | collective-permute-start | bytes 304136 | tf_op jit(solution)/shard_map/ppermute | solution.py:547
  40.9 5.6 %collective-permute-start.6 = (bf16[88,768]{1,0:T(8,128)(2,1)S(1)}, bf16[88,768]{1,0:T(8,128)(2,1)S(1)}, u32[]{:S(2)}, u32[]{:S(2)}) collective-permute-start(bf16[88,768]{1,0:T(8,128)(2,1)S(1)} %get-tuple-element.50), channel_id=1, source_target_pairs={{0,4},{1,5},{2,6},{3,7},{4,0},{5,1},{6,2},{7,3},{8,12},{9,13},{10,... | collective-permute-start | bytes 405512 | tf_op jit(solution)/shard_map/ppermute | solution.py:652
  42.3 4.2 %collective-permute-start.7 = (bf16[88,768]{1,0:T(8,128)(2,1)S(1)}, bf16[88,768]{1,0:T(8,128)(2,1)S(1)}, u32[]{:S(2)}, u32[]{:S(2)}) collective-permute-start(bf16[88,768]{1,0:T(8,128)(2,1)S(1)} %get-tuple-element.51), channel_id=1, source_target_pairs={{1,2},{2,1},{4,5},{5,4},{6,7},{7,6},{9,10},{10,9},{12,13},{13,12},... | collective-permute-start | bytes 405512 | tf_op jit(solution)/shard_map/ppermute | solution.py:653
  52.9 0.7 collective-permute-start.8
  53.6 0.7 collective-permute-start.9
  54.3 10.5 %collective-permute-start.10 = (bf16[8,6336]{1,0:T(8,128)(2,1)S(1)}, bf16[8,6336]{1,0:T(8,128)(2,1)S(1)}, u32[]{:S(2)}, u32[]{:S(2)}) collective-permute-start(bf16[8,6336]{1,0:T(8,128)(2,1)S(1)} %shard_map.111), channel_id=1, source_target_pairs={{16,24},{20,28},{17,25},{21,29},{18,26},{22,30},{19,27},{23,31}} | collective-permute-start | bytes 304136 | tf_op jit(solution)/shard_map/ppermute | solution.py:547
  65.1 7.2 %collective-permute-start.11 = (f32[8,6336]{1,0:T(8,128)S(1)}, f32[8,6336]{1,0:T(8,128)S(1)}, u32[]{:S(2)}, u32[]{:S(2)}) collective-permute-start(f32[8,6336]{1,0:T(8,128)S(1)} %get-tuple-element.64), channel_id=1, source_target_pairs={{0,4},{1,5},{2,6},{3,7},{4,0},{5,1},{6,2},{7,3},{8,12},{9,13},{10,... | collective-permute-start | bytes 608264 | tf_op jit(solution)/shard_map/ppermute | solution.py:674
